TPU v7x, 32 devices: a whole 2x2x4 slice. The times are simulated.
32 devices in a mesh: col: 4 (over z), row: 8 (over y, x, core).
Axes of the slice: x: 2, y: 2, z: 4, core: 2. Of those that a mesh axis runs over, the one named last changes fastest.
Arguments:
- sources: bfloat16 [131072, 1024], P(('col', 'row')), may hold values from -6 to 6
- enc_scale: float32 [131072], P(('col', 'row')), may hold values from 0.5 to 2
- encoder: bfloat16 [256, 4096], replicated, may hold values from -0.09375 to 0.09375
- comp_transfer: bfloat16 [2, 512, 512], replicated, may hold values from -0.25 to 0.25
- comp_gain: float32 [2, 8, 4, 256], P(None, 'row'), may hold values from 0.5 to 1.5
- exp_transfer: bfloat16 [3, 512, 512], replicated, may hold values from -0.25 to 0.25
- exp_gain: float32 [3, 4, 8, 256], P(None, 'col'), may hold values from 0.5 to 1.5
- decoder: bfloat16 [4096, 256], replicated, may hold values from -0.375 to 0.375
- dec_scale: float32 [131072], P(('col', 'row')), may hold values from 0.5 to 2
Outputs:
- field: bfloat16 [131072, 1024], P(('col', 'row'))
All inputs are finite; a program needn't handle non-finite values.
Results may differ from a plain program's by a relative error of at most 0.015.
Values may be sent and summed in bfloat16 or wider, within the bound.
No kernel may reach another device: no remote copies, remote signals or barrier semaphores. Data moves between devices by JAX's collectives and lax.ppermute only.
A program may use at most 128 MiB of HBM per device.

v0:
```python
import jax
import jax.numpy as jnp
from jax import lax
from jax.sharding import PartitionSpec as P


def from_partner(value, axis, bit):
    mask = 2**bit
    pairs = [(source, source ^ mask) for source in range(lax.axis_size(axis))]
    return lax.ppermute(value, axis, pairs)


def pair_step(current, partner, position, level_num, transfer, gain_row):
    skeleton = current.shape[1]
    upper_bit = position // 2**level_num % 2
    first = jnp.where(upper_bit == 0, current, partner)
    second = jnp.where(upper_bit == 0, partner, current)
    stacked = jnp.concatenate([first, second], axis=1)
    chosen = lax.dynamic_slice_in_dim(transfer, upper_bit * skeleton, skeleton, 0)
    mixed_rows = lax.dot_general(
        stacked, chosen, (((1,), (1,)), ((), ())), preferred_element_type=jnp.float32
    )
    return (mixed_rows * gain_row[None, :]).astype(jnp.bfloat16)


def local_level(spread, box_count, level_num, transfer, gain_table):
    skeleton = gain_table.shape[1]
    width = spread.shape[0]
    lower_span = 2**level_num
    upper_span = box_count // (2 * lower_span)
    halves = spread.reshape(width, upper_span, 2, lower_span, skeleton)
    stacked = jnp.concatenate([halves[:, :, 0], halves[:, :, 1]], axis=-1)
    paired = transfer.reshape(2, skeleton, 2 * skeleton)
    mixed_rows = jnp.einsum("shlk,tjk->shtlj", stacked, paired, preferred_element_type=jnp.float32)
    mixed_rows = mixed_rows.reshape(width, box_count, skeleton) * gain_table[None]
    return mixed_rows.astype(jnp.bfloat16).reshape(width, box_count * skeleton)


def body(
    sources,
    enc_scale,
    encoder,
    comp_transfer,
    comp_gain,
    exp_transfer,
    exp_gain,
    decoder,
    dec_scale,
):
    col_count = lax.axis_size("col")
    row_count = lax.axis_size("row")
    col_levels = col_count.bit_length() - 1
    row_levels = row_count.bit_length() - 1
    col_position = lax.axis_index("col")
    scaled = (sources.astype(jnp.float32) * enc_scale[:, None]).astype(jnp.bfloat16)
    coeffs = lax.dot_general(
        scaled, encoder, (((0,), (1,)), ((), ())), preferred_element_type=jnp.float32
    ).astype(jnp.bfloat16)
    for level_num in range(col_levels):
        partner = from_partner(coeffs, "col", level_num)
        gain_row = lax.dynamic_index_in_dim(
            comp_gain[level_num, 0], col_position, 0, keepdims=False
        )
        coeffs = pair_step(
            coeffs, partner, col_position, level_num, comp_transfer[level_num], gain_row
        )
    spread = lax.all_to_all(coeffs, "row", split_axis=0, concat_axis=1, tiled=True)
    for level_num in range(row_levels):
        spread = local_level(
            spread, row_count, level_num, exp_transfer[level_num], exp_gain[level_num, 0]
        )
    coeffs = lax.all_to_all(spread, "row", split_axis=1, concat_axis=0, tiled=True)
    result = lax.dot_general(
        decoder, coeffs, (((1,), (1,)), ((), ())), preferred_element_type=jnp.float32
    )
    return (result * dec_scale[:, None]).astype(jnp.bfloat16)


def solution(mesh):
    in_specs = (
        P(("col", "row"), None),
        P(("col", "row")),
        P(),
        P(),
        P(None, "row", None, None),
        P(),
        P(None, "col", None, None),
        P(),
        P(("col", "row")),
    )
    out_specs = P(("col", "row"), None)
    return jax.shard_map(body, mesh=mesh, in_specs=in_specs, out_specs=out_specs, check_vma=False)
```

profile of v0, /device:TPU:0, one launch (start us, length us, event | category | flops | bytes accessed | tf_op | source)
XLA Modules:
  0.0 97.3 jit_solution(363968949034037290)
XLA Ops:
  0.0 0.0 copy-start
  0.0 0.0 copy-start.5
  0.0 0.0 copy-start.2
  0.0 7.4 %fusion.3 = bf16[1024,256]{0,1:T(8,128)(2,1)} fusion(bf16[256,4096]{1,0:T(8,128)(2,1)} %param.11, bf16[4096,1024]{1,0:T(8,128)(2,1)} %param.9, f32[4096]{0:T(1024)} %param.10), kind=kOutput, calls=%fused_computation.9 | convolution fusion | flops 2160328704 | bytes 11026432 | tf_op jit(solution)/shard_map/dot_general | solution.py:56
  7.4 3.1 %collective-permute-start = (bf16[1024,256]{0,1:T(8,128)(2,1)}, bf16[1024,256]{0,1:T(8,128)(2,1)}, u32[]{:S(2)}, u32[]{:S(2)}) collective-permute-start(bf16[1024,256]{0,1:T(8,128)(2,1)} %fusion.3), channel_id=1, source_target_pairs={{0,8},{8,0},{16,24},{24,16},{1,9},{9,1},{17,25},{25,17},{2,10},{10... | collective-permute-start | bytes 1572872 | tf_op jit(solution)/shard_map/ppermute | solution.py:10
  10.4 0.0 copy-done.5
  10.5 0.0 copy-done.2
  10.5 0.9 fusion.33
  11.3 11.3 %collective-permute-done = bf16[1024,256]{0,1:T(8,128)(2,1)} collective-permute-done((bf16[1024,256]{0,1:T(8,128)(2,1)}, bf16[1024,256]{0,1:T(8,128)(2,1)}, u32[]{:S(2)}, u32[]{:S(2)}) %collective-permute-start) | collective-permute-done | bytes 524320 | tf_op jit(solution)/shard_map/ppermute | solution.py:10
  22.7 1.3 %broadcast_select_fusion.1 = (bf16[1024,256]{0,1:T(8,128)(2,1)S(1)}, bf16[1024,256]{0,1:T(8,128)(2,1)S(1)}) fusion(bf16[1024,256]{0,1:T(8,128)(2,1)} %fusion.3, bf16[1024,256]{0,1:T(8,128)(2,1)} %collective-permute-done, pred[]{:T(512)S(6)} %eq.12), kind=kLoop, calls=%fused_computation.34 | loop fusion | flops 524288 | bytes 2097153 | tf_op jit(solution)/shard_map/jit(_where)/select_n | solution.py:16
  24.0 0.4 fusion.5
  24.4 2.8 %collective-permute-start.1 = (bf16[1024,256]{0,1:T(8,128)(2,1)S(1)}, bf16[1024,256]{0,1:T(8,128)(2,1)S(1)}, u32[]{:S(2)}, u32[]{:S(2)}) collective-permute-start(bf16[1024,256]{0,1:T(8,128)(2,1)S(1)} %fusion.5), channel_id=1, source_target_pairs={{0,16},{8,24},{16,0},{24,8},{1,17},{9,25},{17,1},{25,9},{2,18},{10... | collective-permute-start | bytes 1572872 | tf_op jit(solution)/shard_map/ppermute | solution.py:10
  27.2 0.0 copy-start.3
  27.2 22.5 %collective-permute-done.1 = bf16[1024,256]{0,1:T(8,128)(2,1)S(1)} collective-permute-done((bf16[1024,256]{0,1:T(8,128)(2,1)S(1)}, bf16[1024,256]{0,1:T(8,128)(2,1)S(1)}, u32[]{:S(2)}, u32[]{:S(2)}) %collective-permute-start.1) | collective-permute-done | bytes 524320 | tf_op jit(solution)/shard_map/ppermute | solution.py:10
  49.7 0.1 broadcast_select_fusion.3
  49.8 0.0 copy-start.4
  49.8 0.0 copy-done.3
  49.8 1.3 %fusion.4 = bf16[1024,256]{1,0:T(8,128)(2,1)} fusion(bf16[1024,256]{0,1:T(8,128)(2,1)S(1)} %get-tuple-element.11, bf16[1024,256]{0,1:T(8,128)(2,1)S(1)} %get-tuple-element.10, f32[256]{0:T(256)S(1)} %bitcast.101, bf16[1,512,512]{2,1,0:T(8,128)(2,1)S(1)} %copy-done.3, s32[]{:T(128)S(6)} %select_n.60), kind=kOutput, calls=%fused_computation.10 | convolution fusion | flops 271056896 | bytes 1836036 | tf_op jit(solution)/shard_map/dot_general | solution.py:20
  51.1 3.6 %all-to-all-start = ((bf16[8,128,256]{2,1,0:T(8,128)(2,1)}), bf16[8,128,256]{2,1,0:T(8,128)(2,1)S(1)}, u32[]{:S(2)}, u32[]{:S(2)}) async-start(bf16[8,128,256]{2,1,0:T(8,128)(2,1)} %bitcast.4), calls=%async_computation | async-start | bytes 1048576 | tf_op jit(solution)/shard_map/all_to_all | solution.py:67
  54.7 0.0 copy-done.4
  54.7 2.5 %fusion.32 = (bf16[1,512,512]{2,1,0:T(8,128)(2,1)}, bf16[1,512,512]{2,1,0:T(8,128)(2,1)S(1)}, bf16[1,512,512]{2,1,0:T(8,128)(2,1)}) fusion(bf16[3,512,512]{2,1,0:T(8,128)(2,1)} %param.14), kind=kLoop, calls=%fused_computation.57 | loop fusion | bytes 3145728 | tf_op jit(solution)/shard_map/slice | solution.py:70
  57.2 7.2 %all-to-all-done = bf16[8,128,256]{2,1,0:T(8,128)(2,1)S(1)} async-done(((bf16[8,128,256]{2,1,0:T(8,128)(2,1)}), bf16[8,128,256]{2,1,0:T(8,128)(2,1)S(1)}, u32[]{:S(2)}, u32[]{:S(2)}) %all-to-all-start) | async-done | bytes 524320 | tf_op jit(solution)/shard_map/all_to_all | solution.py:67
  64.4 0.0 copy-start.1
  64.5 1.6 %fusion.14 = f32[128,4,2,256]{3,0,2,1:T(8,128)S(1)} fusion(bf16[2,256,512,1]{2,1,0,3:T(8,128)(2,1)} %bitcast.98, bf16[128,4,1,256]{3,0,1,2:T(8,128)(2,1)S(1)} %get-tuple-element.19, bf16[128,4,1,256]{3,0,1,2:T(8,128)(2,1)S(1)} %get-tuple-element.18), kind=kOutput, calls=%fused_computation.24 | convolution fusion | flops 269484032 | bytes 2097152 | tf_op jit(solution)/shard_map/shlk,tjk->shtlj/dot_general | solution.py:34
  66.0 0.1 fusion.13
  66.2 0.0 copy-done.1
  66.2 0.5 convolution_bitcast_fusion.1
  66.7 0.1 copy.17
  66.8 0.1 multiply_convert_fusion.5
  66.9 0.5 convolution_bitcast_fusion
  67.4 0.0 copy-start.6
  67.4 0.1 copy.18
  67.5 0.1 fusion.12
  67.6 12.1 %all_to_all.32 = bf16[128,8,256]{2,0,1:T(8,128)(2,1)S(1)} all-to-all(bf16[128,8,256]{2,0,1:T(8,128)(2,1)S(1)} %fusion.12), channel_id=1, replica_groups=mesh['col'=4,'row'=8] {'row'}, dimensions={1} | all-to-all | bytes 1048576 | tf_op jit(solution)/shard_map/all_to_all | solution.py:72
  79.7 0.0 copy-done
  79.7 0.0 copy-done.6
  79.7 5.6 %fusion.2 = bf16[4096,1024]{0,1:T(8,128)(2,1)} fusion(f32[4096]{0:T(1024)S(1)} %copy-done.6, bf16[1024,256]{1,0:T(8,128)(2,1)S(1)} %bitcast.99, bf16[4096,256]{1,0:T(8,128)(2,1)S(1)} %copy-done), kind=kOutput, calls=%fused_computation.4 | convolution fusion | flops 2155872256 | bytes 11026432 | tf_op jit(solution)/shard_map/dot_general | solution.py:73
  85.3 11.9 %copy.19 = bf16[4096,1024]{1,0:T(8,128)(2,1)} copy(bf16[4096,1024]{0,1:T(8,128)(2,1)} %fusion.2) | data formatting | bytes 16777216 | tf_op jit(solution)/shard_map/convert_element_type | solution.py:76
  (9 shorter events, 0.1 us)
Async XLA Ops:
  0.0 79.7 %copy-start = (bf16[4096,256]{1,0:T(8,128)(2,1)S(1)}, bf16[4096,256]{1,0:T(8,128)(2,1)}, u32[]{:S(2)}) copy-start(bf16[4096,256]{1,0:T(8,128)(2,1)} %param.16) | copy-start | bytes 6291460
  0.0 10.4 %copy-start.5 = (f32[2,1,4,256]{3,2,1,0:T(4,128)S(1)}, f32[2,1,4,256]{3,2,1,0:T(4,128)}, u32[]{:S(2)}) copy-start(f32[2,1,4,256]{3,2,1,0:T(4,128)} %param.13) | copy-start | bytes 24580
  0.0 10.5 %copy-start.2 = (bf16[2,512,512]{2,1,0:T(8,128)(2,1)S(1)}, bf16[2,512,512]{2,1,0:T(8,128)(2,1)}, u32[]{:S(2)}) copy-start(bf16[2,512,512]{2,1,0:T(8,128)(2,1)} %param.12) | copy-start | bytes 3145732
  7.4 15.3 %collective-permute-start = (bf16[1024,256]{0,1:T(8,128)(2,1)}, bf16[1024,256]{0,1:T(8,128)(2,1)}, u32[]{:S(2)}, u32[]{:S(2)}) collective-permute-start(bf16[1024,256]{0,1:T(8,128)(2,1)} %fusion.3), channel_id=1, source_target_pairs={{0,8},{8,0},{16,24},{24,16},{1,9},{9,1},{17,25},{25,17},{2,10},{10... | collective-permute-start | bytes 1572872 | tf_op jit(solution)/shard_map/ppermute | solution.py:10
  24.4 25.3 %collective-permute-start.1 = (bf16[1024,256]{0,1:T(8,128)(2,1)S(1)}, bf16[1024,256]{0,1:T(8,128)(2,1)S(1)}, u32[]{:S(2)}, u32[]{:S(2)}) collective-permute-start(bf16[1024,256]{0,1:T(8,128)(2,1)S(1)} %fusion.5), channel_id=1, source_target_pairs={{0,16},{8,24},{16,0},{24,8},{1,17},{9,25},{17,1},{25,9},{2,18},{10... | collective-permute-start | bytes 1572872 | tf_op jit(solution)/shard_map/ppermute | solution.py:10
  27.2 22.6 %copy-start.3 = (bf16[1,512,512]{2,1,0:T(8,128)(2,1)S(1)}, bf16[1,512,512]{2,1,0:T(8,128)(2,1)}, u32[]{:S(2)}) copy-start(bf16[1,512,512]{2,1,0:T(8,128)(2,1)} %get-tuple-element.8) | copy-start | bytes 1572868
  49.8 4.9 %copy-start.4 = (f32[3,1,8,256]{3,2,1,0:T(8,128)S(1)}, f32[3,1,8,256]{3,2,1,0:T(8,128)}, u32[]{:S(2)}) copy-start(f32[3,1,8,256]{3,2,1,0:T(8,128)} %param.15) | copy-start | bytes 73732
  51.1 13.3 %all-to-all-start = ((bf16[8,128,256]{2,1,0:T(8,128)(2,1)}), bf16[8,128,256]{2,1,0:T(8,128)(2,1)S(1)}, u32[]{:S(2)}, u32[]{:S(2)}) async-start(bf16[8,128,256]{2,1,0:T(8,128)(2,1)} %bitcast.4), calls=%async_computation | async-start | bytes 1048576 | tf_op jit(solution)/shard_map/all_to_all | solution.py:67
  64.4 1.7 %copy-start.1 = (bf16[1,512,512]{2,1,0:T(8,128)(2,1)S(1)}, bf16[1,512,512]{2,1,0:T(8,128)(2,1)}, u32[]{:S(2)}) copy-start(bf16[1,512,512]{2,1,0:T(8,128)(2,1)} %get-tuple-element.7) | copy-start | bytes 1572868
  67.4 12.3 %copy-start.6 = (f32[4096]{0:T(1024)S(1)}, f32[4096]{0:T(1024)}, u32[]{:S(2)}) copy-start(f32[4096]{0:T(1024)} %param.17) | copy-start | bytes 49156
where the time goes:
time: 97.9 us; the launch traced here: 97.3 us
  waiting for transfers between devices  41 us (42%)
  matrix products  17.2 us (18%)
  local copies, waits for them, and re-layouts  15.6 us (16%)
  blocking collectives  12.1 us (12%)
  starting transfers between devices  9.49 us (10%)
  other arithmetic  1.65 us (2%)
    ppermute x2, waiting for transfers between devices, from_partner(): return lax.ppermute(value, axis, pairs)  33.8 us
    all_to_all x1, blocking collectives, body(): lax.all_to_all(spread, 'row', split_axis=1, concat_axis=0, tiled=True)  12.1 us
    convert_element_type x1, local copies, waits for them, and re-layouts, body(): return (result * dec_scale[:, None]).astype(jnp.bfloat16)  11.9 us
    dot_general x1, matrix products, body(): lax.dot_general(scaled, encoder, (((0,), (1,)), ((), ())), preferred_elem...  7.37 us
    all_to_all x1, waiting for transfers between devices, body(): lax.all_to_all(coeffs, 'row', split_axis=0, concat_axis=1, tiled=True)  7.2 us
    ppermute x2, starting transfers between devices, from_partner(): return lax.ppermute(value, axis, pairs)  5.88 us
    dot_general x1, matrix products, body(): lax.dot_general(decoder, coeffs, (((1,), (1,)), ((), ())), preferred_elem...  5.63 us
    all_to_all x1, starting transfers between devices, body(): lax.all_to_all(coeffs, 'row', split_axis=0, concat_axis=1, tiled=True)  3.6 us
  transfers between devices with their start and end apart: 3, of which 3 were waited for; matrix products, arithmetic and copies ran while one was open for 3% of the time, Pallas kernels for 0%

commit v1 on v0

v1 whole, which is shorter than its diff:
```python
import functools

import jax
import jax.numpy as jnp
from jax import lax
from jax.experimental import pallas as pl
from jax.experimental.pallas import tpu as pltpu
from jax.sharding import PartitionSpec as P

AXES = ("col", "row")
LANES = 128
NT = (((1,), (1,)), ((), ()))


def mm(a, b, dims=(((1,), (0,)), ((), ()))):
    return lax.dot_general(a, b, dims, preferred_element_type=jnp.float32)


def encode_kernel(sources_ref, scale_ref, encoder_ref, gains_ref, out_ref, acc_ref):
    step = pl.program_id(0)
    scaled = (encoder_ref[...].astype(jnp.float32) * scale_ref[...]).astype(jnp.bfloat16)
    part = mm(scaled, sources_ref[...])

    @pl.when(step == 0)
    def _():
        acc_ref[...] = part

    @pl.when(step > 0)
    def _():
        acc_ref[...] += part

    @pl.when(step == pl.num_programs(0) - 1)
    def _():
        parts = out_ref.shape[0]
        pad = gains_ref.shape[0]
        width = (out_ref.shape[1] - pad) // 2
        turned = acc_ref[...].T.astype(jnp.bfloat16).reshape(parts, width, 2 * LANES)
        out_ref[:, :width, :] = turned[:, :, :LANES]
        out_ref[:, width : 2 * width, :] = turned[:, :, LANES:]
        out_ref[:, 2 * width :, :] = jnp.broadcast_to(gains_ref[...][None], (parts, pad, LANES))


def encode(sources, enc_scale, encoder, gains, parts):
    points, width = sources.shape
    skeleton = encoder.shape[0]
    pad = gains.shape[0]
    block = 512
    rows = 2 * (width // parts) + pad
    return pl.pallas_call(
        encode_kernel,
        grid=(points // block,),
        in_specs=[
            pl.BlockSpec((block, width), lambda k: (k, 0)),
            pl.BlockSpec((1, block), lambda k: (0, k)),
            pl.BlockSpec((skeleton, block), lambda k: (0, k)),
            pl.BlockSpec((pad, LANES), lambda k: (0, 0)),
        ],
        out_specs=pl.BlockSpec((parts, rows, LANES), lambda k: (0, 0, 0)),
        out_shape=jax.ShapeDtypeStruct((parts, rows, LANES), jnp.bfloat16),
        scratch_shapes=[pltpu.VMEM((skeleton, width), jnp.float32)],
        compiler_params=pltpu.CompilerParams(dimension_semantics=("arbitrary",)),
    )(sources, enc_scale.reshape(1, points), encoder, gains)


def levels_kernel(strides, pad, packed_ref, comp_ref, exp_ref, out_ref):
    boxes, rows, _ = packed_ref.shape
    width = (rows - pad) // 2
    skeleton = 2 * LANES
    state = jnp.concatenate([packed_ref[:, :width, :], packed_ref[:, width : 2 * width, :]], axis=-1)
    gains = packed_ref[:, 2 * width :, :].astype(jnp.float32)
    for number, stride in enumerate(strides):
        turned = number >= comp_ref.shape[0]
        transfer = exp_ref[number - comp_ref.shape[0]] if turned else comp_ref[number]
        halves = state.reshape(boxes // (2 * stride), 2, stride * width, skeleton)
        low = halves[:, 0].reshape(boxes // 2 * width, skeleton)
        high = halves[:, 1].reshape(boxes // 2 * width, skeleton)
        mixed = mm(low, transfer[:, :skeleton], NT) + mm(high, transfer[:, skeleton:], NT)
        shape = (boxes // (2 * stride), 1, stride, width, skeleton)
        both = jnp.concatenate(
            [mixed[:, :skeleton].reshape(shape), mixed[:, skeleton:].reshape(shape)], axis=1
        ).reshape(boxes, width, skeleton)
        if number + 1 < len(strides):
            gain = jnp.concatenate(
                [gains[:, 2 * number : 2 * number + 1, :], gains[:, 2 * number + 1 : 2 * number + 2, :]],
                axis=-1,
            )
            both = both * gain
        state = both.astype(jnp.bfloat16)
    out_ref[:, :width, :] = state[:, :, :LANES]
    out_ref[:, width:, :] = state[:, :, LANES:]


def levels(packed, comp_transfer, exp_transfer, strides, pad):
    boxes, rows, _ = packed.shape
    return pl.pallas_call(
        functools.partial(levels_kernel, strides, pad),
        in_specs=[pl.BlockSpec(memory_space=pltpu.VMEM)] * 3,
        out_specs=pl.BlockSpec(memory_space=pltpu.VMEM),
        out_shape=jax.ShapeDtypeStruct((boxes, rows - pad, LANES), jnp.bfloat16),
    )(packed, comp_transfer, exp_transfer)


def decode_kernel(packed_ref, decoder_ref, out_ref, turned_ref):
    @pl.when(pl.program_id(0) == 0)
    def _():
        boxes, rows, _ = packed_ref.shape
        width = rows // 2
        coeffs = jnp.concatenate([packed_ref[:, :width, :], packed_ref[:, width:, :]], axis=-1)
        turned_ref[...] = coeffs.reshape(boxes * width, 2 * LANES).T

    out_ref[...] = mm(decoder_ref[...], turned_ref[...]).astype(jnp.bfloat16)


def decode(packed, decoder):
    boxes, rows, _ = packed.shape
    points, skeleton = decoder.shape
    width = boxes * rows // 2
    block = 512
    return pl.pallas_call(
        decode_kernel,
        grid=(points // block,),
        in_specs=[
            pl.BlockSpec((boxes, rows, LANES), lambda k: (0, 0, 0)),
            pl.BlockSpec((block, skeleton), lambda k: (k, 0)),
        ],
        out_specs=pl.BlockSpec((block, width), lambda k: (k, 0)),
        out_shape=jax.ShapeDtypeStruct((points, width), jnp.bfloat16),
        scratch_shapes=[pltpu.VMEM((skeleton, width), jnp.bfloat16)],
        compiler_params=pltpu.CompilerParams(dimension_semantics=("arbitrary",)),
    )(packed, decoder)


def plain_encode(sources, enc_scale, encoder, gains, parts):
    scaled = (encoder.astype(jnp.float32) * enc_scale[None, :]).astype(jnp.bfloat16)
    coeffs = mm(sources, scaled, (((0,), (1,)), ((), ()))).astype(jnp.bfloat16)
    coeffs = coeffs.reshape(parts, -1, 2, LANES).swapaxes(1, 2).reshape(parts, -1, LANES)
    gains = jnp.broadcast_to(gains[None], (parts, *gains.shape))
    return jnp.concatenate([coeffs, gains], axis=1)


def plain_levels(packed, comp_transfer, exp_transfer, strides, pad):
    boxes, rows, _ = packed.shape
    width = (rows - pad) // 2
    skeleton = 2 * LANES
    state = packed[:, : 2 * width].reshape(boxes, 2, width, LANES).swapaxes(1, 2).reshape(boxes, width, skeleton)
    gains = packed[:, 2 * width :].astype(jnp.float32).reshape(boxes, pad // 2, 1, skeleton)
    transfers = jnp.concatenate([comp_transfer, exp_transfer], axis=0)
    for number, stride in enumerate(strides):
        halves = state.reshape(boxes // (2 * stride), 2, stride, width, skeleton)
        stacked = jnp.concatenate([halves[:, 0], halves[:, 1]], axis=-1)
        paired = transfers[number].reshape(2, skeleton, 2 * skeleton)
        both = jnp.einsum("hlsk,tjk->htlsj", stacked, paired, preferred_element_type=jnp.float32)
        both = both.reshape(boxes, width, skeleton)
        if number + 1 < len(strides):
            both = both * gains[:, number]
        state = both.astype(jnp.bfloat16)
    return state.reshape(boxes, width, 2, LANES).swapaxes(1, 2).reshape(boxes, 2 * width, LANES)


def plain_decode(packed, decoder):
    boxes, rows, _ = packed.shape
    width = rows // 2
    coeffs = packed.reshape(boxes, 2, width, LANES).swapaxes(1, 2).reshape(boxes * width, 2 * LANES)
    return mm(decoder, coeffs, NT).astype(jnp.bfloat16)


def body(
    sources,
    enc_scale,
    encoder,
    comp_transfer,
    comp_gain,
    exp_transfer,
    exp_gain,
    decoder,
    dec_scale,
):
    col_count, row_count = lax.axis_size("col"), lax.axis_size("row")
    parts = col_count * row_count
    skeleton = encoder.shape[0]
    comp_levels, exp_levels = comp_transfer.shape[0], exp_transfer.shape[0]
    strides = tuple(row_count * 2**number for number in range(comp_levels)) + tuple(
        2**number for number in range(exp_levels)
    )
    own_comp = lax.dynamic_index_in_dim(comp_gain[:, 0], lax.axis_index("col"), 1, keepdims=False)
    own_exp = lax.dynamic_index_in_dim(exp_gain[:, 0], lax.axis_index("row"), 1, keepdims=False)
    sent = jnp.concatenate([own_comp, own_exp[:-1]], axis=0).astype(jnp.bfloat16).reshape(-1, LANES)
    pad = -(-sent.shape[0] // 8) * 8
    sent = jnp.pad(sent, ((0, pad - sent.shape[0]), (0, 0)))

    kernels = (sources.shape[1] // parts) % 16 == 0 and skeleton == 2 * LANES
    run_encode, run_levels, run_decode = (
        (encode, levels, decode) if kernels else (plain_encode, plain_levels, plain_decode)
    )
    packed = run_encode(sources, enc_scale, encoder, sent, parts)
    packed = lax.all_to_all(packed, AXES, 0, 0, tiled=True)
    result = run_levels(packed, comp_transfer, exp_transfer, strides, pad)
    result = lax.all_to_all(result, AXES, 0, 0, tiled=True)
    factors = dec_scale[:, None] * own_exp[-1][None, :]
    scaled = (decoder.astype(jnp.float32) * factors).astype(jnp.bfloat16)
    return run_decode(result, scaled)


def solution(mesh):
    in_specs = (
        P(AXES, None),
        P(AXES),
        P(),
        P(),
        P(None, "row", None, None),
        P(),
        P(None, "col", None, None),
        P(),
        P(AXES),
    )
    return jax.shard_map(body, mesh=mesh, in_specs=in_specs, out_specs=P(AXES, None), check_vma=False)
```

time: 97.9 us -> 69.4 us (0.71)
  Pallas kernels: 0 us -> 22.1 us
  matrix products: 17.2 us -> 0 us
  blocking collectives: 12.1 us -> 0 us
  local copies, waits for them, and re-layouts: 15.6 us -> 3.72 us
  waiting for transfers between devices: 41 us -> 30.6 us
  starting transfers between devices: 9.49 us -> 10.5 us
    ppermute x2 -> x0, waiting for transfers between devices: 33.8 us -> none  [from_partner(): return lax.ppermute(value, axis, pairs)]
    all_to_all x1 -> x2, waiting for transfers between devices: 7.2 us -> 30.6 us  [the longest x1 16.8 us: body(): packed = lax.all_to_all(packed, AXES, 0, 0, tiled=True)]
    pallas_call x0 -> x3, Pallas kernels: none -> 22.1 us  [the longest x1 9.16 us: encode(): pl.pallas_call(encode_kernel, grid=(points // block,), in_specs=[pl.Block...]
    dot_general x7 -> x0, matrix products: 17.2 us -> none  [the longest x1 7.37 us: body(): lax.dot_general(scaled, encoder, (((0,), (1,)), ((), ())), preferred_elem...]
    all_to_all x1 -> x0, blocking collectives: 12.1 us -> none  [body(): lax.all_to_all(spread, 'row', split_axis=1, concat_axis=0, tiled=True)]
    convert_element_type x1, local copies, waits for them, and re-layouts: 11.9 us -> 0.61 us  [body(): jnp.concatenate([own_comp, own_exp[:-1]], axis=0).astype(jnp.bfloat16)]
    all_to_all x1 -> x2, starting transfers between devices: 3.6 us -> 10.5 us  [the longest x1 7.33 us: body(): packed = lax.all_to_all(packed, AXES, 0, 0, tiled=True)]
    ppermute x2 -> x0, starting transfers between devices: 5.88 us -> none  [from_partner(): return lax.ppermute(value, axis, pairs)]
  transfers between devices with their start and end apart: 3 -> 2, of which waited for: 3 -> 2; matrix products, arithmetic and copies ran while one was open for 3% -> 3% of each run, Pallas kernels for 0% -> 0%
where the time goes in v1:
time: 69.4 us; the launch traced here: 68.8 us
  waiting for transfers between devices  30.6 us (44%)
  Pallas kernels  22.1 us (32%)
  starting transfers between devices  10.5 us (15%)
  local copies, waits for them, and re-layouts  3.72 us (5%)
  other arithmetic  1.75 us (3%)
    all_to_all x1, waiting for transfers between devices, body(): packed = lax.all_to_all(packed, AXES, 0, 0, tiled=True)  16.8 us
    all_to_all x1, waiting for transfers between devices, body(): result = lax.all_to_all(result, AXES, 0, 0, tiled=True)  13.8 us
    pallas_call x1, Pallas kernels, encode(): pl.pallas_call(encode_kernel, grid=(points // block,), in_specs=[pl.Block...  9.16 us
    pallas_call x1, Pallas kernels, decode(): pl.pallas_call(decode_kernel, grid=(points // block,), in_specs=[pl.Block...  8.51 us
    all_to_all x1, starting transfers between devices, body(): packed = lax.all_to_all(packed, AXES, 0, 0, tiled=True)  7.33 us
    pallas_call x1, Pallas kernels, levels(): pl.pallas_call(functools.partial(levels_kernel, strides, pad), in_specs=[...  4.41 us
    all_to_all x1, starting transfers between devices, body(): result = lax.all_to_all(result, AXES, 0, 0, tiled=True)  3.2 us
    unnamed x12, local copies, waits for them, and re-layouts  2.38 us
  transfers between devices with their start and end apart: 2, of which 2 were waited for; matrix products, arithmetic and copies ran while one was open for 3% of the time, Pallas kernels for 0%

profile of v1, /device:TPU:0, one launch (start us, length us, event | category | flops | bytes accessed | tf_op | source)
XLA Modules:
  0.0 68.8 jit_solution(7233001087680217461)
XLA Ops:
  0.0 0.0 copy-start
  0.0 0.7 %copy-done = f32[3,1,8,256]{3,2,1,0:T(8,128)S(1)} copy-done((f32[3,1,8,256]{3,2,1,0:T(8,128)S(1)}, f32[3,1,8,256]{3,2,1,0:T(8,128)}, u32[]{:S(2)}) %copy-start) | copy-done | bytes 24600
  0.8 0.7 %constant_dynamic-slice_fusion.1 = bf16[2,1,1,256]{3,2,1,0:T(2,128)(2,1)S(1)} fusion(f32[2,1,4,256]{3,2,1,0:T(4,128)} %param.13, s32[]{:T(128)S(6)} %select_n.8), kind=kLoop, calls=%fused_computation.7 | loop fusion | bytes 2052 | tf_op jit(solution)/shard_map/jit(dynamic_index_in_dim)/dynamic_slice | solution.py:185
  1.5 0.6 convert_element_type.11.gains_ref
  2.1 9.2 %shard_map.91 = bf16[32,72,128]{2,1,0:T(8,128)(2,1)} custom-call(bf16[4096,1024]{1,0:T(8,128)(2,1)} %sources_ref.1, f32[1,4096]{1,0:T(1,128)} %bitcast.8, bf16[256,4096]{1,0:T(8,128)(2,1)} %encoder_ref.1, bf16[8,128]{1,0:T(8,128)(2,1)} %convert_element_type.11.gains_ref), custom_call_target="tpu_custom_call" | custom-call | tf_op jit(solution)/shard_map/pallas_call | solution.py:49
  11.2 0.0 copy-start.2
  11.3 0.0 copy-start.4
  11.3 7.3 %all-to-all-start = ((bf16[32,72,128]{2,1,0:T(8,128)(2,1)}), bf16[32,72,128]{2,1,0:T(8,128)(2,1)S(1)}, u32[]{:S(2)}, u32[]{:S(2)}) async-start(bf16[32,72,128]{2,1,0:T(8,128)(2,1)} %shard_map.91), calls=%async_computation | async-start | bytes 1179648 | tf_op jit(solution)/shard_map/all_to_all | solution.py:196
  18.6 16.8 %all-to-all-done.packed_ref = bf16[32,72,128]{2,1,0:T(8,128)(2,1)S(1)} async-done(((bf16[32,72,128]{2,1,0:T(8,128)(2,1)}), bf16[32,72,128]{2,1,0:T(8,128)(2,1)S(1)}, u32[]{:S(2)}, u32[]{:S(2)}) %all-to-all-start) | async-done | bytes 589856 | tf_op jit(solution)/shard_map/all_to_all | solution.py:196
  35.4 0.0 copy-start.1
  35.4 0.8 %copy-done.1 = bf16[32,72,128]{2,1,0:T(8,128)(2,1)} copy-done((bf16[32,72,128]{2,1,0:T(8,128)(2,1)}, bf16[32,72,128]{2,1,0:T(8,128)(2,1)S(1)}, u32[]{:S(2)}) %copy-start.1) | copy-done | bytes 589848
  36.2 4.4 %shard_map.92 = bf16[32,64,128]{2,1,0:T(8,128)(2,1)} custom-call(bf16[32,72,128]{2,1,0:T(8,128)(2,1)} %copy-done.1, bf16[2,512,512]{2,1,0:T(8,128)(2,1)} %comp_ref.1, bf16[3,512,512]{2,1,0:T(8,128)(2,1)} %exp_ref.1), custom_call_target="tpu_custom_call" | custom-call | tf_op jit(solution)/shard_map/pallas_call | solution.py:95
  40.6 3.2 %all-to-all-start.1 = ((bf16[32,64,128]{2,1,0:T(8,128)(2,1)}), bf16[32,64,128]{2,1,0:T(8,128)(2,1)S(1)}, u32[]{:S(2)}, u32[]{:S(2)}) async-start(bf16[32,64,128]{2,1,0:T(8,128)(2,1)} %shard_map.92), calls=%async_computation.1 | async-start | bytes 1048576 | tf_op jit(solution)/shard_map/all_to_all | solution.py:198
  43.8 0.0 copy-done.2
  43.8 0.0 copy-done.4
  43.9 1.7 %multiply_convert_fusion.decoder_ref = bf16[4096,256]{1,0:T(8,128)(2,1)} fusion(bf16[4096,256]{1,0:T(8,128)(2,1)S(1)} %copy-done.2, f32[256]{0:T(256)S(1)} %bitcast.9, f32[4096]{0:T(1024)S(1)} %copy-done.4), kind=kLoop, calls=%fused_computation | loop fusion | flops 4194304 | bytes 4211712 | tf_op jit(solution)/shard_map/convert_element_type | solution.py:200
  45.6 13.8 %all-to-all-done.1.packed_ref = bf16[32,64,128]{2,1,0:T(8,128)(2,1)S(1)} async-done(((bf16[32,64,128]{2,1,0:T(8,128)(2,1)}), bf16[32,64,128]{2,1,0:T(8,128)(2,1)S(1)}, u32[]{:S(2)}, u32[]{:S(2)}) %all-to-all-start.1) | async-done | bytes 524320 | tf_op jit(solution)/shard_map/all_to_all | solution.py:198
  59.4 0.0 copy-start.3
  59.4 0.8 %copy-done.3 = bf16[32,64,128]{2,1,0:T(8,128)(2,1)} copy-done((bf16[32,64,128]{2,1,0:T(8,128)(2,1)}, bf16[32,64,128]{2,1,0:T(8,128)(2,1)S(1)}, u32[]{:S(2)}) %copy-start.3) | copy-done | bytes 524312
  60.2 8.5 %shard_map.93 = bf16[4096,1024]{1,0:T(8,128)(2,1)} custom-call(bf16[32,64,128]{2,1,0:T(8,128)(2,1)} %copy-done.3, bf16[4096,256]{1,0:T(8,128)(2,1)} %multiply_convert_fusion.decoder_ref), custom_call_target="tpu_custom_call" | custom-call | tf_op jit(solution)/shard_map/pallas_call | solution.py:119
  (5 shorter events, 0.0 us)
Async XLA Ops:
  0.0 0.7 %copy-start = (f32[3,1,8,256]{3,2,1,0:T(8,128)S(1)}, f32[3,1,8,256]{3,2,1,0:T(8,128)}, u32[]{:S(2)}) copy-start(f32[3,1,8,256]{3,2,1,0:T(8,128)} %param.15) | copy-start | bytes 73732
  11.2 32.6 %copy-start.2 = (bf16[4096,256]{1,0:T(8,128)(2,1)S(1)}, bf16[4096,256]{1,0:T(8,128)(2,1)}, u32[]{:S(2)}) copy-start(bf16[4096,256]{1,0:T(8,128)(2,1)} %param.16) | copy-start | bytes 6291460
  11.3 32.6 %copy-start.4 = (f32[4096]{0:T(1024)S(1)}, f32[4096]{0:T(1024)}, u32[]{:S(2)}) copy-start(f32[4096]{0:T(1024)} %param.17) | copy-start | bytes 49156
  11.3 24.1 %all-to-all-start = ((bf16[32,72,128]{2,1,0:T(8,128)(2,1)}), bf16[32,72,128]{2,1,0:T(8,128)(2,1)S(1)}, u32[]{:S(2)}, u32[]{:S(2)}) async-start(bf16[32,72,128]{2,1,0:T(8,128)(2,1)} %shard_map.91), calls=%async_computation | async-start | bytes 1179648 | tf_op jit(solution)/shard_map/all_to_all | solution.py:196
  35.4 0.8 %copy-start.1 = (bf16[32,72,128]{2,1,0:T(8,128)(2,1)}, bf16[32,72,128]{2,1,0:T(8,128)(2,1)S(1)}, u32[]{:S(2)}) copy-start(bf16[32,72,128]{2,1,0:T(8,128)(2,1)S(1)} %all-to-all-done.packed_ref) | copy-start | bytes 1769476
  40.6 18.8 %all-to-all-start.1 = ((bf16[32,64,128]{2,1,0:T(8,128)(2,1)}), bf16[32,64,128]{2,1,0:T(8,128)(2,1)S(1)}, u32[]{:S(2)}, u32[]{:S(2)}) async-start(bf16[32,64,128]{2,1,0:T(8,128)(2,1)} %shard_map.92), calls=%async_computation.1 | async-start | bytes 1048576 | tf_op jit(solution)/shard_map/all_to_all | solution.py:198
  59.4 0.8 %copy-start.3 = (bf16[32,64,128]{2,1,0:T(8,128)(2,1)}, bf16[32,64,128]{2,1,0:T(8,128)(2,1)S(1)}, u32[]{:S(2)}) copy-start(bf16[32,64,128]{2,1,0:T(8,128)(2,1)S(1)} %all-to-all-done.1.packed_ref) | copy-start | bytes 1572868

commit v2 on v1

--- a/solution.py
+++ b/solution.py
@@ -10,56 +10,80 @@
 AXES = ("col", "row")
 LANES = 128
 NT = (((1,), (1,)), ((), ()))
+HBM = pl.BlockSpec(memory_space=pl.ANY)
+VMEM = pl.BlockSpec(memory_space=pltpu.VMEM)
+
+
+def on_chip(value):
+    return pltpu.with_memory_space_constraint(value, pltpu.VMEM)
 
 
 def mm(a, b, dims=(((1,), (0,)), ((), ()))):
     return lax.dot_general(a, b, dims, preferred_element_type=jnp.float32)
 
 
-def encode_kernel(sources_ref, scale_ref, encoder_ref, gains_ref, out_ref, acc_ref):
-    step = pl.program_id(0)
-    scaled = (encoder_ref[...].astype(jnp.float32) * scale_ref[...]).astype(jnp.bfloat16)
-    part = mm(scaled, sources_ref[...])
-
-    @pl.when(step == 0)
-    def _():
-        acc_ref[...] = part
-
-    @pl.when(step > 0)
-    def _():
-        acc_ref[...] += part
-
-    @pl.when(step == pl.num_programs(0) - 1)
-    def _():
-        parts = out_ref.shape[0]
-        pad = gains_ref.shape[0]
-        width = (out_ref.shape[1] - pad) // 2
-        turned = acc_ref[...].T.astype(jnp.bfloat16).reshape(parts, width, 2 * LANES)
-        out_ref[:, :width, :] = turned[:, :, :LANES]
-        out_ref[:, width : 2 * width, :] = turned[:, :, LANES:]
-        out_ref[:, 2 * width :, :] = jnp.broadcast_to(gains_ref[...][None], (parts, pad, LANES))
-
-
-def encode(sources, enc_scale, encoder, gains, parts):
+def encode_kernel(blocks, sources_hbm, scale_ref, encoder_hbm, comp_ref, exp_ref, out_ref, held, table, acc_ref, sems):
+    block = sources_hbm.shape[0] // blocks
+    copies = []
+    for number in range(blocks):
+        span = pl.ds(number * block, block)
+        copies.append(
+            (
+                pltpu.make_async_copy(encoder_hbm.at[:, span], table.at[:, span], sems.at[0, number]),
+                pltpu.make_async_copy(sources_hbm.at[span], held.at[span], sems.at[1, number]),
+            )
+        )
+        for copy in copies[-1]:
+            copy.start()
+
+    parts, rows, _ = out_ref.shape
+    own = [comp_ref[number, pl.ds(lax.axis_index("col"), 1), :] for number in range(comp_ref.shape[0])]
+    own += [exp_ref[number, pl.ds(lax.axis_index("row"), 1), :] for number in range(exp_ref.shape[0] - 1)]
+    gains = [half for gain in own for half in (gain[:, :LANES], gain[:, LANES:])]
+    pad = -(-len(gains) // 8) * 8
+    gains += [jnp.zeros((1, LANES), jnp.float32)] * (pad - len(gains))
+    gains = jnp.concatenate(gains, axis=0).astype(jnp.bfloat16)
+    width = (rows - pad) // 2
+
+    for number in range(blocks):
+        for copy in copies[number]:
+            copy.wait()
+        span = slice(number * block, (number + 1) * block)
+        scaled = (table[:, span].astype(jnp.float32) * scale_ref[:, span]).astype(jnp.bfloat16)
+        part = mm(scaled, held[span, :])
+        if number == 0:
+            acc_ref[...] = part
+        else:
+            acc_ref[...] += part
+
+    turned = acc_ref[...].T.astype(jnp.bfloat16).reshape(parts, width, 2 * LANES)
+    out_ref[:, :width, :] = turned[:, :, :LANES]
+    out_ref[:, width : 2 * width, :] = turned[:, :, LANES:]
+    out_ref[:, 2 * width :, :] = jnp.broadcast_to(gains[None], (parts, pad, LANES))
+
+
+def encode(sources, enc_scale, encoder, comp_gain, exp_gain, parts):
     points, width = sources.shape
     skeleton = encoder.shape[0]
-    pad = gains.shape[0]
-    block = 512
-    rows = 2 * (width // parts) + pad
+    pad = gain_rows(comp_gain, exp_gain)
+    blocks = 8
     return pl.pallas_call(
-        encode_kernel,
-        grid=(points // block,),
-        in_specs=[
-            pl.BlockSpec((block, width), lambda k: (k, 0)),
-            pl.BlockSpec((1, block), lambda k: (0, k)),
-            pl.BlockSpec((skeleton, block), lambda k: (0, k)),
-            pl.BlockSpec((pad, LANES), lambda k: (0, 0)),
+        functools.partial(encode_kernel, blocks),
+        in_specs=[HBM, VMEM, HBM, VMEM, VMEM],
+        out_specs=VMEM,
+        out_shape=jax.ShapeDtypeStruct((parts, 2 * (width // parts) + pad, LANES), jnp.bfloat16),
+        scratch_shapes=[
+            pltpu.VMEM((points, width), jnp.bfloat16),
+            pltpu.VMEM((skeleton, points), jnp.bfloat16),
+            pltpu.VMEM((skeleton, width), jnp.float32),
+            pltpu.SemaphoreType.DMA((2, blocks)),
         ],
-        out_specs=pl.BlockSpec((parts, rows, LANES), lambda k: (0, 0, 0)),
-        out_shape=jax.ShapeDtypeStruct((parts, rows, LANES), jnp.bfloat16),
-        scratch_shapes=[pltpu.VMEM((skeleton, width), jnp.float32)],
-        compiler_params=pltpu.CompilerParams(dimension_semantics=("arbitrary",)),
-    )(sources, enc_scale.reshape(1, points), encoder, gains)
+    )(sources, enc_scale.reshape(1, points), encoder, comp_gain, exp_gain)
+
+
+def gain_rows(comp_gain, exp_gain):
+    sent = 2 * (comp_gain.shape[0] + exp_gain.shape[0] - 1)
+    return -(-sent // 8) * 8
 
 
 def levels_kernel(strides, pad, packed_ref, comp_ref, exp_ref, out_ref):
@@ -94,43 +118,52 @@
     boxes, rows, _ = packed.shape
     return pl.pallas_call(
         functools.partial(levels_kernel, strides, pad),
-        in_specs=[pl.BlockSpec(memory_space=pltpu.VMEM)] * 3,
-        out_specs=pl.BlockSpec(memory_space=pltpu.VMEM),
+        in_specs=[VMEM] * 3,
+        out_specs=VMEM,
         out_shape=jax.ShapeDtypeStruct((boxes, rows - pad, LANES), jnp.bfloat16),
-    )(packed, comp_transfer, exp_transfer)
-
-
-def decode_kernel(packed_ref, decoder_ref, out_ref, turned_ref):
-    @pl.when(pl.program_id(0) == 0)
-    def _():
-        boxes, rows, _ = packed_ref.shape
-        width = rows // 2
-        coeffs = jnp.concatenate([packed_ref[:, :width, :], packed_ref[:, width:, :]], axis=-1)
-        turned_ref[...] = coeffs.reshape(boxes * width, 2 * LANES).T
-
-    out_ref[...] = mm(decoder_ref[...], turned_ref[...]).astype(jnp.bfloat16)
+    )(on_chip(packed), on_chip(comp_transfer), on_chip(exp_transfer))
+
+
+def decode_kernel(blocks, packed_ref, decoder_ref, out_hbm, turned_ref, held, sems):
+    boxes, rows, _ = packed_ref.shape
+    width = rows // 2
+    block = decoder_ref.shape[0] // blocks
+    coeffs = jnp.concatenate([packed_ref[:, :width, :], packed_ref[:, width:, :]], axis=-1)
+    turned_ref[...] = coeffs.reshape(boxes * width, 2 * LANES).T
+    copies = []
+    for number in range(blocks):
+        span = pl.ds(number * block, block)
+        rows_of = slice(number * block, (number + 1) * block)
+        held[rows_of, :] = mm(decoder_ref[rows_of, :], turned_ref[...]).astype(jnp.bfloat16)
+        copies.append(pltpu.make_async_copy(held.at[span], out_hbm.at[span], sems.at[number]))
+        copies[-1].start()
+    for copy in copies:
+        copy.wait()
 
 
 def decode(packed, decoder):
     boxes, rows, _ = packed.shape
     points, skeleton = decoder.shape
     width = boxes * rows // 2
-    block = 512
+    blocks = 8
     return pl.pallas_call(
-        decode_kernel,
-        grid=(points // block,),
-        in_specs=[
-            pl.BlockSpec((boxes, rows, LANES), lambda k: (0, 0, 0)),
-            pl.BlockSpec((block, skeleton), lambda k: (k, 0)),
+        functools.partial(decode_kernel, blocks),
+        in_specs=[VMEM, VMEM],
+        out_specs=HBM,
+        out_shape=jax.ShapeDtypeStruct((points, width), jnp.bfloat16),
+        scratch_shapes=[
+            pltpu.VMEM((skeleton, width), jnp.bfloat16),
+            pltpu.VMEM((points, width), jnp.bfloat16),
+            pltpu.SemaphoreType.DMA((blocks,)),
         ],
-        out_specs=pl.BlockSpec((block, width), lambda k: (k, 0)),
-        out_shape=jax.ShapeDtypeStruct((points, width), jnp.bfloat16),
-        scratch_shapes=[pltpu.VMEM((skeleton, width), jnp.bfloat16)],
-        compiler_params=pltpu.CompilerParams(dimension_semantics=("arbitrary",)),
-    )(packed, decoder)
-
-
-def plain_encode(sources, enc_scale, encoder, gains, parts):
+    )(on_chip(packed), on_chip(decoder))
+
+
+def plain_encode(sources, enc_scale, encoder, comp_gain, exp_gain, parts):
+    own_comp = lax.dynamic_index_in_dim(comp_gain, lax.axis_index("col"), 1, keepdims=False)
+    own_exp = lax.dynamic_index_in_dim(exp_gain, lax.axis_index("row"), 1, keepdims=False)
+    gains = jnp.concatenate([own_comp, own_exp[:-1]], axis=0).astype(jnp.bfloat16).reshape(-1, LANES)
+    gains = jnp.pad(gains, ((0, gain_rows(comp_gain, exp_gain) - gains.shape[0]), (0, 0)))
     scaled = (encoder.astype(jnp.float32) * enc_scale[None, :]).astype(jnp.bfloat16)
     coeffs = mm(sources, scaled, (((0,), (1,)), ((), ()))).astype(jnp.bfloat16)
     coeffs = coeffs.reshape(parts, -1, 2, LANES).swapaxes(1, 2).reshape(parts, -1, LANES)
@@ -182,21 +215,19 @@
     strides = tuple(row_count * 2**number for number in range(comp_levels)) + tuple(
         2**number for number in range(exp_levels)
     )
-    own_comp = lax.dynamic_index_in_dim(comp_gain[:, 0], lax.axis_index("col"), 1, keepdims=False)
-    own_exp = lax.dynamic_index_in_dim(exp_gain[:, 0], lax.axis_index("row"), 1, keepdims=False)
-    sent = jnp.concatenate([own_comp, own_exp[:-1]], axis=0).astype(jnp.bfloat16).reshape(-1, LANES)
-    pad = -(-sent.shape[0] // 8) * 8
-    sent = jnp.pad(sent, ((0, pad - sent.shape[0]), (0, 0)))
+    comp_gain, exp_gain = comp_gain[:, 0], exp_gain[:, 0]
+    pad = gain_rows(comp_gain, exp_gain)
+    last_gain = lax.dynamic_index_in_dim(exp_gain[-1], lax.axis_index("row"), 0, keepdims=False)
 
     kernels = (sources.shape[1] // parts) % 16 == 0 and skeleton == 2 * LANES
     run_encode, run_levels, run_decode = (
         (encode, levels, decode) if kernels else (plain_encode, plain_levels, plain_decode)
     )
-    packed = run_encode(sources, enc_scale, encoder, sent, parts)
+    packed = run_encode(sources, enc_scale, encoder, comp_gain, exp_gain, parts)
     packed = lax.all_to_all(packed, AXES, 0, 0, tiled=True)
     result = run_levels(packed, comp_transfer, exp_transfer, strides, pad)
     result = lax.all_to_all(result, AXES, 0, 0, tiled=True)
-    factors = dec_scale[:, None] * own_exp[-1][None, :]
+    factors = dec_scale[:, None] * last_gain[None, :]
     scaled = (decoder.astype(jnp.float32) * factors).astype(jnp.bfloat16)
     return run_decode(result, scaled)
 

time: 69.4 us -> 56.2 us (0.81)
  Pallas kernels: 22.1 us -> 12.8 us
  local copies, waits for them, and re-layouts: 3.72 us -> 0.73 us
  waiting for transfers between devices: 30.6 us -> 29.7 us
    pallas_call x2, Pallas kernels: 17.7 us -> 10.3 us  [the longest x1 6.41 us: encode(): pl.pallas_call(functools.partial(encode_kernel, blocks), in_specs=[HBM, V...]
    unnamed x12 -> x6, local copies, waits for them, and re-layouts: 2.38 us -> 0.01 us
    pallas_call x1, Pallas kernels: 4.41 us -> 2.49 us  [levels(): pl.pallas_call(functools.partial(levels_kernel, strides, pad), in_specs=[...]
    all_to_all x1, waiting for transfers between devices: 16.8 us -> 16.1 us  [body(): packed = lax.all_to_all(packed, AXES, 0, 0, tiled=True)]
    dynamic_slice x1, local copies, waits for them, and re-layouts: 0.71 us -> 0.01 us  [body(): lax.dynamic_index_in_dim(exp_gain[-1], lax.axis_index('row'), 0, keepdims...]
  transfers between devices with their start and end apart: 2 -> 2, of which waited for: 2 -> 2; matrix products, arithmetic and copies ran while one was open for 3% -> 5% of each run, Pallas kernels for 0% -> 0%
where the time goes in v2:
time: 56.2 us; the launch traced here: 55.8 us
  waiting for transfers between devices  29.7 us (53%)
  Pallas kernels  12.8 us (23%)
  starting transfers between devices  10.5 us (19%)
  other arithmetic  1.94 us (3%)
  local copies, waits for them, and re-layouts  0.73 us (1%)
    all_to_all x1, waiting for transfers between devices, body(): packed = lax.all_to_all(packed, AXES, 0, 0, tiled=True)  16.1 us
    all_to_all x1, waiting for transfers between devices, body(): result = lax.all_to_all(result, AXES, 0, 0, tiled=True)  13.6 us
    all_to_all x1, starting transfers between devices, body(): packed = lax.all_to_all(packed, AXES, 0, 0, tiled=True)  7.33 us
    pallas_call x1, Pallas kernels, encode(): pl.pallas_call(functools.partial(encode_kernel, blocks), in_specs=[HBM, V...  6.41 us
    pallas_call x1, Pallas kernels, decode(): pl.pallas_call(functools.partial(decode_kernel, blocks), in_specs=[VMEM,...  3.9 us
    all_to_all x1, starting transfers between devices, body(): result = lax.all_to_all(result, AXES, 0, 0, tiled=True)  3.19 us
    pallas_call x1, Pallas kernels, levels(): pl.pallas_call(functools.partial(levels_kernel, strides, pad), in_specs=[...  2.49 us
    convert_element_type x1, other arithmetic, body(): scaled = (decoder.astype(jnp.float32) * factors).astype(jnp.bfloat16)  1.94 us
  transfers between devices with their start and end apart: 2, of which 2 were waited for; matrix products, arithmetic and copies ran while one was open for 5% of the time, Pallas kernels for 0%

profile of v2, /device:TPU:0, one launch (start us, length us, event | category | flops | bytes accessed | tf_op | source)
XLA Modules:
  0.0 55.8 jit_solution(11516469326269172675)
XLA Ops:
  0.0 0.0 copy-start
  0.0 0.0 copy-start.1
  0.0 6.4 %shard_map.91 = bf16[32,72,128]{2,1,0:T(8,128)(2,1)} custom-call(bf16[4096,1024]{1,0:T(8,128)(2,1)} %sources_hbm.1, f32[1,4096]{1,0:T(1,128)} %bitcast.5, bf16[256,4096]{1,0:T(8,128)(2,1)} %encoder_hbm.1, f32[2,4,256]{2,1,0:T(4,128)} %bitcast.6, f32[3,8,256]{2,1,0:T(8,128)} %bitcast.4), custom_call_target="tpu_custom_call" | custom-call | tf_op jit(solution)/shard_map/pallas_call | solution.py:70
  6.4 0.0 copy-start.2
  6.4 7.3 %all-to-all-start = ((bf16[32,72,128]{2,1,0:T(8,128)(2,1)}), bf16[32,72,128]{2,1,0:T(8,128)(2,1)S(1)}, u32[]{:S(2)}, u32[]{:S(2)}) async-start(bf16[32,72,128]{2,1,0:T(8,128)(2,1)} %shard_map.91), calls=%async_computation | async-start | bytes 1179648 | tf_op jit(solution)/shard_map/all_to_all | solution.py:227
  13.8 0.7 %slice.4 = f32[1,1,8,256]{3,2,1,0:T(8,128)S(1)} slice(f32[3,1,8,256]{3,2,1,0:T(8,128)} %param.15), slice={[2:3], [0:1], [0:8], [0:256]} | slice | bytes 16384 | tf_op jit(solution)/shard_map/slice | solution.py:220
  14.5 16.1 %all-to-all-done.packed_ref = bf16[32,72,128]{2,1,0:T(8,128)(2,1)S(1)} async-done(((bf16[32,72,128]{2,1,0:T(8,128)(2,1)}), bf16[32,72,128]{2,1,0:T(8,128)(2,1)S(1)}, u32[]{:S(2)}, u32[]{:S(2)}) %all-to-all-start) | async-done | bytes 589856 | tf_op jit(solution)/shard_map/all_to_all | solution.py:227
  30.6 0.0 copy-done
  30.6 0.0 copy-done.1
  30.6 2.5 %shard_map.92 = bf16[32,64,128]{2,1,0:T(8,128)(2,1)} custom-call(bf16[32,72,128]{2,1,0:T(8,128)(2,1)S(1)} %all-to-all-done.packed_ref, bf16[2,512,512]{2,1,0:T(8,128)(2,1)S(1)} %copy-done.1, bf16[3,512,512]{2,1,0:T(8,128)(2,1)S(1)} %copy-done), custom_call_target="tpu_custom_call" | custom-call | tf_op jit(solution)/shard_map/pallas_call | solution.py:119
  33.1 3.2 %all-to-all-start.1 = ((bf16[32,64,128]{2,1,0:T(8,128)(2,1)}), bf16[32,64,128]{2,1,0:T(8,128)(2,1)S(1)}, u32[]{:S(2)}, u32[]{:S(2)}) async-start(bf16[32,64,128]{2,1,0:T(8,128)(2,1)} %shard_map.92), calls=%async_computation.1 | async-start | bytes 1048576 | tf_op jit(solution)/shard_map/all_to_all | solution.py:229
  36.3 0.0 copy-done.2
  36.3 1.9 %multiply_convert_fusion.decoder_ref = bf16[4096,256]{1,0:T(8,128)(2,1)S(1)} fusion(bf16[4096,256]{1,0:T(8,128)(2,1)} %param.16, f32[256]{0:T(256)S(1)} %bitcast.7, f32[4096]{0:T(1024)S(1)} %copy-done.2), kind=kLoop, calls=%fused_computation | loop fusion | flops 4194304 | bytes 4211712 | tf_op jit(solution)/shard_map/convert_element_type | solution.py:231
  38.2 13.6 %all-to-all-done.1.packed_ref = bf16[32,64,128]{2,1,0:T(8,128)(2,1)S(1)} async-done(((bf16[32,64,128]{2,1,0:T(8,128)(2,1)}), bf16[32,64,128]{2,1,0:T(8,128)(2,1)S(1)}, u32[]{:S(2)}, u32[]{:S(2)}) %all-to-all-start.1) | async-done | bytes 524320 | tf_op jit(solution)/shard_map/all_to_all | solution.py:229
  51.9 3.9 %shard_map.93 = bf16[4096,1024]{1,0:T(8,128)(2,1)} custom-call(bf16[32,64,128]{2,1,0:T(8,128)(2,1)S(1)} %all-to-all-done.1.packed_ref, bf16[4096,256]{1,0:T(8,128)(2,1)S(1)} %multiply_convert_fusion.decoder_ref), custom_call_target="tpu_custom_call" | custom-call | tf_op jit(solution)/shard_map/pallas_call | solution.py:149
  (1 shorter events, 0.0 us)
Async XLA Ops:
  0.0 30.6 %copy-start = (bf16[3,512,512]{2,1,0:T(8,128)(2,1)S(1)}, bf16[3,512,512]{2,1,0:T(8,128)(2,1)}, u32[]{:S(2)}) copy-start(bf16[3,512,512]{2,1,0:T(8,128)(2,1)} %exp_ref.1) | copy-start | bytes 4718596
  0.0 30.6 %copy-start.1 = (bf16[2,512,512]{2,1,0:T(8,128)(2,1)S(1)}, bf16[2,512,512]{2,1,0:T(8,128)(2,1)}, u32[]{:S(2)}) copy-start(bf16[2,512,512]{2,1,0:T(8,128)(2,1)} %comp_ref.1) | copy-start | bytes 3145732
  6.4 29.9 %copy-start.2 = (f32[4096]{0:T(1024)S(1)}, f32[4096]{0:T(1024)}, u32[]{:S(2)}) copy-start(f32[4096]{0:T(1024)} %param.17) | copy-start | bytes 49156
  6.4 24.1 %all-to-all-start = ((bf16[32,72,128]{2,1,0:T(8,128)(2,1)}), bf16[32,72,128]{2,1,0:T(8,128)(2,1)S(1)}, u32[]{:S(2)}, u32[]{:S(2)}) async-start(bf16[32,72,128]{2,1,0:T(8,128)(2,1)} %shard_map.91), calls=%async_computation | async-start | bytes 1179648 | tf_op jit(solution)/shard_map/all_to_all | solution.py:227
  33.1 18.8 %all-to-all-start.1 = ((bf16[32,64,128]{2,1,0:T(8,128)(2,1)}), bf16[32,64,128]{2,1,0:T(8,128)(2,1)S(1)}, u32[]{:S(2)}, u32[]{:S(2)}) async-start(bf16[32,64,128]{2,1,0:T(8,128)(2,1)} %shard_map.92), calls=%async_computation.1 | async-start | bytes 1048576 | tf_op jit(solution)/shard_map/all_to_all | solution.py:229

commit v3 on v2

--- a/solution.py
+++ b/solution.py
@@ -7,10 +7,11 @@
 from jax.experimental.pallas import tpu as pltpu
 from jax.sharding import PartitionSpec as P
 
+
 AXES = ("col", "row")
 LANES = 128
 NT = (((1,), (1,)), ((), ()))
-HBM = pl.BlockSpec(memory_space=pl.ANY)
+HBM = pl.BlockSpec(memory_space=pltpu.HBM)
 VMEM = pl.BlockSpec(memory_space=pltpu.VMEM)
 
 
@@ -18,24 +19,55 @@
     return pltpu.with_memory_space_constraint(value, pltpu.VMEM)
 
 
+def in_hbm(value):
+    return pltpu.with_memory_space_constraint(value, pltpu.HBM)
+
+
 def mm(a, b, dims=(((1,), (0,)), ((), ()))):
     return lax.dot_general(a, b, dims, preferred_element_type=jnp.float32)
 
 
-def encode_kernel(blocks, sources_hbm, scale_ref, encoder_hbm, comp_ref, exp_ref, out_ref, held, table, acc_ref, sems):
+def start_loads(blocks, first, sources_hbm, encoder_hbm, held, table, sems):
     block = sources_hbm.shape[0] // blocks
     copies = []
     for number in range(blocks):
         span = pl.ds(number * block, block)
+        wanted = sources_hbm.at[span, pl.ds(first, held.shape[1])]
         copies.append(
             (
                 pltpu.make_async_copy(encoder_hbm.at[:, span], table.at[:, span], sems.at[0, number]),
-                pltpu.make_async_copy(sources_hbm.at[span], held.at[span], sems.at[1, number]),
+                pltpu.make_async_copy(wanted, held.at[span], sems.at[1, number]),
             )
         )
         for copy in copies[-1]:
             copy.start()
-
+    return copies
+
+
+def add_up(copies, scale_ref, held, table, acc_ref):
+    block = held.shape[0] // len(copies)
+    for number, pair in enumerate(copies):
+        for copy in pair:
+            copy.wait()
+        span = slice(number * block, (number + 1) * block)
+        scaled = (table[:, span].astype(jnp.float32) * scale_ref[:, span]).astype(jnp.bfloat16)
+        part = mm(scaled, held[span, :])
+        if number == 0:
+            acc_ref[...] = part
+        else:
+            acc_ref[...] += part
+
+
+def encode_kernel(
+    blocks, first, sources_hbm, scale_hbm, encoder_hbm, comp_hbm, exp_hbm, out_ref, held, table, acc_ref, sems, scale_ref, comp_ref, exp_ref, small
+):
+    pairs = ((scale_hbm, scale_ref), (comp_hbm, comp_ref), (exp_hbm, exp_ref))
+    first_copies = [pltpu.make_async_copy(*pair, small.at[number]) for number, pair in enumerate(pairs)]
+    for copy in first_copies:
+        copy.start()
+    copies = start_loads(blocks, first, sources_hbm, encoder_hbm, held, table, sems)
+    for copy in first_copies:
+        copy.wait()
     parts, rows, _ = out_ref.shape
     own = [comp_ref[number, pl.ds(lax.axis_index("col"), 1), :] for number in range(comp_ref.shape[0])]
     own += [exp_ref[number, pl.ds(lax.axis_index("row"), 1), :] for number in range(exp_ref.shape[0] - 1)]
@@ -44,32 +76,23 @@
     gains += [jnp.zeros((1, LANES), jnp.float32)] * (pad - len(gains))
     gains = jnp.concatenate(gains, axis=0).astype(jnp.bfloat16)
     width = (rows - pad) // 2
-
-    for number in range(blocks):
-        for copy in copies[number]:
-            copy.wait()
-        span = slice(number * block, (number + 1) * block)
-        scaled = (table[:, span].astype(jnp.float32) * scale_ref[:, span]).astype(jnp.bfloat16)
-        part = mm(scaled, held[span, :])
-        if number == 0:
-            acc_ref[...] = part
-        else:
-            acc_ref[...] += part
-
-    turned = acc_ref[...].T.astype(jnp.bfloat16).reshape(parts, width, 2 * LANES)
-    out_ref[:, :width, :] = turned[:, :, :LANES]
-    out_ref[:, width : 2 * width, :] = turned[:, :, LANES:]
+    add_up(copies, scale_ref, held, table, acc_ref)
+    turned = acc_ref[...].T.reshape(parts, width, 2 * LANES)
+    out_ref[:, :width, :] = turned[:, :, :LANES].astype(jnp.bfloat16)
+    out_ref[:, width : 2 * width, :] = turned[:, :, LANES:].astype(jnp.bfloat16)
     out_ref[:, 2 * width :, :] = jnp.broadcast_to(gains[None], (parts, pad, LANES))
 
 
-def encode(sources, enc_scale, encoder, comp_gain, exp_gain, parts):
+def encode(sources, enc_scale, encoder, comp_gain, exp_gain, parts, first):
     points, width = sources.shape
+    width -= first
     skeleton = encoder.shape[0]
     pad = gain_rows(comp_gain, exp_gain)
     blocks = 8
     return pl.pallas_call(
-        functools.partial(encode_kernel, blocks),
-        in_specs=[HBM, VMEM, HBM, VMEM, VMEM],
+        functools.partial(encode_kernel, blocks, first),
+        in_specs=[HBM] * 5,
+        compiler_params=pltpu.CompilerParams(vmem_limit_bytes=20 * 2**20),
         out_specs=VMEM,
         out_shape=jax.ShapeDtypeStruct((parts, 2 * (width // parts) + pad, LANES), jnp.bfloat16),
         scratch_shapes=[
@@ -77,8 +100,64 @@
             pltpu.VMEM((skeleton, points), jnp.bfloat16),
             pltpu.VMEM((skeleton, width), jnp.float32),
             pltpu.SemaphoreType.DMA((2, blocks)),
+            pltpu.VMEM((1, points), jnp.float32),
+            pltpu.VMEM(comp_gain.shape, jnp.float32),
+            pltpu.VMEM(exp_gain.shape, jnp.float32),
+            pltpu.SemaphoreType.DMA((3,)),
         ],
-    )(sources, enc_scale.reshape(1, points), encoder, comp_gain, exp_gain)
+    )(sources, in_hbm(enc_scale.reshape(1, points)), encoder, in_hbm(comp_gain), in_hbm(exp_gain))
+
+
+def side_encode_kernel(blocks, sources_hbm, scale_ref, encoder_hbm, out_ref, held, table, acc_ref, sems):
+    copies = start_loads(blocks, 0, sources_hbm, encoder_hbm, held, table, sems)
+    add_up(copies, scale_ref, held, table, acc_ref)
+    out_ref[...] = acc_ref[...].astype(jnp.bfloat16)
+
+
+def side_encode(sources, enc_scale, encoder, width):
+    points = sources.shape[0]
+    skeleton = encoder.shape[0]
+    blocks = 8
+    return pl.pallas_call(
+        functools.partial(side_encode_kernel, blocks),
+        in_specs=[HBM, VMEM, HBM],
+        compiler_params=pltpu.CompilerParams(vmem_limit_bytes=12 * 2**20),
+        out_specs=VMEM,
+        out_shape=jax.ShapeDtypeStruct((skeleton, width), jnp.bfloat16),
+        scratch_shapes=[
+            pltpu.VMEM((points, width), jnp.bfloat16),
+            pltpu.VMEM((skeleton, points), jnp.bfloat16),
+            pltpu.VMEM((skeleton, width), jnp.float32),
+            pltpu.SemaphoreType.DMA((2, blocks)),
+        ],
+    )(sources, enc_scale.reshape(1, points), encoder)
+
+
+def side_level_kernel(axis, bit, number, scaled, own_ref, partner_ref, transfer_ref, gain_ref, out_ref):
+    skeleton = own_ref.shape[0]
+    position = lax.axis_index(axis)
+    upper = position // 2**bit % 2
+    here = pl.multiple_of(upper * skeleton, skeleton)
+    there = pl.multiple_of((1 - upper) * skeleton, skeleton)
+    rows = pl.ds(here, skeleton)
+    mixed = mm(transfer_ref[number, rows, pl.ds(here, skeleton)], own_ref[...])
+    mixed += mm(transfer_ref[number, rows, pl.ds(there, skeleton)], partner_ref[...])
+    if scaled:
+        gain = jnp.broadcast_to(gain_ref[number, pl.ds(position, 1), :], (8, skeleton)).T
+        mixed *= gain[:, :1]
+    out_ref[...] = mixed.astype(jnp.bfloat16)
+
+
+def side_level(own, axis, bit, number, scaled, transfer, gain):
+    pairs = [(source, source ^ 2**bit) for source in range(lax.axis_size(axis))]
+    partner = lax.ppermute(own, axis, pairs)
+    return pl.pallas_call(
+        functools.partial(side_level_kernel, axis, bit, number, scaled),
+        in_specs=[VMEM] * 4,
+        compiler_params=pltpu.CompilerParams(vmem_limit_bytes=8 * 2**20),
+        out_specs=VMEM,
+        out_shape=jax.ShapeDtypeStruct(own.shape, jnp.bfloat16),
+    )(on_chip(own), on_chip(partner), transfer, gain)
 
 
 def gain_rows(comp_gain, exp_gain):
@@ -91,16 +170,17 @@
     width = (rows - pad) // 2
     skeleton = 2 * LANES
     state = jnp.concatenate([packed_ref[:, :width, :], packed_ref[:, width : 2 * width, :]], axis=-1)
+    state = state.astype(jnp.float32)
     gains = packed_ref[:, 2 * width :, :].astype(jnp.float32)
     for number, stride in enumerate(strides):
         turned = number >= comp_ref.shape[0]
         transfer = exp_ref[number - comp_ref.shape[0]] if turned else comp_ref[number]
         halves = state.reshape(boxes // (2 * stride), 2, stride * width, skeleton)
-        low = halves[:, 0].reshape(boxes // 2 * width, skeleton)
-        high = halves[:, 1].reshape(boxes // 2 * width, skeleton)
+        low = halves[:, 0].reshape(boxes // 2 * width, skeleton).astype(jnp.bfloat16)
+        high = halves[:, 1].reshape(boxes // 2 * width, skeleton).astype(jnp.bfloat16)
         mixed = mm(low, transfer[:, :skeleton], NT) + mm(high, transfer[:, skeleton:], NT)
         shape = (boxes // (2 * stride), 1, stride, width, skeleton)
-        both = jnp.concatenate(
+        state = jnp.concatenate(
             [mixed[:, :skeleton].reshape(shape), mixed[:, skeleton:].reshape(shape)], axis=1
         ).reshape(boxes, width, skeleton)
         if number + 1 < len(strides):
@@ -108,10 +188,9 @@
                 [gains[:, 2 * number : 2 * number + 1, :], gains[:, 2 * number + 1 : 2 * number + 2, :]],
                 axis=-1,
             )
-            both = both * gain
-        state = both.astype(jnp.bfloat16)
-    out_ref[:, :width, :] = state[:, :, :LANES]
-    out_ref[:, width:, :] = state[:, :, LANES:]
+            state = state * gain
+    out_ref[:, :width, :] = state[:, :, :LANES].astype(jnp.bfloat16)
+    out_ref[:, width:, :] = state[:, :, LANES:].astype(jnp.bfloat16)
 
 
 def levels(packed, comp_transfer, exp_transfer, strides, pad):
@@ -119,17 +198,20 @@
     return pl.pallas_call(
         functools.partial(levels_kernel, strides, pad),
         in_specs=[VMEM] * 3,
+        compiler_params=pltpu.CompilerParams(vmem_limit_bytes=20 * 2**20),
         out_specs=VMEM,
         out_shape=jax.ShapeDtypeStruct((boxes, rows - pad, LANES), jnp.bfloat16),
-    )(on_chip(packed), on_chip(comp_transfer), on_chip(exp_transfer))
-
-
-def decode_kernel(blocks, packed_ref, decoder_ref, out_hbm, turned_ref, held, sems):
+    )(on_chip(packed), comp_transfer, exp_transfer)
+
+
+def decode_kernel(blocks, side_ref, packed_ref, decoder_ref, out_hbm, turned_ref, held, sems):
     boxes, rows, _ = packed_ref.shape
-    width = rows // 2
+    width, side = rows // 2, side_ref.shape[1]
+    coeffs = jnp.concatenate([packed_ref[:, :width, :], packed_ref[:, width:, :]], axis=-1)
+    coeffs = coeffs.astype(jnp.float32).reshape(boxes * width, 2 * LANES)
+    turned_ref[:, :side] = side_ref[...]
+    turned_ref[:, side:] = coeffs.T.astype(jnp.bfloat16)
     block = decoder_ref.shape[0] // blocks
-    coeffs = jnp.concatenate([packed_ref[:, :width, :], packed_ref[:, width:, :]], axis=-1)
-    turned_ref[...] = coeffs.reshape(boxes * width, 2 * LANES).T
     copies = []
     for number in range(blocks):
         span = pl.ds(number * block, block)
@@ -141,14 +223,15 @@
         copy.wait()
 
 
-def decode(packed, decoder):
+def decode(side, packed, decoder):
     boxes, rows, _ = packed.shape
     points, skeleton = decoder.shape
-    width = boxes * rows // 2
+    width = side.shape[1] + boxes * rows // 2
     blocks = 8
     return pl.pallas_call(
         functools.partial(decode_kernel, blocks),
-        in_specs=[VMEM, VMEM],
+        in_specs=[VMEM, VMEM, VMEM],
+        compiler_params=pltpu.CompilerParams(vmem_limit_bytes=20 * 2**20),
         out_specs=HBM,
         out_shape=jax.ShapeDtypeStruct((points, width), jnp.bfloat16),
         scratch_shapes=[
@@ -156,7 +239,7 @@
             pltpu.VMEM((points, width), jnp.bfloat16),
             pltpu.SemaphoreType.DMA((blocks,)),
         ],
-    )(on_chip(packed), on_chip(decoder))
+    )(on_chip(side), on_chip(packed), decoder)
 
 
 def plain_encode(sources, enc_scale, encoder, comp_gain, exp_gain, parts):
@@ -218,18 +301,31 @@
     comp_gain, exp_gain = comp_gain[:, 0], exp_gain[:, 0]
     pad = gain_rows(comp_gain, exp_gain)
     last_gain = lax.dynamic_index_in_dim(exp_gain[-1], lax.axis_index("row"), 0, keepdims=False)
-
-    kernels = (sources.shape[1] // parts) % 16 == 0 and skeleton == 2 * LANES
-    run_encode, run_levels, run_decode = (
-        (encode, levels, decode) if kernels else (plain_encode, plain_levels, plain_decode)
-    )
-    packed = run_encode(sources, enc_scale, encoder, comp_gain, exp_gain, parts)
+    factors = dec_scale[:, None] * last_gain[None, :]
+    width = sources.shape[1]
+    side = width // 4
+
+    if side % LANES or (width - side) % (8 * parts) or skeleton != 2 * LANES:
+        packed = plain_encode(sources, enc_scale, encoder, comp_gain, exp_gain, parts)
+        packed = lax.all_to_all(packed, AXES, 0, 0, tiled=True)
+        packed = plain_levels(packed, comp_transfer, exp_transfer, strides, pad)
+        packed = lax.all_to_all(packed, AXES, 0, 0, tiled=True)
+        return plain_decode(packed, (decoder.astype(jnp.float32) * factors).astype(jnp.bfloat16))
+
+    comp_transfer, exp_transfer = on_chip(comp_transfer), on_chip(exp_transfer)
+    sources, encoder = in_hbm(sources), in_hbm(encoder)
+    packed = encode(sources, enc_scale, encoder, comp_gain, exp_gain, parts, side)
     packed = lax.all_to_all(packed, AXES, 0, 0, tiled=True)
-    result = run_levels(packed, comp_transfer, exp_transfer, strides, pad)
-    result = lax.all_to_all(result, AXES, 0, 0, tiled=True)
-    factors = dec_scale[:, None] * last_gain[None, :]
-    scaled = (decoder.astype(jnp.float32) * factors).astype(jnp.bfloat16)
-    return run_decode(result, scaled)
+    coeffs = side_encode(sources, enc_scale, encoder, side)
+    for number in range(comp_levels):
+        coeffs = side_level(coeffs, "col", number, number, True, comp_transfer, comp_gain)
+    packed = levels(packed, comp_transfer, exp_transfer, strides, pad)
+    packed = lax.all_to_all(packed, AXES, 0, 0, tiled=True)
+    for number in range(exp_levels):
+        scaled = number + 1 < exp_levels
+        coeffs = side_level(coeffs, "row", number, number, scaled, exp_transfer, exp_gain)
+    scaled = on_chip((decoder.astype(jnp.float32) * factors).astype(jnp.bfloat16))
+    return decode(coeffs, packed, scaled)
 
 
 def solution(mesh):
@@ -244,4 +340,8 @@
         P(),
         P(AXES),
     )
-    return jax.shard_map(body, mesh=mesh, in_specs=in_specs, out_specs=P(AXES, None), check_vma=False)
+
+    def step(*args):
+        return jax.shard_map(body, mesh=mesh, in_specs=in_specs, out_specs=P(AXES, None), check_vma=False)(*args)
+
+    return step

time: 56.2 us -> 71.2 us (1.27)
  starting transfers between devices: 10.5 us -> 19.7 us
  Pallas kernels: 12.8 us -> 17.7 us
  other arithmetic: 1.94 us -> 2.9 us
  local copies, waits for them, and re-layouts: 0.73 us -> 1.64 us
  waiting for transfers between devices: 29.7 us -> 28.8 us
    ppermute x0 -> x5, waiting for transfers between devices: none -> 18.7 us  [side_level(): partner = lax.ppermute(own, axis, pairs)]
    all_to_all x1 -> x0, waiting for transfers between devices: 13.6 us -> none  [body(): result = lax.all_to_all(result, AXES, 0, 0, tiled=True)]
    ppermute x0 -> x5, starting transfers between devices: none -> 8.37 us  [side_level(): partner = lax.ppermute(own, axis, pairs)]
    all_to_all x1 -> x2, waiting for transfers between devices: 16.1 us -> 10.1 us  [body(): packed = lax.all_to_all(packed, AXES, 0, 0, tiled=True)]
    pallas_call x1 -> x7, Pallas kernels: 6.41 us -> 11.6 us  [the longest x1 7.21 us: encode(): pl.pallas_call(functools.partial(encode_kernel, blocks, first), in_specs=...]
    all_to_all x1 -> x2, starting transfers between devices: 7.33 us -> 11.4 us  [body(): packed = lax.all_to_all(packed, AXES, 0, 0, tiled=True)]
    all_to_all x1 -> x0, starting transfers between devices: 3.19 us -> none  [body(): result = lax.all_to_all(result, AXES, 0, 0, tiled=True)]
    unnamed x6 -> x14, local copies, waits for them, and re-layouts: 0.01 us -> 1.63 us
  transfers between devices with their start and end apart: 2 -> 7, of which waited for: 2 -> 5; matrix products, arithmetic and copies ran while one was open for 5% -> 4% of each run, Pallas kernels for 0% -> 9%
where the time goes in v3:
time: 71.2 us; the launch traced here: 70.9 us
  waiting for transfers between devices  28.8 us (40%)
  starting transfers between devices  19.7 us (28%)
  Pallas kernels  17.7 us (25%)
  other arithmetic  2.9 us (4%)
  local copies, waits for them, and re-layouts  1.64 us (2%)
    ppermute x5, waiting for transfers between devices, side_level(): partner = lax.ppermute(own, axis, pairs)  18.7 us
    all_to_all x2, starting transfers between devices, body(): packed = lax.all_to_all(packed, AXES, 0, 0, tiled=True)  11.4 us
    all_to_all x2, waiting for transfers between devices, body(): packed = lax.all_to_all(packed, AXES, 0, 0, tiled=True)  10.1 us
    ppermute x5, starting transfers between devices, side_level(): partner = lax.ppermute(own, axis, pairs)  8.37 us
    pallas_call x1, Pallas kernels, encode(): pl.pallas_call(functools.partial(encode_kernel, blocks, first), in_specs=...  7.21 us
    pallas_call x1, Pallas kernels, decode(): pl.pallas_call(functools.partial(decode_kernel, blocks), in_specs=[VMEM,...  3.88 us
    pallas_call x1, Pallas kernels, side_encode(): pl.pallas_call(functools.partial(side_encode_kernel, blocks), in_specs=[H...  2.93 us
    convert_element_type x1, other arithmetic, body(): (decoder.astype(jnp.float32) * factors).astype(jnp.bfloat16)  2.9 us
  transfers between devices with their start and end apart: 7, of which 5 were waited for; matrix products, arithmetic and copies ran while one was open for 4% of the time, Pallas kernels for 9%

profile of v3, /device:TPU:0, one launch (start us, length us, event | category | flops | bytes accessed | tf_op | source)
XLA Modules:
  0.0 70.9 jit_solution(14921015018923867982)
XLA Ops:
  0.0 0.0 copy-start.5
  0.0 7.2 %shard_map.97 = bf16[32,56,128]{2,1,0:T(8,128)(2,1)} custom-call(bf16[4096,1024]{1,0:T(8,128)(2,1)} %sources_hbm.3, f32[1,4096]{1,0:T(1,128)} %bitcast.11, bf16[256,4096]{1,0:T(8,128)(2,1)} %encoder_hbm.3, f32[2,4,256]{2,1,0:T(4,128)} %bitcast.8, f32[3,8,256]{2,1,0:T(8,128)} %bitcast.4), custom_call_target="tpu_custom_call" | custom-call | tf_op jit(solution)/shard_map/pallas_call | solution.py:92
  7.2 7.1 %all-to-all-start = ((bf16[32,56,128]{2,1,0:T(8,128)(2,1)}), bf16[32,56,128]{2,1,0:T(8,128)(2,1)S(1)}, u32[]{:S(2)}, u32[]{:S(2)}) async-start(bf16[32,56,128]{2,1,0:T(8,128)(2,1)} %shard_map.97), calls=%async_computation | async-start | bytes 917504 | tf_op jit(solution)/shard_map/all_to_all | solution.py:318
  14.4 0.0 copy-done.5
  14.4 0.0 copy-start.1
  14.4 0.0 copy-start.4
  14.4 0.0 copy-start
  14.4 0.0 copy-start.3
  14.4 2.9 %shard_map.91.own_ref = bf16[256,256]{1,0:T(8,128)(2,1)S(1)} custom-call(bf16[4096,1024]{1,0:T(8,128)(2,1)} %sources_hbm.3, f32[1,4096]{1,0:T(1,128)S(1)} %bitcast.12, bf16[256,4096]{1,0:T(8,128)(2,1)} %encoder_hbm.3), custom_call_target="tpu_custom_call" | custom-call | tf_op jit(solution)/shard_map/pallas_call | solution.py:121
  17.4 1.8 %collective-permute-start = (bf16[256,256]{1,0:T(8,128)(2,1)S(1)}, bf16[256,256]{1,0:T(8,128)(2,1)S(1)}, u32[]{:S(2)}, u32[]{:S(2)}) collective-permute-start(bf16[256,256]{1,0:T(8,128)(2,1)S(1)} %shard_map.91.own_ref), channel_id=1, source_target_pairs={{0,8},{8,0},{16,24},{24,16},{1,9},{9,1},{17,25},{25,17},{2,10},{10... | collective-permute-start | bytes 393224 | tf_op jit(solution)/shard_map/ppermute | solution.py:153
  19.2 7.3 %collective-permute-done.partner_ref = bf16[256,256]{1,0:T(8,128)(2,1)S(1)} collective-permute-done((bf16[256,256]{1,0:T(8,128)(2,1)S(1)}, bf16[256,256]{1,0:T(8,128)(2,1)S(1)}, u32[]{:S(2)}, u32[]{:S(2)}) %collective-permute-start) | collective-permute-done | bytes 131104 | tf_op jit(solution)/shard_map/ppermute | solution.py:153
  26.5 0.0 copy-done.1
  26.5 0.0 copy-done.4
  26.5 0.3 shard_map.92.own_ref
  26.8 3.4 %collective-permute-start.1 = (bf16[256,256]{1,0:T(8,128)(2,1)S(1)}, bf16[256,256]{1,0:T(8,128)(2,1)S(1)}, u32[]{:S(2)}, u32[]{:S(2)}) collective-permute-start(bf16[256,256]{1,0:T(8,128)(2,1)S(1)} %shard_map.92.own_ref), channel_id=1, source_target_pairs={{0,16},{8,24},{16,0},{24,8},{1,17},{9,25},{17,1},{25,9},{2,18},{10... | collective-permute-start | bytes 393224 | tf_op jit(solution)/shard_map/ppermute | solution.py:153
  30.2 6.0 %collective-permute-done.1.partner_ref = bf16[256,256]{1,0:T(8,128)(2,1)S(1)} collective-permute-done((bf16[256,256]{1,0:T(8,128)(2,1)S(1)}, bf16[256,256]{1,0:T(8,128)(2,1)S(1)}, u32[]{:S(2)}, u32[]{:S(2)}) %collective-permute-start.1) | collective-permute-done | bytes 131104 | tf_op jit(solution)/shard_map/ppermute | solution.py:153
  36.2 0.3 shard_map.93.own_ref
  36.5 0.0 copy-start.6
  36.5 0.1 collective-permute-start.2
  36.6 1.3 %collective-permute-done.2.partner_ref = bf16[256,256]{1,0:T(8,128)(2,1)S(1)} collective-permute-done((bf16[256,256]{1,0:T(8,128)(2,1)S(1)}, bf16[256,256]{1,0:T(8,128)(2,1)S(1)}, u32[]{:S(2)}, u32[]{:S(2)}) %collective-permute-start.2) | collective-permute-done | bytes 131104 | tf_op jit(solution)/shard_map/ppermute | solution.py:153
  37.9 0.0 copy-done
  37.9 0.0 copy-done.3
  37.9 0.3 shard_map.94.own_ref
  38.2 1.5 %collective-permute-start.3 = (bf16[256,256]{1,0:T(8,128)(2,1)S(1)}, bf16[256,256]{1,0:T(8,128)(2,1)S(1)}, u32[]{:S(2)}, u32[]{:S(2)}) collective-permute-start(bf16[256,256]{1,0:T(8,128)(2,1)S(1)} %shard_map.94.own_ref), channel_id=1, source_target_pairs={{0,2},{1,3},{2,0},{3,1},{4,6},{5,7},{6,4},{7,5},{8,10},{9,11},{10,... | collective-permute-start | bytes 393224 | tf_op jit(solution)/shard_map/ppermute | solution.py:153
  39.8 4.1 %collective-permute-done.3.partner_ref = bf16[256,256]{1,0:T(8,128)(2,1)S(1)} collective-permute-done((bf16[256,256]{1,0:T(8,128)(2,1)S(1)}, bf16[256,256]{1,0:T(8,128)(2,1)S(1)}, u32[]{:S(2)}, u32[]{:S(2)}) %collective-permute-start.3) | collective-permute-done | bytes 131104 | tf_op jit(solution)/shard_map/ppermute | solution.py:153
  43.8 0.3 shard_map.95.own_ref
  44.1 1.6 %collective-permute-start.4 = (bf16[256,256]{1,0:T(8,128)(2,1)S(1)}, bf16[256,256]{1,0:T(8,128)(2,1)S(1)}, u32[]{:S(2)}, u32[]{:S(2)}) collective-permute-start(bf16[256,256]{1,0:T(8,128)(2,1)S(1)} %shard_map.95.own_ref), channel_id=1, source_target_pairs={{0,4},{1,5},{2,6},{3,7},{4,0},{5,1},{6,2},{7,3},{8,12},{9,13},{10,... | collective-permute-start | bytes 393224 | tf_op jit(solution)/shard_map/ppermute | solution.py:153
  45.7 0.0 all-to-all-done.packed_ref
  45.7 2.3 %shard_map.98 = bf16[32,48,128]{2,1,0:T(8,128)(2,1)} custom-call(bf16[32,56,128]{2,1,0:T(8,128)(2,1)S(1)} %all-to-all-done.packed_ref, bf16[2,512,512]{2,1,0:T(8,128)(2,1)S(1)} %copy-done.1, bf16[3,512,512]{2,1,0:T(8,128)(2,1)S(1)} %copy-done), custom_call_target="tpu_custom_call" | custom-call | tf_op jit(solution)/shard_map/pallas_call | solution.py:198
  47.9 4.2 %all-to-all-start.1 = ((bf16[32,48,128]{2,1,0:T(8,128)(2,1)}), bf16[32,48,128]{2,1,0:T(8,128)(2,1)S(1)}, u32[]{:S(2)}, u32[]{:S(2)}) async-start(bf16[32,48,128]{2,1,0:T(8,128)(2,1)} %shard_map.98), calls=%async_computation.1 | async-start | bytes 786432 | tf_op jit(solution)/shard_map/all_to_all | solution.py:323
  52.2 0.0 copy-done.6
  52.2 2.9 %multiply_convert_fusion.decoder_ref = bf16[4096,256]{1,0:T(8,128)(2,1)} fusion(bf16[4096,256]{1,0:T(8,128)(2,1)} %param.16, f32[256]{0:T(256)S(1)} %bitcast.13, f32[4096]{0:T(1024)S(1)} %copy-done.6), kind=kLoop, calls=%fused_computation | loop fusion | flops 4194304 | bytes 4211712 | tf_op jit(solution)/shard_map/convert_element_type | solution.py:327
  55.1 0.0 collective-permute-done.4.partner_ref
  55.1 0.2 shard_map.96.side_ref
  55.3 10.1 %all-to-all-done.1.packed_ref = bf16[32,48,128]{2,1,0:T(8,128)(2,1)S(1)} async-done(((bf16[32,48,128]{2,1,0:T(8,128)(2,1)}), bf16[32,48,128]{2,1,0:T(8,128)(2,1)S(1)}, u32[]{:S(2)}, u32[]{:S(2)}) %all-to-all-start.1) | async-done | bytes 393248 | tf_op jit(solution)/shard_map/all_to_all | solution.py:323
  65.4 0.0 copy-start.2
  65.4 1.6 %copy-done.2 = bf16[4096,256]{1,0:T(8,128)(2,1)S(1)} copy-done((bf16[4096,256]{1,0:T(8,128)(2,1)S(1)}, bf16[4096,256]{1,0:T(8,128)(2,1)}, u32[]{:S(2)}) %copy-start.2) | copy-done | bytes 2097176
  67.0 3.9 %shard_map.99 = bf16[4096,1024]{1,0:T(8,128)(2,1)} custom-call(bf16[256,256]{1,0:T(8,128)(2,1)S(1)} %shard_map.96.side_ref, bf16[32,48,128]{2,1,0:T(8,128)(2,1)S(1)} %all-to-all-done.1.packed_ref, bf16[4096,256]{1,0:T(8,128)(2,1)S(1)} %copy-done.2), custom_call_target="tpu_custom_call" | custom-call | tf_op jit(solution)/shard_map/pallas_call | solution.py:231
  (2 shorter events, 0.0 us)
Async XLA Ops:
  0.0 14.4 %copy-start.5 = (f32[4096]{0:T(1024)S(1)}, f32[4096]{0:T(1024)}, u32[]{:S(2)}) copy-start(f32[4096]{0:T(1024)} %param.10) | copy-start | bytes 49156
  7.2 38.5 %all-to-all-start = ((bf16[32,56,128]{2,1,0:T(8,128)(2,1)}), bf16[32,56,128]{2,1,0:T(8,128)(2,1)S(1)}, u32[]{:S(2)}, u32[]{:S(2)}) async-start(bf16[32,56,128]{2,1,0:T(8,128)(2,1)} %shard_map.97), calls=%async_computation | async-start | bytes 917504 | tf_op jit(solution)/shard_map/all_to_all | solution.py:318
  14.4 12.1 %copy-start.1 = (bf16[2,512,512]{2,1,0:T(8,128)(2,1)S(1)}, bf16[2,512,512]{2,1,0:T(8,128)(2,1)}, u32[]{:S(2)}) copy-start(bf16[2,512,512]{2,1,0:T(8,128)(2,1)} %comp_ref.1) | copy-start | bytes 3145732
  14.4 12.1 %copy-start.4 = (f32[2,1,4,256]{3,2,1,0:T(4,128)S(1)}, f32[2,1,4,256]{3,2,1,0:T(4,128)}, u32[]{:S(2)}) copy-start(f32[2,1,4,256]{3,2,1,0:T(4,128)} %param.13) | copy-start | bytes 24580
  14.4 23.5 %copy-start = (bf16[3,512,512]{2,1,0:T(8,128)(2,1)S(1)}, bf16[3,512,512]{2,1,0:T(8,128)(2,1)}, u32[]{:S(2)}) copy-start(bf16[3,512,512]{2,1,0:T(8,128)(2,1)} %exp_ref.1) | copy-start | bytes 4718596
  14.4 23.5 %copy-start.3 = (f32[3,1,8,256]{3,2,1,0:T(8,128)S(1)}, f32[3,1,8,256]{3,2,1,0:T(8,128)}, u32[]{:S(2)}) copy-start(f32[3,1,8,256]{3,2,1,0:T(8,128)} %param.15) | copy-start | bytes 73732
  17.4 9.1 %collective-permute-start = (bf16[256,256]{1,0:T(8,128)(2,1)S(1)}, bf16[256,256]{1,0:T(8,128)(2,1)S(1)}, u32[]{:S(2)}, u32[]{:S(2)}) collective-permute-start(bf16[256,256]{1,0:T(8,128)(2,1)S(1)} %shard_map.91.own_ref), channel_id=1, source_target_pairs={{0,8},{8,0},{16,24},{24,16},{1,9},{9,1},{17,25},{25,17},{2,10},{10... | collective-permute-start | bytes 393224 | tf_op jit(solution)/shard_map/ppermute | solution.py:153
  26.8 9.4 %collective-permute-start.1 = (bf16[256,256]{1,0:T(8,128)(2,1)S(1)}, bf16[256,256]{1,0:T(8,128)(2,1)S(1)}, u32[]{:S(2)}, u32[]{:S(2)}) collective-permute-start(bf16[256,256]{1,0:T(8,128)(2,1)S(1)} %shard_map.92.own_ref), channel_id=1, source_target_pairs={{0,16},{8,24},{16,0},{24,8},{1,17},{9,25},{17,1},{25,9},{2,18},{10... | collective-permute-start | bytes 393224 | tf_op jit(solution)/shard_map/ppermute | solution.py:153
  36.5 15.7 %copy-start.6 = (f32[4096]{0:T(1024)S(1)}, f32[4096]{0:T(1024)}, u32[]{:S(2)}) copy-start(f32[4096]{0:T(1024)} %param.17) | copy-start | bytes 49156
  36.5 1.4 %collective-permute-start.2 = (bf16[256,256]{1,0:T(8,128)(2,1)S(1)}, bf16[256,256]{1,0:T(8,128)(2,1)S(1)}, u32[]{:S(2)}, u32[]{:S(2)}) collective-permute-start(bf16[256,256]{1,0:T(8,128)(2,1)S(1)} %shard_map.93.own_ref), channel_id=1, source_target_pairs={{0,1},{1,0},{2,3},{3,2},{4,5},{5,4},{6,7},{7,6},{8,9},{9,8},{10,11... | collective-permute-start | bytes 393224 | tf_op jit(solution)/shard_map/ppermute | solution.py:153
  38.2 5.6 %collective-permute-start.3 = (bf16[256,256]{1,0:T(8,128)(2,1)S(1)}, bf16[256,256]{1,0:T(8,128)(2,1)S(1)}, u32[]{:S(2)}, u32[]{:S(2)}) collective-permute-start(bf16[256,256]{1,0:T(8,128)(2,1)S(1)} %shard_map.94.own_ref), channel_id=1, source_target_pairs={{0,2},{1,3},{2,0},{3,1},{4,6},{5,7},{6,4},{7,5},{8,10},{9,11},{10,... | collective-permute-start | bytes 393224 | tf_op jit(solution)/shard_map/ppermute | solution.py:153
  44.1 11.0 %collective-permute-start.4 = (bf16[256,256]{1,0:T(8,128)(2,1)S(1)}, bf16[256,256]{1,0:T(8,128)(2,1)S(1)}, u32[]{:S(2)}, u32[]{:S(2)}) collective-permute-start(bf16[256,256]{1,0:T(8,128)(2,1)S(1)} %shard_map.95.own_ref), channel_id=1, source_target_pairs={{0,4},{1,5},{2,6},{3,7},{4,0},{5,1},{6,2},{7,3},{8,12},{9,13},{10,... | collective-permute-start | bytes 393224 | tf_op jit(solution)/shard_map/ppermute | solution.py:153
  47.9 17.5 %all-to-all-start.1 = ((bf16[32,48,128]{2,1,0:T(8,128)(2,1)}), bf16[32,48,128]{2,1,0:T(8,128)(2,1)S(1)}, u32[]{:S(2)}, u32[]{:S(2)}) async-start(bf16[32,48,128]{2,1,0:T(8,128)(2,1)} %shard_map.98), calls=%async_computation.1 | async-start | bytes 786432 | tf_op jit(solution)/shard_map/all_to_all | solution.py:323
  65.4 1.6 %copy-start.2 = (bf16[4096,256]{1,0:T(8,128)(2,1)S(1)}, bf16[4096,256]{1,0:T(8,128)(2,1)}, u32[]{:S(2)}) copy-start(bf16[4096,256]{1,0:T(8,128)(2,1)} %multiply_convert_fusion.decoder_ref) | copy-start | bytes 6291460

commit v4 on v3

--- a/solution.py
+++ b/solution.py
@@ -27,25 +27,43 @@
     return lax.dot_general(a, b, dims, preferred_element_type=jnp.float32)
 
 
-def start_loads(blocks, first, sources_hbm, encoder_hbm, held, table, sems):
+def encode_kernel(
+    blocks,
+    sources_hbm,
+    scale_hbm,
+    encoder_hbm,
+    comp_hbm,
+    exp_hbm,
+    side_ref,
+    out_hbm,
+    held,
+    table,
+    acc_ref,
+    sems,
+    scale_ref,
+    comp_ref,
+    exp_ref,
+    out_ref,
+    small,
+):
+    pairs = ((scale_hbm, scale_ref), (comp_hbm, comp_ref), (exp_hbm, exp_ref))
+    first_copies = [pltpu.make_async_copy(*pair, small.at[number]) for number, pair in enumerate(pairs)]
+    for copy in first_copies:
+        copy.start()
     block = sources_hbm.shape[0] // blocks
     copies = []
     for number in range(blocks):
         span = pl.ds(number * block, block)
-        wanted = sources_hbm.at[span, pl.ds(first, held.shape[1])]
         copies.append(
             (
                 pltpu.make_async_copy(encoder_hbm.at[:, span], table.at[:, span], sems.at[0, number]),
-                pltpu.make_async_copy(wanted, held.at[span], sems.at[1, number]),
+                pltpu.make_async_copy(sources_hbm.at[span], held.at[span], sems.at[1, number]),
             )
         )
         for copy in copies[-1]:
             copy.start()
-    return copies
-
-
-def add_up(copies, scale_ref, held, table, acc_ref):
-    block = held.shape[0] // len(copies)
+    for copy in first_copies:
+        copy.wait()
     for number, pair in enumerate(copies):
         for copy in pair:
             copy.wait()
@@ -57,44 +75,36 @@
         else:
             acc_ref[...] += part
 
-
-def encode_kernel(
-    blocks, first, sources_hbm, scale_hbm, encoder_hbm, comp_hbm, exp_hbm, out_ref, held, table, acc_ref, sems, scale_ref, comp_ref, exp_ref, small
-):
-    pairs = ((scale_hbm, scale_ref), (comp_hbm, comp_ref), (exp_hbm, exp_ref))
-    first_copies = [pltpu.make_async_copy(*pair, small.at[number]) for number, pair in enumerate(pairs)]
-    for copy in first_copies:
-        copy.start()
-    copies = start_loads(blocks, first, sources_hbm, encoder_hbm, held, table, sems)
-    for copy in first_copies:
-        copy.wait()
-    parts, rows, _ = out_ref.shape
     own = [comp_ref[number, pl.ds(lax.axis_index("col"), 1), :] for number in range(comp_ref.shape[0])]
     own += [exp_ref[number, pl.ds(lax.axis_index("row"), 1), :] for number in range(exp_ref.shape[0] - 1)]
     gains = [half for gain in own for half in (gain[:, :LANES], gain[:, LANES:])]
     pad = -(-len(gains) // 8) * 8
     gains += [jnp.zeros((1, LANES), jnp.float32)] * (pad - len(gains))
-    gains = jnp.concatenate(gains, axis=0).astype(jnp.bfloat16)
-    width = (rows - pad) // 2
-    add_up(copies, scale_ref, held, table, acc_ref)
-    turned = acc_ref[...].T.reshape(parts, width, 2 * LANES)
-    out_ref[:, :width, :] = turned[:, :, :LANES].astype(jnp.bfloat16)
-    out_ref[:, width : 2 * width, :] = turned[:, :, LANES:].astype(jnp.bfloat16)
-    out_ref[:, 2 * width :, :] = jnp.broadcast_to(gains[None], (parts, pad, LANES))
-
-
-def encode(sources, enc_scale, encoder, comp_gain, exp_gain, parts, first):
+    gains = jnp.concatenate(gains, axis=0)
+    parts, rows, _ = out_ref.shape
+    width, side = (rows - pad) // 2, side_ref.shape[1]
+    side_ref[...] = acc_ref[:, :side].astype(jnp.bfloat16)
+    turned = acc_ref[:, side:].T.reshape(parts, width, 2 * LANES)
+    gains = jnp.broadcast_to(gains[None], (parts, pad, LANES))
+    joined = jnp.concatenate([turned[:, :, :LANES], turned[:, :, LANES:], gains], axis=1)
+    out_ref[...] = joined.astype(jnp.bfloat16)
+    copy = pltpu.make_async_copy(out_ref, out_hbm, small.at[len(pairs)])
+    copy.start()
+    copy.wait()
+
+
+def encode(sources, enc_scale, encoder, comp_gain, exp_gain, parts, side):
     points, width = sources.shape
-    width -= first
     skeleton = encoder.shape[0]
     pad = gain_rows(comp_gain, exp_gain)
+    packed = (parts, 2 * ((width - side) // parts) + pad, LANES)
     blocks = 8
     return pl.pallas_call(
-        functools.partial(encode_kernel, blocks, first),
+        functools.partial(encode_kernel, blocks),
         in_specs=[HBM] * 5,
-        compiler_params=pltpu.CompilerParams(vmem_limit_bytes=20 * 2**20),
-        out_specs=VMEM,
-        out_shape=jax.ShapeDtypeStruct((parts, 2 * (width // parts) + pad, LANES), jnp.bfloat16),
+        out_specs=[VMEM, HBM],
+        compiler_params=pltpu.CompilerParams(vmem_limit_bytes=24 * 2**20),
+        out_shape=[jax.ShapeDtypeStruct((skeleton, side), jnp.bfloat16), pltpu.HBM(packed, jnp.bfloat16)],
         scratch_shapes=[
             pltpu.VMEM((points, width), jnp.bfloat16),
             pltpu.VMEM((skeleton, points), jnp.bfloat16),
@@ -103,34 +113,10 @@
             pltpu.VMEM((1, points), jnp.float32),
             pltpu.VMEM(comp_gain.shape, jnp.float32),
             pltpu.VMEM(exp_gain.shape, jnp.float32),
-            pltpu.SemaphoreType.DMA((3,)),
+            pltpu.VMEM(packed, jnp.bfloat16),
+            pltpu.SemaphoreType.DMA((4,)),
         ],
     )(sources, in_hbm(enc_scale.reshape(1, points)), encoder, in_hbm(comp_gain), in_hbm(exp_gain))
-
-
-def side_encode_kernel(blocks, sources_hbm, scale_ref, encoder_hbm, out_ref, held, table, acc_ref, sems):
-    copies = start_loads(blocks, 0, sources_hbm, encoder_hbm, held, table, sems)
-    add_up(copies, scale_ref, held, table, acc_ref)
-    out_ref[...] = acc_ref[...].astype(jnp.bfloat16)
-
-
-def side_encode(sources, enc_scale, encoder, width):
-    points = sources.shape[0]
-    skeleton = encoder.shape[0]
-    blocks = 8
-    return pl.pallas_call(
-        functools.partial(side_encode_kernel, blocks),
-        in_specs=[HBM, VMEM, HBM],
-        compiler_params=pltpu.CompilerParams(vmem_limit_bytes=12 * 2**20),
-        out_specs=VMEM,
-        out_shape=jax.ShapeDtypeStruct((skeleton, width), jnp.bfloat16),
-        scratch_shapes=[
-            pltpu.VMEM((points, width), jnp.bfloat16),
-            pltpu.VMEM((skeleton, points), jnp.bfloat16),
-            pltpu.VMEM((skeleton, width), jnp.float32),
-            pltpu.SemaphoreType.DMA((2, blocks)),
-        ],
-    )(sources, enc_scale.reshape(1, points), encoder)
 
 
 def side_level_kernel(axis, bit, number, scaled, own_ref, partner_ref, transfer_ref, gain_ref, out_ref):
@@ -169,9 +155,9 @@
     boxes, rows, _ = packed_ref.shape
     width = (rows - pad) // 2
     skeleton = 2 * LANES
-    state = jnp.concatenate([packed_ref[:, :width, :], packed_ref[:, width : 2 * width, :]], axis=-1)
-    state = state.astype(jnp.float32)
-    gains = packed_ref[:, 2 * width :, :].astype(jnp.float32)
+    packed = packed_ref[...].astype(jnp.float32)
+    state = jnp.concatenate([packed[:, :width, :], packed[:, width : 2 * width, :]], axis=-1)
+    gains = packed[:, 2 * width :, :]
     for number, stride in enumerate(strides):
         turned = number >= comp_ref.shape[0]
         transfer = exp_ref[number - comp_ref.shape[0]] if turned else comp_ref[number]
@@ -189,8 +175,7 @@
                 axis=-1,
             )
             state = state * gain
-    out_ref[:, :width, :] = state[:, :, :LANES].astype(jnp.bfloat16)
-    out_ref[:, width:, :] = state[:, :, LANES:].astype(jnp.bfloat16)
+    out_ref[...] = jnp.concatenate([state[:, :, :LANES], state[:, :, LANES:]], axis=1).astype(jnp.bfloat16)
 
 
 def levels(packed, comp_transfer, exp_transfer, strides, pad):
@@ -204,20 +189,47 @@
     )(on_chip(packed), comp_transfer, exp_transfer)
 
 
-def decode_kernel(blocks, side_ref, packed_ref, decoder_ref, out_hbm, turned_ref, held, sems):
+def table_kernel(decoder_ref, scale_ref, gain_ref, out_ref):
+    gain = gain_ref[gain_ref.shape[0] - 1, pl.ds(lax.axis_index("row"), 1), :]
+    count = scale_ref.shape[0]
+    scales = scale_ref[...].T
+    for number in range(count):
+        rows = slice(number * LANES, (number + 1) * LANES)
+        factors = scales[:, number : number + 1] * gain
+        out_ref[rows, :] = (decoder_ref[rows, :].astype(jnp.float32) * factors).astype(jnp.bfloat16)
+
+
+def scaled_table(decoder, dec_scale, exp_gain):
+    return pl.pallas_call(
+        table_kernel,
+        in_specs=[VMEM] * 3,
+        out_specs=VMEM,
+        compiler_params=pltpu.CompilerParams(vmem_limit_bytes=8 * 2**20),
+        out_shape=jax.ShapeDtypeStruct(decoder.shape, jnp.bfloat16),
+    )(decoder, dec_scale.reshape(-1, LANES), exp_gain)
+
+
+def decode_kernel(blocks, side_ref, packed_ref, decoder_hbm, out_hbm, turned_ref, held, decoder_ref, sems):
+    block = decoder_ref.shape[0] // blocks
+    loads = []
+    for number in range(blocks):
+        span = pl.ds(number * block, block)
+        loads.append(pltpu.make_async_copy(decoder_hbm.at[span], decoder_ref.at[span], sems.at[0, number]))
+        loads[-1].start()
     boxes, rows, _ = packed_ref.shape
     width, side = rows // 2, side_ref.shape[1]
-    coeffs = jnp.concatenate([packed_ref[:, :width, :], packed_ref[:, width:, :]], axis=-1)
-    coeffs = coeffs.astype(jnp.float32).reshape(boxes * width, 2 * LANES)
+    packed = packed_ref[...].astype(jnp.float32)
+    coeffs = jnp.concatenate([packed[:, :width, :], packed[:, width:, :]], axis=-1)
+    coeffs = coeffs.reshape(boxes * width, 2 * LANES)
     turned_ref[:, :side] = side_ref[...]
     turned_ref[:, side:] = coeffs.T.astype(jnp.bfloat16)
-    block = decoder_ref.shape[0] // blocks
     copies = []
     for number in range(blocks):
+        loads[number].wait()
         span = pl.ds(number * block, block)
         rows_of = slice(number * block, (number + 1) * block)
         held[rows_of, :] = mm(decoder_ref[rows_of, :], turned_ref[...]).astype(jnp.bfloat16)
-        copies.append(pltpu.make_async_copy(held.at[span], out_hbm.at[span], sems.at[number]))
+        copies.append(pltpu.make_async_copy(held.at[span], out_hbm.at[span], sems.at[1, number]))
         copies[-1].start()
     for copy in copies:
         copy.wait()
@@ -230,16 +242,17 @@
     blocks = 8
     return pl.pallas_call(
         functools.partial(decode_kernel, blocks),
-        in_specs=[VMEM, VMEM, VMEM],
+        in_specs=[VMEM, VMEM, HBM],
         compiler_params=pltpu.CompilerParams(vmem_limit_bytes=20 * 2**20),
         out_specs=HBM,
         out_shape=jax.ShapeDtypeStruct((points, width), jnp.bfloat16),
         scratch_shapes=[
             pltpu.VMEM((skeleton, width), jnp.bfloat16),
             pltpu.VMEM((points, width), jnp.bfloat16),
-            pltpu.SemaphoreType.DMA((blocks,)),
+            pltpu.VMEM((points, skeleton), jnp.bfloat16),
+            pltpu.SemaphoreType.DMA((2, blocks)),
         ],
-    )(on_chip(side), on_chip(packed), decoder)
+    )(on_chip(side), on_chip(packed), in_hbm(decoder))
 
 
 def plain_encode(sources, enc_scale, encoder, comp_gain, exp_gain, parts):
@@ -314,18 +327,17 @@
 
     comp_transfer, exp_transfer = on_chip(comp_transfer), on_chip(exp_transfer)
     sources, encoder = in_hbm(sources), in_hbm(encoder)
-    packed = encode(sources, enc_scale, encoder, comp_gain, exp_gain, parts, side)
+    coeffs, packed = encode(sources, enc_scale, encoder, comp_gain, exp_gain, parts, side)
     packed = lax.all_to_all(packed, AXES, 0, 0, tiled=True)
-    coeffs = side_encode(sources, enc_scale, encoder, side)
     for number in range(comp_levels):
         coeffs = side_level(coeffs, "col", number, number, True, comp_transfer, comp_gain)
+    table = scaled_table(decoder, dec_scale, exp_gain)
     packed = levels(packed, comp_transfer, exp_transfer, strides, pad)
     packed = lax.all_to_all(packed, AXES, 0, 0, tiled=True)
     for number in range(exp_levels):
         scaled = number + 1 < exp_levels
         coeffs = side_level(coeffs, "row", number, number, scaled, exp_transfer, exp_gain)
-    scaled = on_chip((decoder.astype(jnp.float32) * factors).astype(jnp.bfloat16))
-    return decode(coeffs, packed, scaled)
+    return decode(coeffs, packed, table)
 
 
 def solution(mesh):

time: 71.2 us -> 74.3 us (1.044)
  blocking collectives: 0 us -> 21.8 us
  starting transfers between devices: 19.7 us -> 10.5 us
  waiting for transfers between devices: 28.8 us -> 22.6 us
  other arithmetic: 2.9 us -> 0 us
    all_to_all x0 -> x1, blocking collectives: none -> 21.8 us  [body(): packed = lax.all_to_all(packed, AXES, 0, 0, tiled=True)]
    all_to_all x2 -> x1, waiting for transfers between devices: 10.1 us -> 0.01 us  [body(): packed = lax.all_to_all(packed, AXES, 0, 0, tiled=True)]
    all_to_all x2 -> x1, starting transfers between devices: 11.4 us -> 2.75 us  [body(): packed = lax.all_to_all(packed, AXES, 0, 0, tiled=True)]
    ppermute x5, waiting for transfers between devices: 18.7 us -> 22.6 us  [side_level(): partner = lax.ppermute(own, axis, pairs)]
    convert_element_type x1 -> x0, other arithmetic: 2.9 us -> none  [body(): (decoder.astype(jnp.float32) * factors).astype(jnp.bfloat16)]
    pallas_call x2, Pallas kernels: 10.1 us -> 8.21 us  [the longest x1 7.44 us: encode(): pl.pallas_call(functools.partial(encode_kernel, blocks), in_specs=[HBM] *...]
    pallas_call x1, Pallas kernels: 3.88 us -> 5.67 us  [decode(): pl.pallas_call(functools.partial(decode_kernel, blocks), in_specs=[VMEM,...]
  transfers between devices with their start and end apart: 7 -> 6, of which waited for: 5 -> 5; matrix products, arithmetic and copies ran while one was open for 4% -> 0% of each run, Pallas kernels for 9% -> 3%
where the time goes in v4:
time: 74.3 us; the launch traced here: 73.9 us
  waiting for transfers between devices  22.6 us (30%)
  blocking collectives  21.8 us (29%)
  Pallas kernels  17.5 us (24%)
  starting transfers between devices  10.5 us (14%)
  local copies, waits for them, and re-layouts  1.36 us (2%)
    ppermute x5, waiting for transfers between devices, side_level(): partner = lax.ppermute(own, axis, pairs)  22.6 us
    all_to_all x1, blocking collectives, body(): packed = lax.all_to_all(packed, AXES, 0, 0, tiled=True)  21.8 us
    ppermute x5, starting transfers between devices, side_level(): partner = lax.ppermute(own, axis, pairs)  7.76 us
    pallas_call x1, Pallas kernels, encode(): pl.pallas_call(functools.partial(encode_kernel, blocks), in_specs=[HBM] *...  7.44 us
    pallas_call x1, Pallas kernels, decode(): pl.pallas_call(functools.partial(decode_kernel, blocks), in_specs=[VMEM,...  5.67 us
    all_to_all x1, starting transfers between devices, body(): packed = lax.all_to_all(packed, AXES, 0, 0, tiled=True)  2.75 us
    pallas_call x1, Pallas kernels, levels(): pl.pallas_call(functools.partial(levels_kernel, strides, pad), in_specs=[...  2.26 us
  transfers between devices with their start and end apart: 6, of which 5 were waited for; matrix products, arithmetic and copies ran while one was open for 0% of the time, Pallas kernels for 3%

profile of v4, /device:TPU:0, one launch (start us, length us, event | category | flops | bytes accessed | tf_op | source)
XLA Modules:
  0.0 73.9 jit_solution(11507984974981852337)
XLA Ops:
  0.0 0.0 copy-start
  0.0 0.0 copy-start.1
  0.0 7.4 %shard_map.91 = (bf16[256,256]{1,0:T(8,128)(2,1)S(1)}, bf16[32,56,128]{2,1,0:T(8,128)(2,1)}) custom-call(bf16[4096,1024]{1,0:T(8,128)(2,1)} %sources_hbm.1, f32[1,4096]{1,0:T(1,128)} %bitcast.13, bf16[256,4096]{1,0:T(8,128)(2,1)} %encoder_hbm.1, f32[2,4,256]{2,1,0:T(4,128)} %bitcast.9, f32[3,8,256]{2,1,0:T(8,128)} %bitcast.4), custom_call_target="tpu_custom_call" | custom-call | tf_op jit(solution)/shard_map/pallas_call | solution.py:102
  7.5 21.8 %all_to_all.10.packed_ref = bf16[32,56,128]{2,1,0:T(8,128)(2,1)S(1)} all-to-all(bf16[32,56,128]{2,1,0:T(8,128)(2,1)} %get-tuple-element.8), channel_id=1, replica_groups=mesh['col'=4,'row'=8] {'col','row'}, dimensions={0} | all-to-all | bytes 917504 | tf_op jit(solution)/shard_map/all_to_all | solution.py:331
  29.2 0.0 copy-done
  29.2 0.0 copy-done.1
  29.2 0.0 copy-start.5
  29.2 2.3 %shard_map.97 = bf16[32,48,128]{2,1,0:T(8,128)(2,1)} custom-call(bf16[32,56,128]{2,1,0:T(8,128)(2,1)S(1)} %all_to_all.10.packed_ref, bf16[2,512,512]{2,1,0:T(8,128)(2,1)S(1)} %copy-done.1, bf16[3,512,512]{2,1,0:T(8,128)(2,1)S(1)} %copy-done), custom_call_target="tpu_custom_call" | custom-call | tf_op jit(solution)/shard_map/pallas_call | solution.py:183
  31.5 0.0 copy-start.4
  31.5 2.8 %all-to-all-start.1 = ((bf16[32,48,128]{2,1,0:T(8,128)(2,1)}), bf16[32,48,128]{2,1,0:T(8,128)(2,1)S(1)}, u32[]{:S(2)}, u32[]{:S(2)}) async-start(bf16[32,48,128]{2,1,0:T(8,128)(2,1)} %shard_map.97), calls=%async_computation.1 | async-start | bytes 786432 | tf_op jit(solution)/shard_map/all_to_all | solution.py:336
  34.2 1.8 %collective-permute-start = (bf16[256,256]{1,0:T(8,128)(2,1)S(1)}, bf16[256,256]{1,0:T(8,128)(2,1)S(1)}, u32[]{:S(2)}, u32[]{:S(2)}) collective-permute-start(bf16[256,256]{1,0:T(8,128)(2,1)S(1)} %get-tuple-element.7.own_ref), channel_id=1, source_target_pairs={{0,8},{8,0},{16,24},{24,16},{1,9},{9,1},{17,25},{25,17},{2,10},{10... | collective-permute-start | bytes 393224 | tf_op jit(solution)/shard_map/ppermute | solution.py:139
  36.1 9.9 %collective-permute-done.partner_ref = bf16[256,256]{1,0:T(8,128)(2,1)S(1)} collective-permute-done((bf16[256,256]{1,0:T(8,128)(2,1)S(1)}, bf16[256,256]{1,0:T(8,128)(2,1)S(1)}, u32[]{:S(2)}, u32[]{:S(2)}) %collective-permute-start) | collective-permute-done | bytes 131104 | tf_op jit(solution)/shard_map/ppermute | solution.py:139
  45.9 0.0 copy-done.5
  45.9 0.3 shard_map.92.own_ref
  46.2 2.8 %collective-permute-start.1 = (bf16[256,256]{1,0:T(8,128)(2,1)S(1)}, bf16[256,256]{1,0:T(8,128)(2,1)S(1)}, u32[]{:S(2)}, u32[]{:S(2)}) collective-permute-start(bf16[256,256]{1,0:T(8,128)(2,1)S(1)} %shard_map.92.own_ref), channel_id=1, source_target_pairs={{0,16},{8,24},{16,0},{24,8},{1,17},{9,25},{17,1},{25,9},{2,18},{10... | collective-permute-start | bytes 393224 | tf_op jit(solution)/shard_map/ppermute | solution.py:139
  49.0 6.0 %collective-permute-done.1.partner_ref = bf16[256,256]{1,0:T(8,128)(2,1)S(1)} collective-permute-done((bf16[256,256]{1,0:T(8,128)(2,1)S(1)}, bf16[256,256]{1,0:T(8,128)(2,1)S(1)}, u32[]{:S(2)}, u32[]{:S(2)}) %collective-permute-start.1) | collective-permute-done | bytes 131104 | tf_op jit(solution)/shard_map/ppermute | solution.py:139
  55.0 0.3 shard_map.93.own_ref
  55.3 0.0 copy-start.3
  55.3 0.0 copy-start.6
  55.3 0.1 collective-permute-start.2
  55.4 1.3 %collective-permute-done.2.partner_ref = bf16[256,256]{1,0:T(8,128)(2,1)S(1)} collective-permute-done((bf16[256,256]{1,0:T(8,128)(2,1)S(1)}, bf16[256,256]{1,0:T(8,128)(2,1)S(1)}, u32[]{:S(2)}, u32[]{:S(2)}) %collective-permute-start.2) | collective-permute-done | bytes 131104 | tf_op jit(solution)/shard_map/ppermute | solution.py:139
  56.8 0.0 copy-done.4
  56.8 0.3 shard_map.94.own_ref
  57.1 1.5 %collective-permute-start.3 = (bf16[256,256]{1,0:T(8,128)(2,1)S(1)}, bf16[256,256]{1,0:T(8,128)(2,1)S(1)}, u32[]{:S(2)}, u32[]{:S(2)}) collective-permute-start(bf16[256,256]{1,0:T(8,128)(2,1)S(1)} %shard_map.94.own_ref), channel_id=1, source_target_pairs={{0,2},{1,3},{2,0},{3,1},{4,6},{5,7},{6,4},{7,5},{8,10},{9,11},{10,... | collective-permute-start | bytes 393224 | tf_op jit(solution)/shard_map/ppermute | solution.py:139
  58.6 4.1 %collective-permute-done.3.partner_ref = bf16[256,256]{1,0:T(8,128)(2,1)S(1)} collective-permute-done((bf16[256,256]{1,0:T(8,128)(2,1)S(1)}, bf16[256,256]{1,0:T(8,128)(2,1)S(1)}, u32[]{:S(2)}, u32[]{:S(2)}) %collective-permute-start.3) | collective-permute-done | bytes 131104 | tf_op jit(solution)/shard_map/ppermute | solution.py:139
  62.7 0.3 shard_map.95.own_ref
  63.0 1.5 %collective-permute-start.4 = (bf16[256,256]{1,0:T(8,128)(2,1)S(1)}, bf16[256,256]{1,0:T(8,128)(2,1)S(1)}, u32[]{:S(2)}, u32[]{:S(2)}) collective-permute-start(bf16[256,256]{1,0:T(8,128)(2,1)S(1)} %shard_map.95.own_ref), channel_id=1, source_target_pairs={{0,4},{1,5},{2,6},{3,7},{4,0},{5,1},{6,2},{7,3},{8,12},{9,13},{10,... | collective-permute-start | bytes 393224 | tf_op jit(solution)/shard_map/ppermute | solution.py:139
  64.5 0.0 copy-done.3
  64.5 0.0 copy-done.6
  64.5 0.8 %shard_map.98.decoder_hbm = bf16[4096,256]{1,0:T(8,128)(2,1)S(1)} custom-call(bf16[4096,256]{1,0:T(8,128)(2,1)S(1)} %copy-done.3, f32[32,128]{1,0:T(8,128)S(1)} %bitcast.12, f32[3,8,256]{2,1,0:T(8,128)S(1)} %bitcast.7), custom_call_target="tpu_custom_call" | custom-call | tf_op jit(solution)/shard_map/pallas_call | solution.py:203
  65.3 0.0 copy-start.2
  65.3 1.3 %copy-done.2 = bf16[4096,256]{1,0:T(8,128)(2,1)} copy-done((bf16[4096,256]{1,0:T(8,128)(2,1)}, bf16[4096,256]{1,0:T(8,128)(2,1)S(1)}, u32[]{:S(2)}) %copy-start.2) | copy-done | bytes 2097176
  66.6 1.4 %collective-permute-done.4.partner_ref = bf16[256,256]{1,0:T(8,128)(2,1)S(1)} collective-permute-done((bf16[256,256]{1,0:T(8,128)(2,1)S(1)}, bf16[256,256]{1,0:T(8,128)(2,1)S(1)}, u32[]{:S(2)}, u32[]{:S(2)}) %collective-permute-start.4) | collective-permute-done | bytes 131104 | tf_op jit(solution)/shard_map/ppermute | solution.py:139
  68.0 0.2 shard_map.96.side_ref
  68.2 0.0 all-to-all-done.1.packed_ref
  68.2 5.7 %shard_map.99 = bf16[4096,1024]{1,0:T(8,128)(2,1)} custom-call(bf16[256,256]{1,0:T(8,128)(2,1)S(1)} %shard_map.96.side_ref, bf16[32,48,128]{2,1,0:T(8,128)(2,1)S(1)} %all-to-all-done.1.packed_ref, bf16[4096,256]{1,0:T(8,128)(2,1)} %copy-done.2), custom_call_target="tpu_custom_call" | custom-call | tf_op jit(solution)/shard_map/pallas_call | solution.py:243
Async XLA Ops:
  0.0 29.2 %copy-start = (bf16[3,512,512]{2,1,0:T(8,128)(2,1)S(1)}, bf16[3,512,512]{2,1,0:T(8,128)(2,1)}, u32[]{:S(2)}) copy-start(bf16[3,512,512]{2,1,0:T(8,128)(2,1)} %exp_ref.1) | copy-start | bytes 4718596
  0.0 29.2 %copy-start.1 = (bf16[2,512,512]{2,1,0:T(8,128)(2,1)S(1)}, bf16[2,512,512]{2,1,0:T(8,128)(2,1)}, u32[]{:S(2)}) copy-start(bf16[2,512,512]{2,1,0:T(8,128)(2,1)} %comp_ref.1) | copy-start | bytes 3145732
  29.2 16.7 %copy-start.5 = (f32[2,1,4,256]{3,2,1,0:T(4,128)S(1)}, f32[2,1,4,256]{3,2,1,0:T(4,128)}, u32[]{:S(2)}) copy-start(f32[2,1,4,256]{3,2,1,0:T(4,128)} %param.13) | copy-start | bytes 24580
  31.5 25.3 %copy-start.4 = (f32[3,1,8,256]{3,2,1,0:T(8,128)S(1)}, f32[3,1,8,256]{3,2,1,0:T(8,128)}, u32[]{:S(2)}) copy-start(f32[3,1,8,256]{3,2,1,0:T(8,128)} %param.15) | copy-start | bytes 73732
  31.5 36.8 %all-to-all-start.1 = ((bf16[32,48,128]{2,1,0:T(8,128)(2,1)}), bf16[32,48,128]{2,1,0:T(8,128)(2,1)S(1)}, u32[]{:S(2)}, u32[]{:S(2)}) async-start(bf16[32,48,128]{2,1,0:T(8,128)(2,1)} %shard_map.97), calls=%async_computation.1 | async-start | bytes 786432 | tf_op jit(solution)/shard_map/all_to_all | solution.py:336
  34.2 11.7 %collective-permute-start = (bf16[256,256]{1,0:T(8,128)(2,1)S(1)}, bf16[256,256]{1,0:T(8,128)(2,1)S(1)}, u32[]{:S(2)}, u32[]{:S(2)}) collective-permute-start(bf16[256,256]{1,0:T(8,128)(2,1)S(1)} %get-tuple-element.7.own_ref), channel_id=1, source_target_pairs={{0,8},{8,0},{16,24},{24,16},{1,9},{9,1},{17,25},{25,17},{2,10},{10... | collective-permute-start | bytes 393224 | tf_op jit(solution)/shard_map/ppermute | solution.py:139
  46.2 8.8 %collective-permute-start.1 = (bf16[256,256]{1,0:T(8,128)(2,1)S(1)}, bf16[256,256]{1,0:T(8,128)(2,1)S(1)}, u32[]{:S(2)}, u32[]{:S(2)}) collective-permute-start(bf16[256,256]{1,0:T(8,128)(2,1)S(1)} %shard_map.92.own_ref), channel_id=1, source_target_pairs={{0,16},{8,24},{16,0},{24,8},{1,17},{9,25},{17,1},{25,9},{2,18},{10... | collective-permute-start | bytes 393224 | tf_op jit(solution)/shard_map/ppermute | solution.py:139
  55.3 9.2 %copy-start.3 = (bf16[4096,256]{1,0:T(8,128)(2,1)S(1)}, bf16[4096,256]{1,0:T(8,128)(2,1)}, u32[]{:S(2)}) copy-start(bf16[4096,256]{1,0:T(8,128)(2,1)} %decoder_ref.1) | copy-start | bytes 6291460
  55.3 9.2 %copy-start.6 = (f32[4096]{0:T(1024)S(1)}, f32[4096]{0:T(1024)}, u32[]{:S(2)}) copy-start(f32[4096]{0:T(1024)} %param.17) | copy-start | bytes 49156
  55.3 1.4 %collective-permute-start.2 = (bf16[256,256]{1,0:T(8,128)(2,1)S(1)}, bf16[256,256]{1,0:T(8,128)(2,1)S(1)}, u32[]{:S(2)}, u32[]{:S(2)}) collective-permute-start(bf16[256,256]{1,0:T(8,128)(2,1)S(1)} %shard_map.93.own_ref), channel_id=1, source_target_pairs={{0,1},{1,0},{2,3},{3,2},{4,5},{5,4},{6,7},{7,6},{8,9},{9,8},{10,11... | collective-permute-start | bytes 393224 | tf_op jit(solution)/shard_map/ppermute | solution.py:139
  57.1 5.6 %collective-permute-start.3 = (bf16[256,256]{1,0:T(8,128)(2,1)S(1)}, bf16[256,256]{1,0:T(8,128)(2,1)S(1)}, u32[]{:S(2)}, u32[]{:S(2)}) collective-permute-start(bf16[256,256]{1,0:T(8,128)(2,1)S(1)} %shard_map.94.own_ref), channel_id=1, source_target_pairs={{0,2},{1,3},{2,0},{3,1},{4,6},{5,7},{6,4},{7,5},{8,10},{9,11},{10,... | collective-permute-start | bytes 393224 | tf_op jit(solution)/shard_map/ppermute | solution.py:139
  63.0 5.0 %collective-permute-start.4 = (bf16[256,256]{1,0:T(8,128)(2,1)S(1)}, bf16[256,256]{1,0:T(8,128)(2,1)S(1)}, u32[]{:S(2)}, u32[]{:S(2)}) collective-permute-start(bf16[256,256]{1,0:T(8,128)(2,1)S(1)} %shard_map.95.own_ref), channel_id=1, source_target_pairs={{0,4},{1,5},{2,6},{3,7},{4,0},{5,1},{6,2},{7,3},{8,12},{9,13},{10,... | collective-permute-start | bytes 393224 | tf_op jit(solution)/shard_map/ppermute | solution.py:139
  65.3 1.3 %copy-start.2 = (bf16[4096,256]{1,0:T(8,128)(2,1)}, bf16[4096,256]{1,0:T(8,128)(2,1)S(1)}, u32[]{:S(2)}) copy-start(bf16[4096,256]{1,0:T(8,128)(2,1)S(1)} %shard_map.98.decoder_hbm) | copy-start | bytes 6291460

commit v5 on v3

--- a/solution.py
+++ b/solution.py
@@ -9,6 +9,7 @@
 
 
 AXES = ("col", "row")
+ORDER = ("row", "col")
 LANES = 128
 NT = (((1,), (1,)), ((), ()))
 HBM = pl.BlockSpec(memory_space=pltpu.HBM)
@@ -59,7 +60,23 @@
 
 
 def encode_kernel(
-    blocks, first, sources_hbm, scale_hbm, encoder_hbm, comp_hbm, exp_hbm, out_ref, held, table, acc_ref, sems, scale_ref, comp_ref, exp_ref, small
+    blocks,
+    first,
+    sources_hbm,
+    scale_hbm,
+    encoder_hbm,
+    comp_hbm,
+    exp_hbm,
+    out_hbm,
+    held,
+    table,
+    acc_ref,
+    sems,
+    scale_ref,
+    comp_ref,
+    exp_ref,
+    out_ref,
+    small,
 ):
     pairs = ((scale_hbm, scale_ref), (comp_hbm, comp_ref), (exp_hbm, exp_ref))
     first_copies = [pltpu.make_async_copy(*pair, small.at[number]) for number, pair in enumerate(pairs)]
@@ -68,19 +85,22 @@
     copies = start_loads(blocks, first, sources_hbm, encoder_hbm, held, table, sems)
     for copy in first_copies:
         copy.wait()
-    parts, rows, _ = out_ref.shape
+    add_up(copies, scale_ref, held, table, acc_ref)
     own = [comp_ref[number, pl.ds(lax.axis_index("col"), 1), :] for number in range(comp_ref.shape[0])]
     own += [exp_ref[number, pl.ds(lax.axis_index("row"), 1), :] for number in range(exp_ref.shape[0] - 1)]
     gains = [half for gain in own for half in (gain[:, :LANES], gain[:, LANES:])]
     pad = -(-len(gains) // 8) * 8
     gains += [jnp.zeros((1, LANES), jnp.float32)] * (pad - len(gains))
-    gains = jnp.concatenate(gains, axis=0).astype(jnp.bfloat16)
+    gains = jnp.concatenate(gains, axis=0)
+    parts, rows, _ = out_ref.shape
     width = (rows - pad) // 2
-    add_up(copies, scale_ref, held, table, acc_ref)
     turned = acc_ref[...].T.reshape(parts, width, 2 * LANES)
-    out_ref[:, :width, :] = turned[:, :, :LANES].astype(jnp.bfloat16)
-    out_ref[:, width : 2 * width, :] = turned[:, :, LANES:].astype(jnp.bfloat16)
-    out_ref[:, 2 * width :, :] = jnp.broadcast_to(gains[None], (parts, pad, LANES))
+    gains = jnp.broadcast_to(gains[None], (parts, pad, LANES))
+    joined = jnp.concatenate([turned[:, :, :LANES], turned[:, :, LANES:], gains], axis=1)
+    out_ref[...] = joined.astype(jnp.bfloat16)
+    copy = pltpu.make_async_copy(out_ref, out_hbm, small.at[len(pairs)])
+    copy.start()
+    copy.wait()
 
 
 def encode(sources, enc_scale, encoder, comp_gain, exp_gain, parts, first):
@@ -88,13 +108,14 @@
     width -= first
     skeleton = encoder.shape[0]
     pad = gain_rows(comp_gain, exp_gain)
+    packed = (parts, 2 * (width // parts) + pad, LANES)
     blocks = 8
     return pl.pallas_call(
         functools.partial(encode_kernel, blocks, first),
         in_specs=[HBM] * 5,
+        out_specs=HBM,
         compiler_params=pltpu.CompilerParams(vmem_limit_bytes=20 * 2**20),
-        out_specs=VMEM,
-        out_shape=jax.ShapeDtypeStruct((parts, 2 * (width // parts) + pad, LANES), jnp.bfloat16),
+        out_shape=pltpu.HBM(packed, jnp.bfloat16),
         scratch_shapes=[
             pltpu.VMEM((points, width), jnp.bfloat16),
             pltpu.VMEM((skeleton, points), jnp.bfloat16),
@@ -103,13 +124,17 @@
             pltpu.VMEM((1, points), jnp.float32),
             pltpu.VMEM(comp_gain.shape, jnp.float32),
             pltpu.VMEM(exp_gain.shape, jnp.float32),
-            pltpu.SemaphoreType.DMA((3,)),
+            pltpu.VMEM(packed, jnp.bfloat16),
+            pltpu.SemaphoreType.DMA((4,)),
         ],
     )(sources, in_hbm(enc_scale.reshape(1, points)), encoder, in_hbm(comp_gain), in_hbm(exp_gain))
 
 
-def side_encode_kernel(blocks, sources_hbm, scale_ref, encoder_hbm, out_ref, held, table, acc_ref, sems):
+def side_encode_kernel(blocks, sources_hbm, scale_hbm, encoder_hbm, out_ref, held, table, acc_ref, sems, scale_ref, small):
+    first_copy = pltpu.make_async_copy(scale_hbm, scale_ref, small)
+    first_copy.start()
     copies = start_loads(blocks, 0, sources_hbm, encoder_hbm, held, table, sems)
+    first_copy.wait()
     add_up(copies, scale_ref, held, table, acc_ref)
     out_ref[...] = acc_ref[...].astype(jnp.bfloat16)
 
@@ -117,47 +142,76 @@
 def side_encode(sources, enc_scale, encoder, width):
     points = sources.shape[0]
     skeleton = encoder.shape[0]
-    blocks = 8
+    blocks = 4
     return pl.pallas_call(
         functools.partial(side_encode_kernel, blocks),
-        in_specs=[HBM, VMEM, HBM],
+        in_specs=[HBM] * 3,
+        out_specs=VMEM,
         compiler_params=pltpu.CompilerParams(vmem_limit_bytes=12 * 2**20),
-        out_specs=VMEM,
         out_shape=jax.ShapeDtypeStruct((skeleton, width), jnp.bfloat16),
         scratch_shapes=[
             pltpu.VMEM((points, width), jnp.bfloat16),
             pltpu.VMEM((skeleton, points), jnp.bfloat16),
             pltpu.VMEM((skeleton, width), jnp.float32),
             pltpu.SemaphoreType.DMA((2, blocks)),
+            pltpu.VMEM((1, points), jnp.float32),
+            pltpu.SemaphoreType.DMA,
         ],
-    )(sources, enc_scale.reshape(1, points), encoder)
-
-
-def side_level_kernel(axis, bit, number, scaled, own_ref, partner_ref, transfer_ref, gain_ref, out_ref):
+    )(sources, in_hbm(enc_scale.reshape(1, points)), encoder)
+
+
+def pick_kernel(comp_hbm, exp_hbm, *refs):
+    *outs, sems = refs
+    copies = []
+    for number, out_ref in enumerate(outs):
+        level = number - comp_hbm.shape[0]
+        source, axis = (comp_hbm.at[number], "col") if level < 0 else (exp_hbm.at[level], "row")
+        bit = number if level < 0 else level
+        skeleton = out_ref.shape[0]
+        here = pl.multiple_of(lax.axis_index(axis) // 2**bit % 2 * skeleton, skeleton)
+        copies.append(pltpu.make_async_copy(source.at[pl.ds(here, skeleton)], out_ref, sems.at[number]))
+        copies[-1].start()
+    for copy in copies:
+        copy.wait()
+
+
+def pick(comp_transfer, exp_transfer):
+    count = comp_transfer.shape[0] + exp_transfer.shape[0]
+    skeleton = comp_transfer.shape[1] // 2
+    return pl.pallas_call(
+        pick_kernel,
+        in_specs=[HBM] * 2,
+        out_specs=[VMEM] * count,
+        compiler_params=pltpu.CompilerParams(vmem_limit_bytes=4 * 2**20),
+        out_shape=[jax.ShapeDtypeStruct((skeleton, 2 * skeleton), jnp.bfloat16)] * count,
+        scratch_shapes=[pltpu.SemaphoreType.DMA((count,))],
+    )(in_hbm(comp_transfer), in_hbm(exp_transfer))
+
+
+def side_level_kernel(axis, bit, scaled, own_ref, partner_ref, rows_ref, gain_ref, out_ref):
     skeleton = own_ref.shape[0]
     position = lax.axis_index(axis)
     upper = position // 2**bit % 2
     here = pl.multiple_of(upper * skeleton, skeleton)
     there = pl.multiple_of((1 - upper) * skeleton, skeleton)
-    rows = pl.ds(here, skeleton)
-    mixed = mm(transfer_ref[number, rows, pl.ds(here, skeleton)], own_ref[...])
-    mixed += mm(transfer_ref[number, rows, pl.ds(there, skeleton)], partner_ref[...])
+    mixed = mm(rows_ref[:, pl.ds(here, skeleton)], own_ref[...])
+    mixed += mm(rows_ref[:, pl.ds(there, skeleton)], partner_ref[...])
     if scaled:
-        gain = jnp.broadcast_to(gain_ref[number, pl.ds(position, 1), :], (8, skeleton)).T
+        gain = jnp.broadcast_to(gain_ref[bit, pl.ds(position, 1), :], (8, skeleton)).T
         mixed *= gain[:, :1]
     out_ref[...] = mixed.astype(jnp.bfloat16)
 
 
-def side_level(own, axis, bit, number, scaled, transfer, gain):
+def side_level(own, axis, bit, scaled, rows, gain):
     pairs = [(source, source ^ 2**bit) for source in range(lax.axis_size(axis))]
     partner = lax.ppermute(own, axis, pairs)
     return pl.pallas_call(
-        functools.partial(side_level_kernel, axis, bit, number, scaled),
+        functools.partial(side_level_kernel, axis, bit, scaled),
         in_specs=[VMEM] * 4,
-        compiler_params=pltpu.CompilerParams(vmem_limit_bytes=8 * 2**20),
+        compiler_params=pltpu.CompilerParams(vmem_limit_bytes=4 * 2**20),
         out_specs=VMEM,
         out_shape=jax.ShapeDtypeStruct(own.shape, jnp.bfloat16),
-    )(on_chip(own), on_chip(partner), transfer, gain)
+    )(on_chip(own), on_chip(partner), on_chip(rows), gain)
 
 
 def gain_rows(comp_gain, exp_gain):
@@ -165,15 +219,21 @@
     return -(-sent // 8) * 8
 
 
-def levels_kernel(strides, pad, packed_ref, comp_ref, exp_ref, out_ref):
+def levels_kernel(strides, pad, packed_ref, comp_ref, exp_hbm, out_ref, exp_ref, sems):
+    copies = []
+    for number in range(exp_hbm.shape[0]):
+        copies.append(pltpu.make_async_copy(exp_hbm.at[number], exp_ref.at[number], sems.at[number]))
+        copies[-1].start()
     boxes, rows, _ = packed_ref.shape
     width = (rows - pad) // 2
     skeleton = 2 * LANES
-    state = jnp.concatenate([packed_ref[:, :width, :], packed_ref[:, width : 2 * width, :]], axis=-1)
-    state = state.astype(jnp.float32)
-    gains = packed_ref[:, 2 * width :, :].astype(jnp.float32)
+    packed = packed_ref[...].astype(jnp.float32)
+    state = jnp.concatenate([packed[:, :width, :], packed[:, width : 2 * width, :]], axis=-1)
+    gains = packed[:, 2 * width :, :]
     for number, stride in enumerate(strides):
         turned = number >= comp_ref.shape[0]
+        if turned:
+            copies[number - comp_ref.shape[0]].wait()
         transfer = exp_ref[number - comp_ref.shape[0]] if turned else comp_ref[number]
         halves = state.reshape(boxes // (2 * stride), 2, stride * width, skeleton)
         low = halves[:, 0].reshape(boxes // 2 * width, skeleton).astype(jnp.bfloat16)
@@ -189,26 +249,30 @@
                 axis=-1,
             )
             state = state * gain
-    out_ref[:, :width, :] = state[:, :, :LANES].astype(jnp.bfloat16)
-    out_ref[:, width:, :] = state[:, :, LANES:].astype(jnp.bfloat16)
+    out_ref[...] = jnp.concatenate([state[:, :, :LANES], state[:, :, LANES:]], axis=1).astype(jnp.bfloat16)
 
 
 def levels(packed, comp_transfer, exp_transfer, strides, pad):
     boxes, rows, _ = packed.shape
     return pl.pallas_call(
         functools.partial(levels_kernel, strides, pad),
-        in_specs=[VMEM] * 3,
+        in_specs=[VMEM, VMEM, HBM],
         compiler_params=pltpu.CompilerParams(vmem_limit_bytes=20 * 2**20),
         out_specs=VMEM,
         out_shape=jax.ShapeDtypeStruct((boxes, rows - pad, LANES), jnp.bfloat16),
-    )(on_chip(packed), comp_transfer, exp_transfer)
+        scratch_shapes=[
+            pltpu.VMEM(exp_transfer.shape, jnp.bfloat16),
+            pltpu.SemaphoreType.DMA((exp_transfer.shape[0],)),
+        ],
+    )(on_chip(packed), on_chip(comp_transfer), in_hbm(exp_transfer))
 
 
 def decode_kernel(blocks, side_ref, packed_ref, decoder_ref, out_hbm, turned_ref, held, sems):
     boxes, rows, _ = packed_ref.shape
     width, side = rows // 2, side_ref.shape[1]
-    coeffs = jnp.concatenate([packed_ref[:, :width, :], packed_ref[:, width:, :]], axis=-1)
-    coeffs = coeffs.astype(jnp.float32).reshape(boxes * width, 2 * LANES)
+    packed = packed_ref[...].astype(jnp.float32)
+    coeffs = jnp.concatenate([packed[:, :width, :], packed[:, width:, :]], axis=-1)
+    coeffs = coeffs.reshape(boxes * width, 2 * LANES)
     turned_ref[:, :side] = side_ref[...]
     turned_ref[:, side:] = coeffs.T.astype(jnp.bfloat16)
     block = decoder_ref.shape[0] // blocks
@@ -295,9 +359,8 @@
     parts = col_count * row_count
     skeleton = encoder.shape[0]
     comp_levels, exp_levels = comp_transfer.shape[0], exp_transfer.shape[0]
-    strides = tuple(row_count * 2**number for number in range(comp_levels)) + tuple(
-        2**number for number in range(exp_levels)
-    )
+    strides = tuple(2**number for number in range(comp_levels))
+    strides += tuple(col_count * 2**number for number in range(exp_levels))
     comp_gain, exp_gain = comp_gain[:, 0], exp_gain[:, 0]
     pad = gain_rows(comp_gain, exp_gain)
     last_gain = lax.dynamic_index_in_dim(exp_gain[-1], lax.axis_index("row"), 0, keepdims=False)
@@ -307,25 +370,25 @@
 
     if side % LANES or (width - side) % (8 * parts) or skeleton != 2 * LANES:
         packed = plain_encode(sources, enc_scale, encoder, comp_gain, exp_gain, parts)
-        packed = lax.all_to_all(packed, AXES, 0, 0, tiled=True)
+        packed = lax.all_to_all(packed, ORDER, 0, 0, tiled=True)
         packed = plain_levels(packed, comp_transfer, exp_transfer, strides, pad)
-        packed = lax.all_to_all(packed, AXES, 0, 0, tiled=True)
+        packed = lax.all_to_all(packed, ORDER, 0, 0, tiled=True)
         return plain_decode(packed, (decoder.astype(jnp.float32) * factors).astype(jnp.bfloat16))
 
-    comp_transfer, exp_transfer = on_chip(comp_transfer), on_chip(exp_transfer)
     sources, encoder = in_hbm(sources), in_hbm(encoder)
     packed = encode(sources, enc_scale, encoder, comp_gain, exp_gain, parts, side)
-    packed = lax.all_to_all(packed, AXES, 0, 0, tiled=True)
+    packed = lax.all_to_all(packed, ORDER, 0, 0, tiled=True)
     coeffs = side_encode(sources, enc_scale, encoder, side)
+    rows = pick(comp_transfer, exp_transfer)
     for number in range(comp_levels):
-        coeffs = side_level(coeffs, "col", number, number, True, comp_transfer, comp_gain)
+        coeffs = side_level(coeffs, "col", number, True, rows[number], comp_gain)
     packed = levels(packed, comp_transfer, exp_transfer, strides, pad)
-    packed = lax.all_to_all(packed, AXES, 0, 0, tiled=True)
+    packed = lax.all_to_all(packed, ORDER, 0, 0, tiled=True)
     for number in range(exp_levels):
         scaled = number + 1 < exp_levels
-        coeffs = side_level(coeffs, "row", number, number, scaled, exp_transfer, exp_gain)
-    scaled = on_chip((decoder.astype(jnp.float32) * factors).astype(jnp.bfloat16))
-    return decode(coeffs, packed, scaled)
+        coeffs = side_level(coeffs, "row", number, scaled, rows[comp_levels + number], exp_gain)
+    table = on_chip((decoder.astype(jnp.float32) * factors).astype(jnp.bfloat16))
+    return decode(coeffs, packed, table)
 
 
 def solution(mesh):

time: 71.2 us -> 69.9 us (0.982); the launches traced: 70.9 us -> 68.9 us
  Pallas kernels: 17.7 us -> 20.5 us
  waiting for transfers between devices: 28.8 us -> 27.1 us
  local copies, waits for them, and re-layouts: 1.64 us -> 0.04 us
  other arithmetic: 2.9 us -> 1.94 us
    unnamed x14 -> x8, local copies, waits for them, and re-layouts: 1.63 us -> 0.03 us
    pallas_call x5 -> x6, Pallas kernels: 1.41 us -> 2.74 us  [the longest x5 1.41 us: side_level(): pl.pallas_call(functools.partial(side_level_kernel, axis, bit, scaled), i...]
    ppermute x5, waiting for transfers between devices: 18.7 us -> 17.4 us  [side_level(): partner = lax.ppermute(own, axis, pairs)]
    pallas_call x1, Pallas kernels: 2.25 us -> 3.44 us  [levels(): pl.pallas_call(functools.partial(levels_kernel, strides, pad), in_specs=[...]
    convert_element_type x1, other arithmetic: 2.9 us -> 1.94 us  [body(): (decoder.astype(jnp.float32) * factors).astype(jnp.bfloat16)]
  transfers between devices with their start and end apart: 7 -> 7, of which waited for: 5 -> 5; matrix products, arithmetic and copies ran while one was open for 4% -> 3% of each run, Pallas kernels for 9% -> 14%
where the time goes in v5:
time: 69.9 us; the launch traced here: 68.9 us
  waiting for transfers between devices  27.1 us (39%)
  Pallas kernels  20.5 us (29%)
  starting transfers between devices  19.1 us (27%)
  other arithmetic  1.94 us (3%)
    ppermute x5, waiting for transfers between devices, side_level(): partner = lax.ppermute(own, axis, pairs)  17.4 us
    all_to_all x2, starting transfers between devices, body(): packed = lax.all_to_all(packed, ORDER, 0, 0, tiled=True)  11.3 us
    all_to_all x2, waiting for transfers between devices, body(): packed = lax.all_to_all(packed, ORDER, 0, 0, tiled=True)  9.64 us
    ppermute x5, starting transfers between devices, side_level(): partner = lax.ppermute(own, axis, pairs)  7.81 us
    pallas_call x1, Pallas kernels, encode(): pl.pallas_call(functools.partial(encode_kernel, blocks, first), in_specs=...  7.02 us
    pallas_call x1, Pallas kernels, decode(): pl.pallas_call(functools.partial(decode_kernel, blocks), in_specs=[VMEM,...  3.88 us
    pallas_call x1, Pallas kernels, levels(): pl.pallas_call(functools.partial(levels_kernel, strides, pad), in_specs=[...  3.44 us
    pallas_call x1, Pallas kernels, side_encode(): pl.pallas_call(functools.partial(side_encode_kernel, blocks), in_specs=[H...  3.44 us
  transfers between devices with their start and end apart: 7, of which 5 were waited for; matrix products, arithmetic and copies ran while one was open for 3% of the time, Pallas kernels for 14%

profile of v5, /device:TPU:0, one launch (start us, length us, event | category | flops | bytes accessed | tf_op | source)
XLA Modules:
  0.0 68.9 jit_solution(16426205074679092134)
XLA Ops:
  0.0 7.0 %shard_map.98 = bf16[32,56,128]{2,1,0:T(8,128)(2,1)} custom-call(bf16[4096,1024]{1,0:T(8,128)(2,1)} %sources_hbm.3, f32[1,4096]{1,0:T(1,128)} %bitcast.11, bf16[256,4096]{1,0:T(8,128)(2,1)} %encoder_hbm.3, f32[2,4,256]{2,1,0:T(4,128)} %bitcast.8, f32[3,8,256]{2,1,0:T(8,128)} %bitcast.4), custom_call_target="tpu_custom_call" | custom-call | tf_op jit(solution)/shard_map/pallas_call | solution.py:113
  7.0 7.3 %all-to-all-start = ((bf16[32,56,128]{2,1,0:T(8,128)(2,1)}), bf16[32,56,128]{2,1,0:T(8,128)(2,1)S(1)}, u32[]{:S(2)}, u32[]{:S(2)}) async-start(bf16[32,56,128]{2,1,0:T(8,128)(2,1)} %shard_map.98), calls=%async_computation | async-start | bytes 917504 | tf_op jit(solution)/shard_map/all_to_all | solution.py:380
  14.4 0.0 copy-start.2
  14.4 0.0 copy-start.1
  14.4 3.4 %shard_map.91.own_ref = bf16[256,256]{1,0:T(8,128)(2,1)S(1)} custom-call(bf16[4096,1024]{1,0:T(8,128)(2,1)} %sources_hbm.3, f32[1,4096]{1,0:T(1,128)} %bitcast.12, bf16[256,4096]{1,0:T(8,128)(2,1)} %encoder_hbm.3), custom_call_target="tpu_custom_call" | custom-call | tf_op jit(solution)/shard_map/pallas_call | solution.py:146
  17.8 0.0 copy-start
  17.8 0.0 copy-start.3
  17.9 1.8 %collective-permute-start = (bf16[256,256]{1,0:T(8,128)(2,1)S(1)}, bf16[256,256]{1,0:T(8,128)(2,1)S(1)}, u32[]{:S(2)}, u32[]{:S(2)}) collective-permute-start(bf16[256,256]{1,0:T(8,128)(2,1)S(1)} %shard_map.91.own_ref), channel_id=1, source_target_pairs={{0,8},{8,0},{16,24},{24,16},{1,9},{9,1},{17,25},{25,17},{2,10},{10... | collective-permute-start | bytes 393224 | tf_op jit(solution)/shard_map/ppermute | solution.py:207
  19.7 1.3 %shard_map.92 = (bf16[256,512]{1,0:T(8,128)(2,1)S(1)}, bf16[256,512]{1,0:T(8,128)(2,1)S(1)}, bf16[256,512]{1,0:T(8,128)(2,1)S(1)}, bf16[256,512]{1,0:T(8,128)(2,1)S(1)}, bf16[256,512]{1,0:T(8,128)(2,1)S(1)}) custom-call(bf16[2,512,512]{2,1,0:T(8,128)(2,1)} %comp_ref.1, bf16[3,512,512]{2,1,0:T(8,128)(2,1)} %exp_hbm.3), custom_call_target="tpu_custom_call" | custom-call | tf_op jit(solution)/shard_map/pallas_call | solution.py:181
  21.0 6.0 %collective-permute-done.partner_ref = bf16[256,256]{1,0:T(8,128)(2,1)S(1)} collective-permute-done((bf16[256,256]{1,0:T(8,128)(2,1)S(1)}, bf16[256,256]{1,0:T(8,128)(2,1)S(1)}, u32[]{:S(2)}, u32[]{:S(2)}) %collective-permute-start) | collective-permute-done | bytes 131104 | tf_op jit(solution)/shard_map/ppermute | solution.py:207
  27.1 0.0 copy-done.2
  27.1 0.3 shard_map.93.own_ref
  27.4 2.8 %collective-permute-start.1 = (bf16[256,256]{1,0:T(8,128)(2,1)S(1)}, bf16[256,256]{1,0:T(8,128)(2,1)S(1)}, u32[]{:S(2)}, u32[]{:S(2)}) collective-permute-start(bf16[256,256]{1,0:T(8,128)(2,1)S(1)} %shard_map.93.own_ref), channel_id=1, source_target_pairs={{0,16},{8,24},{16,0},{24,8},{1,17},{9,25},{17,1},{25,9},{2,18},{10... | collective-permute-start | bytes 393224 | tf_op jit(solution)/shard_map/ppermute | solution.py:207
  30.2 6.0 %collective-permute-done.1.partner_ref = bf16[256,256]{1,0:T(8,128)(2,1)S(1)} collective-permute-done((bf16[256,256]{1,0:T(8,128)(2,1)S(1)}, bf16[256,256]{1,0:T(8,128)(2,1)S(1)}, u32[]{:S(2)}, u32[]{:S(2)}) %collective-permute-start.1) | collective-permute-done | bytes 131104 | tf_op jit(solution)/shard_map/ppermute | solution.py:207
  36.2 0.3 shard_map.94.own_ref
  36.5 0.1 collective-permute-start.2
  36.6 1.3 %collective-permute-done.2.partner_ref = bf16[256,256]{1,0:T(8,128)(2,1)S(1)} collective-permute-done((bf16[256,256]{1,0:T(8,128)(2,1)S(1)}, bf16[256,256]{1,0:T(8,128)(2,1)S(1)}, u32[]{:S(2)}, u32[]{:S(2)}) %collective-permute-start.2) | collective-permute-done | bytes 131104 | tf_op jit(solution)/shard_map/ppermute | solution.py:207
  37.9 0.0 copy-done.1
  37.9 0.3 shard_map.95.own_ref
  38.2 1.5 %collective-permute-start.3 = (bf16[256,256]{1,0:T(8,128)(2,1)S(1)}, bf16[256,256]{1,0:T(8,128)(2,1)S(1)}, u32[]{:S(2)}, u32[]{:S(2)}) collective-permute-start(bf16[256,256]{1,0:T(8,128)(2,1)S(1)} %shard_map.95.own_ref), channel_id=1, source_target_pairs={{0,2},{1,3},{2,0},{3,1},{4,6},{5,7},{6,4},{7,5},{8,10},{9,11},{10,... | collective-permute-start | bytes 393224 | tf_op jit(solution)/shard_map/ppermute | solution.py:207
  39.8 4.1 %collective-permute-done.3.partner_ref = bf16[256,256]{1,0:T(8,128)(2,1)S(1)} collective-permute-done((bf16[256,256]{1,0:T(8,128)(2,1)S(1)}, bf16[256,256]{1,0:T(8,128)(2,1)S(1)}, u32[]{:S(2)}, u32[]{:S(2)}) %collective-permute-start.3) | collective-permute-done | bytes 131104 | tf_op jit(solution)/shard_map/ppermute | solution.py:207
  43.8 0.3 shard_map.96.own_ref
  44.1 1.6 %collective-permute-start.4 = (bf16[256,256]{1,0:T(8,128)(2,1)S(1)}, bf16[256,256]{1,0:T(8,128)(2,1)S(1)}, u32[]{:S(2)}, u32[]{:S(2)}) collective-permute-start(bf16[256,256]{1,0:T(8,128)(2,1)S(1)} %shard_map.96.own_ref), channel_id=1, source_target_pairs={{0,4},{1,5},{2,6},{3,7},{4,0},{5,1},{6,2},{7,3},{8,12},{9,13},{10,... | collective-permute-start | bytes 393224 | tf_op jit(solution)/shard_map/ppermute | solution.py:207
  45.7 0.0 all-to-all-done.packed_ref
  45.7 0.0 copy-done
  45.7 3.4 %shard_map.99 = bf16[32,48,128]{2,1,0:T(8,128)(2,1)} custom-call(bf16[32,56,128]{2,1,0:T(8,128)(2,1)S(1)} %all-to-all-done.packed_ref, bf16[2,512,512]{2,1,0:T(8,128)(2,1)S(1)} %copy-done, bf16[3,512,512]{2,1,0:T(8,128)(2,1)} %exp_hbm.3), custom_call_target="tpu_custom_call" | custom-call | tf_op jit(solution)/shard_map/pallas_call | solution.py:257
  49.1 4.0 %all-to-all-start.1 = ((bf16[32,48,128]{2,1,0:T(8,128)(2,1)}), bf16[32,48,128]{2,1,0:T(8,128)(2,1)S(1)}, u32[]{:S(2)}, u32[]{:S(2)}) async-start(bf16[32,48,128]{2,1,0:T(8,128)(2,1)} %shard_map.99), calls=%async_computation.1 | async-start | bytes 786432 | tf_op jit(solution)/shard_map/all_to_all | solution.py:386
  53.1 0.0 copy-done.3
  53.1 1.9 %multiply_convert_fusion.decoder_ref = bf16[4096,256]{1,0:T(8,128)(2,1)S(1)} fusion(bf16[4096,256]{1,0:T(8,128)(2,1)} %param.16, f32[256]{0:T(256)S(1)} %bitcast.13, f32[4096]{0:T(1024)S(1)} %copy-done.3), kind=kLoop, calls=%fused_computation | loop fusion | flops 4194304 | bytes 4211712 | tf_op jit(solution)/shard_map/convert_element_type | solution.py:390
  55.1 0.0 collective-permute-done.4.partner_ref
  55.1 0.2 shard_map.97.side_ref
  55.3 9.6 %all-to-all-done.1.packed_ref = bf16[32,48,128]{2,1,0:T(8,128)(2,1)S(1)} async-done(((bf16[32,48,128]{2,1,0:T(8,128)(2,1)}), bf16[32,48,128]{2,1,0:T(8,128)(2,1)S(1)}, u32[]{:S(2)}, u32[]{:S(2)}) %all-to-all-start.1) | async-done | bytes 393248 | tf_op jit(solution)/shard_map/all_to_all | solution.py:386
  65.0 3.9 %shard_map.100 = bf16[4096,1024]{1,0:T(8,128)(2,1)} custom-call(bf16[256,256]{1,0:T(8,128)(2,1)S(1)} %shard_map.97.side_ref, bf16[32,48,128]{2,1,0:T(8,128)(2,1)S(1)} %all-to-all-done.1.packed_ref, bf16[4096,256]{1,0:T(8,128)(2,1)S(1)} %multiply_convert_fusion.decoder_ref), custom_call_target="tpu_custom_call" | custom-call | tf_op jit(solution)/shard_map/pallas_call | solution.py:295
  (2 shorter events, 0.0 us)
Async XLA Ops:
  7.0 38.6 %all-to-all-start = ((bf16[32,56,128]{2,1,0:T(8,128)(2,1)}), bf16[32,56,128]{2,1,0:T(8,128)(2,1)S(1)}, u32[]{:S(2)}, u32[]{:S(2)}) async-start(bf16[32,56,128]{2,1,0:T(8,128)(2,1)} %shard_map.98), calls=%async_computation | async-start | bytes 917504 | tf_op jit(solution)/shard_map/all_to_all | solution.py:380
  14.4 12.7 %copy-start.2 = (f32[2,1,4,256]{3,2,1,0:T(4,128)S(1)}, f32[2,1,4,256]{3,2,1,0:T(4,128)}, u32[]{:S(2)}) copy-start(f32[2,1,4,256]{3,2,1,0:T(4,128)} %param.13) | copy-start | bytes 24580
  14.4 23.5 %copy-start.1 = (f32[3,1,8,256]{3,2,1,0:T(8,128)S(1)}, f32[3,1,8,256]{3,2,1,0:T(8,128)}, u32[]{:S(2)}) copy-start(f32[3,1,8,256]{3,2,1,0:T(8,128)} %param.15) | copy-start | bytes 73732
  17.8 27.8 %copy-start = (bf16[2,512,512]{2,1,0:T(8,128)(2,1)S(1)}, bf16[2,512,512]{2,1,0:T(8,128)(2,1)}, u32[]{:S(2)}) copy-start(bf16[2,512,512]{2,1,0:T(8,128)(2,1)} %comp_ref.1) | copy-start | bytes 3145732
  17.8 35.3 %copy-start.3 = (f32[4096]{0:T(1024)S(1)}, f32[4096]{0:T(1024)}, u32[]{:S(2)}) copy-start(f32[4096]{0:T(1024)} %param.17) | copy-start | bytes 49156
  17.9 9.2 %collective-permute-start = (bf16[256,256]{1,0:T(8,128)(2,1)S(1)}, bf16[256,256]{1,0:T(8,128)(2,1)S(1)}, u32[]{:S(2)}, u32[]{:S(2)}) collective-permute-start(bf16[256,256]{1,0:T(8,128)(2,1)S(1)} %shard_map.91.own_ref), channel_id=1, source_target_pairs={{0,8},{8,0},{16,24},{24,16},{1,9},{9,1},{17,25},{25,17},{2,10},{10... | collective-permute-start | bytes 393224 | tf_op jit(solution)/shard_map/ppermute | solution.py:207
  27.4 8.8 %collective-permute-start.1 = (bf16[256,256]{1,0:T(8,128)(2,1)S(1)}, bf16[256,256]{1,0:T(8,128)(2,1)S(1)}, u32[]{:S(2)}, u32[]{:S(2)}) collective-permute-start(bf16[256,256]{1,0:T(8,128)(2,1)S(1)} %shard_map.93.own_ref), channel_id=1, source_target_pairs={{0,16},{8,24},{16,0},{24,8},{1,17},{9,25},{17,1},{25,9},{2,18},{10... | collective-permute-start | bytes 393224 | tf_op jit(solution)/shard_map/ppermute | solution.py:207
  36.5 1.4 %collective-permute-start.2 = (bf16[256,256]{1,0:T(8,128)(2,1)S(1)}, bf16[256,256]{1,0:T(8,128)(2,1)S(1)}, u32[]{:S(2)}, u32[]{:S(2)}) collective-permute-start(bf16[256,256]{1,0:T(8,128)(2,1)S(1)} %shard_map.94.own_ref), channel_id=1, source_target_pairs={{0,1},{1,0},{2,3},{3,2},{4,5},{5,4},{6,7},{7,6},{8,9},{9,8},{10,11... | collective-permute-start | bytes 393224 | tf_op jit(solution)/shard_map/ppermute | solution.py:207
  38.2 5.6 %collective-permute-start.3 = (bf16[256,256]{1,0:T(8,128)(2,1)S(1)}, bf16[256,256]{1,0:T(8,128)(2,1)S(1)}, u32[]{:S(2)}, u32[]{:S(2)}) collective-permute-start(bf16[256,256]{1,0:T(8,128)(2,1)S(1)} %shard_map.95.own_ref), channel_id=1, source_target_pairs={{0,2},{1,3},{2,0},{3,1},{4,6},{5,7},{6,4},{7,5},{8,10},{9,11},{10,... | collective-permute-start | bytes 393224 | tf_op jit(solution)/shard_map/ppermute | solution.py:207
  44.1 11.0 %collective-permute-start.4 = (bf16[256,256]{1,0:T(8,128)(2,1)S(1)}, bf16[256,256]{1,0:T(8,128)(2,1)S(1)}, u32[]{:S(2)}, u32[]{:S(2)}) collective-permute-start(bf16[256,256]{1,0:T(8,128)(2,1)S(1)} %shard_map.96.own_ref), channel_id=1, source_target_pairs={{0,4},{1,5},{2,6},{3,7},{4,0},{5,1},{6,2},{7,3},{8,12},{9,13},{10,... | collective-permute-start | bytes 393224 | tf_op jit(solution)/shard_map/ppermute | solution.py:207
  49.1 15.9 %all-to-all-start.1 = ((bf16[32,48,128]{2,1,0:T(8,128)(2,1)}), bf16[32,48,128]{2,1,0:T(8,128)(2,1)S(1)}, u32[]{:S(2)}, u32[]{:S(2)}) async-start(bf16[32,48,128]{2,1,0:T(8,128)(2,1)} %shard_map.99), calls=%async_computation.1 | async-start | bytes 786432 | tf_op jit(solution)/shard_map/all_to_all | solution.py:386

commit v6 on v5

--- a/solution.py
+++ b/solution.py
@@ -28,35 +28,19 @@
     return lax.dot_general(a, b, dims, preferred_element_type=jnp.float32)
 
 
-def start_loads(blocks, first, sources_hbm, encoder_hbm, held, table, sems):
-    block = sources_hbm.shape[0] // blocks
-    copies = []
-    for number in range(blocks):
-        span = pl.ds(number * block, block)
-        wanted = sources_hbm.at[span, pl.ds(first, held.shape[1])]
-        copies.append(
-            (
-                pltpu.make_async_copy(encoder_hbm.at[:, span], table.at[:, span], sems.at[0, number]),
-                pltpu.make_async_copy(wanted, held.at[span], sems.at[1, number]),
-            )
-        )
-        for copy in copies[-1]:
+def add_up(window, loads, multiply, acc_ref):
+    for copies in loads[:window]:
+        for copy in copies:
             copy.start()
-    return copies
-
-
-def add_up(copies, scale_ref, held, table, acc_ref):
-    block = held.shape[0] // len(copies)
-    for number, pair in enumerate(copies):
-        for copy in pair:
+    for number, copies in enumerate(loads):
+        for copy in copies:
             copy.wait()
-        span = slice(number * block, (number + 1) * block)
-        scaled = (table[:, span].astype(jnp.float32) * scale_ref[:, span]).astype(jnp.bfloat16)
-        part = mm(scaled, held[span, :])
+        for copy in loads[number + window] if number + window < len(loads) else ():
+            copy.start()
         if number == 0:
-            acc_ref[...] = part
+            acc_ref[...] = multiply(number)
         else:
-            acc_ref[...] += part
+            acc_ref[...] += multiply(number)
 
 
 def encode_kernel(
@@ -82,10 +66,27 @@
     first_copies = [pltpu.make_async_copy(*pair, small.at[number]) for number, pair in enumerate(pairs)]
     for copy in first_copies:
         copy.start()
-    copies = start_loads(blocks, first, sources_hbm, encoder_hbm, held, table, sems)
-    for copy in first_copies:
-        copy.wait()
-    add_up(copies, scale_ref, held, table, acc_ref)
+    block = held.shape[0] // blocks
+    loads = []
+    for number in range(blocks):
+        span = pl.ds(number * block, block)
+        wanted = sources_hbm.at[span, pl.ds(first, held.shape[1])]
+        loads.append(
+            (
+                pltpu.make_async_copy(encoder_hbm.at[:, span], table.at[:, span], sems.at[0, number]),
+                pltpu.make_async_copy(wanted, held.at[span], sems.at[1, number]),
+            )
+        )
+
+    def multiply(number):
+        if number == 0:
+            for copy in first_copies:
+                copy.wait()
+        span = slice(number * block, (number + 1) * block)
+        scaled = (table[:, span].astype(jnp.float32) * scale_ref[:, span]).astype(jnp.bfloat16)
+        return mm(scaled, held[span, :])
+
+    add_up(4, loads, multiply, acc_ref)
     own = [comp_ref[number, pl.ds(lax.axis_index("col"), 1), :] for number in range(comp_ref.shape[0])]
     own += [exp_ref[number, pl.ds(lax.axis_index("row"), 1), :] for number in range(exp_ref.shape[0] - 1)]
     gains = [half for gain in own for half in (gain[:, :LANES], gain[:, LANES:])]
@@ -133,9 +134,26 @@
 def side_encode_kernel(blocks, sources_hbm, scale_hbm, encoder_hbm, out_ref, held, table, acc_ref, sems, scale_ref, small):
     first_copy = pltpu.make_async_copy(scale_hbm, scale_ref, small)
     first_copy.start()
-    copies = start_loads(blocks, 0, sources_hbm, encoder_hbm, held, table, sems)
-    first_copy.wait()
-    add_up(copies, scale_ref, held, table, acc_ref)
+    block = held.shape[0] // blocks
+    loads = []
+    for number in range(blocks):
+        span = pl.ds(number * block, block)
+        wanted = sources_hbm.at[span, pl.ds(0, held.shape[1])]
+        loads.append(
+            (
+                pltpu.make_async_copy(encoder_hbm.at[:, span], table.at[:, span], sems.at[0, number]),
+                pltpu.make_async_copy(wanted, held.at[span], sems.at[1, number]),
+            )
+        )
+
+    def multiply(number):
+        if number == 0:
+            first_copy.wait()
+        span = slice(number * block, (number + 1) * block)
+        scaled = (table[:, span].astype(jnp.float32) * scale_ref[:, span]).astype(jnp.bfloat16)
+        return mm(scaled, held[span, :])
+
+    add_up(3, loads, multiply, acc_ref)
     out_ref[...] = acc_ref[...].astype(jnp.bfloat16)
 
 
@@ -160,32 +178,29 @@
     )(sources, in_hbm(enc_scale.reshape(1, points)), encoder)
 
 
-def pick_kernel(comp_hbm, exp_hbm, *refs):
+def pick_kernel(exp_hbm, *refs):
     *outs, sems = refs
     copies = []
     for number, out_ref in enumerate(outs):
-        level = number - comp_hbm.shape[0]
-        source, axis = (comp_hbm.at[number], "col") if level < 0 else (exp_hbm.at[level], "row")
-        bit = number if level < 0 else level
         skeleton = out_ref.shape[0]
-        here = pl.multiple_of(lax.axis_index(axis) // 2**bit % 2 * skeleton, skeleton)
-        copies.append(pltpu.make_async_copy(source.at[pl.ds(here, skeleton)], out_ref, sems.at[number]))
+        here = pl.multiple_of(lax.axis_index("row") // 2**number % 2 * skeleton, skeleton)
+        copies.append(pltpu.make_async_copy(exp_hbm.at[number, pl.ds(here, skeleton)], out_ref, sems.at[number]))
         copies[-1].start()
     for copy in copies:
         copy.wait()
 
 
-def pick(comp_transfer, exp_transfer):
-    count = comp_transfer.shape[0] + exp_transfer.shape[0]
-    skeleton = comp_transfer.shape[1] // 2
+def pick(exp_transfer):
+    count = exp_transfer.shape[0]
+    skeleton = exp_transfer.shape[1] // 2
     return pl.pallas_call(
         pick_kernel,
-        in_specs=[HBM] * 2,
+        in_specs=[HBM],
         out_specs=[VMEM] * count,
         compiler_params=pltpu.CompilerParams(vmem_limit_bytes=4 * 2**20),
         out_shape=[jax.ShapeDtypeStruct((skeleton, 2 * skeleton), jnp.bfloat16)] * count,
         scratch_shapes=[pltpu.SemaphoreType.DMA((count,))],
-    )(in_hbm(comp_transfer), in_hbm(exp_transfer))
+    )(in_hbm(exp_transfer))
 
 
 def side_level_kernel(axis, bit, scaled, own_ref, partner_ref, rows_ref, gain_ref, out_ref):
@@ -194,6 +209,8 @@
     upper = position // 2**bit % 2
     here = pl.multiple_of(upper * skeleton, skeleton)
     there = pl.multiple_of((1 - upper) * skeleton, skeleton)
+    if len(rows_ref.shape) == 3:
+        rows_ref = rows_ref.at[bit, pl.ds(here, skeleton)]
     mixed = mm(rows_ref[:, pl.ds(here, skeleton)], own_ref[...])
     mixed += mm(rows_ref[:, pl.ds(there, skeleton)], partner_ref[...])
     if scaled:
@@ -219,11 +236,7 @@
     return -(-sent // 8) * 8
 
 
-def levels_kernel(strides, pad, packed_ref, comp_ref, exp_hbm, out_ref, exp_ref, sems):
-    copies = []
-    for number in range(exp_hbm.shape[0]):
-        copies.append(pltpu.make_async_copy(exp_hbm.at[number], exp_ref.at[number], sems.at[number]))
-        copies[-1].start()
+def levels_kernel(strides, pad, packed_ref, comp_ref, exp_ref, out_ref):
     boxes, rows, _ = packed_ref.shape
     width = (rows - pad) // 2
     skeleton = 2 * LANES
@@ -232,8 +245,6 @@
     gains = packed[:, 2 * width :, :]
     for number, stride in enumerate(strides):
         turned = number >= comp_ref.shape[0]
-        if turned:
-            copies[number - comp_ref.shape[0]].wait()
         transfer = exp_ref[number - comp_ref.shape[0]] if turned else comp_ref[number]
         halves = state.reshape(boxes // (2 * stride), 2, stride * width, skeleton)
         low = halves[:, 0].reshape(boxes // 2 * width, skeleton).astype(jnp.bfloat16)
@@ -256,15 +267,11 @@
     boxes, rows, _ = packed.shape
     return pl.pallas_call(
         functools.partial(levels_kernel, strides, pad),
-        in_specs=[VMEM, VMEM, HBM],
+        in_specs=[VMEM] * 3,
         compiler_params=pltpu.CompilerParams(vmem_limit_bytes=20 * 2**20),
         out_specs=VMEM,
         out_shape=jax.ShapeDtypeStruct((boxes, rows - pad, LANES), jnp.bfloat16),
-        scratch_shapes=[
-            pltpu.VMEM(exp_transfer.shape, jnp.bfloat16),
-            pltpu.SemaphoreType.DMA((exp_transfer.shape[0],)),
-        ],
-    )(on_chip(packed), on_chip(comp_transfer), in_hbm(exp_transfer))
+    )(on_chip(packed), on_chip(comp_transfer), on_chip(exp_transfer))
 
 
 def decode_kernel(blocks, side_ref, packed_ref, decoder_ref, out_hbm, turned_ref, held, sems):
@@ -379,14 +386,13 @@
     packed = encode(sources, enc_scale, encoder, comp_gain, exp_gain, parts, side)
     packed = lax.all_to_all(packed, ORDER, 0, 0, tiled=True)
     coeffs = side_encode(sources, enc_scale, encoder, side)
-    rows = pick(comp_transfer, exp_transfer)
+    rows = pick(exp_transfer)
     for number in range(comp_levels):
-        coeffs = side_level(coeffs, "col", number, True, rows[number], comp_gain)
+        coeffs = side_level(coeffs, "col", number, True, comp_transfer, comp_gain)
     packed = levels(packed, comp_transfer, exp_transfer, strides, pad)
     packed = lax.all_to_all(packed, ORDER, 0, 0, tiled=True)
     for number in range(exp_levels):
-        scaled = number + 1 < exp_levels
-        coeffs = side_level(coeffs, "row", number, scaled, rows[comp_levels + number], exp_gain)
+        coeffs = side_level(coeffs, "row", number, number + 1 < exp_levels, rows[number], exp_gain)
     table = on_chip((decoder.astype(jnp.float32) * factors).astype(jnp.bfloat16))
     return decode(coeffs, packed, table)
 

time: 69.9 us -> 70 us (level)
  local copies, waits for them, and re-layouts: 0.04 us -> 3.03 us
  Pallas kernels: 20.5 us -> 17.9 us
    unnamed x8 -> x18, local copies, waits for them, and re-layouts: 0.03 us -> 3.02 us
    pallas_call x1, Pallas kernels: 3.44 us -> 2.24 us  [levels(): pl.pallas_call(functools.partial(levels_kernel, strides, pad), in_specs=[...]
    pallas_call x1, Pallas kernels: 7.02 us -> 6 us  [encode(): pl.pallas_call(functools.partial(encode_kernel, blocks, first), in_specs=...]
    all_to_all x2, waiting for transfers between devices: 9.64 us -> 8.69 us  [body(): packed = lax.all_to_all(packed, ORDER, 0, 0, tiled=True)]
  transfers between devices with their start and end apart: 7 -> 7, of which waited for: 5 -> 4; matrix products, arithmetic and copies ran while one was open for 3% -> 3% of each run, Pallas kernels for 14% -> 12%
where the time goes in v6:
time: 70 us; the launch traced here: 68.9 us
  waiting for transfers between devices  26.7 us (38%)
  starting transfers between devices  19.2 us (27%)
  Pallas kernels  17.9 us (26%)
  local copies, waits for them, and re-layouts  3.03 us (4%)
  other arithmetic  1.94 us (3%)
    ppermute x5, waiting for transfers between devices, side_level(): partner = lax.ppermute(own, axis, pairs)  18.1 us
    all_to_all x2, starting transfers between devices, body(): packed = lax.all_to_all(packed, ORDER, 0, 0, tiled=True)  11.4 us
    all_to_all x2, waiting for transfers between devices, body(): packed = lax.all_to_all(packed, ORDER, 0, 0, tiled=True)  8.69 us
    ppermute x5, starting transfers between devices, side_level(): partner = lax.ppermute(own, axis, pairs)  7.75 us
    pallas_call x1, Pallas kernels, encode(): pl.pallas_call(functools.partial(encode_kernel, blocks, first), in_specs=...  6 us
    pallas_call x1, Pallas kernels, decode(): pl.pallas_call(functools.partial(decode_kernel, blocks), in_specs=[VMEM,...  3.89 us
    pallas_call x1, Pallas kernels, side_encode(): pl.pallas_call(functools.partial(side_encode_kernel, blocks), in_specs=[H...  3.16 us
    unnamed x18, local copies, waits for them, and re-layouts  3.02 us
  transfers between devices with their start and end apart: 7, of which 4 were waited for; matrix products, arithmetic and copies ran while one was open for 3% of the time, Pallas kernels for 12%

profile of v6, /device:TPU:0, one launch (start us, length us, event | category | flops | bytes accessed | tf_op | source)
XLA Modules:
  0.0 68.9 jit_solution(12995915564400439244)
XLA Ops:
  0.0 6.0 %shard_map.98 = bf16[32,56,128]{2,1,0:T(8,128)(2,1)} custom-call(bf16[4096,1024]{1,0:T(8,128)(2,1)} %sources_hbm.3, f32[1,4096]{1,0:T(1,128)} %bitcast.11, bf16[256,4096]{1,0:T(8,128)(2,1)} %encoder_hbm.3, f32[2,4,256]{2,1,0:T(4,128)} %bitcast.8, f32[3,8,256]{2,1,0:T(8,128)} %bitcast.4), custom_call_target="tpu_custom_call" | custom-call | tf_op jit(solution)/shard_map/pallas_call | solution.py:114
  6.0 7.3 %all-to-all-start = ((bf16[32,56,128]{2,1,0:T(8,128)(2,1)}), bf16[32,56,128]{2,1,0:T(8,128)(2,1)S(1)}, u32[]{:S(2)}, u32[]{:S(2)}) async-start(bf16[32,56,128]{2,1,0:T(8,128)(2,1)} %shard_map.98), calls=%async_computation | async-start | bytes 917504 | tf_op jit(solution)/shard_map/all_to_all | solution.py:387
  13.4 0.0 copy-start
  13.4 0.0 copy-start.7
  13.4 3.2 %shard_map.91.own_ref = bf16[256,256]{1,0:T(8,128)(2,1)S(1)} custom-call(bf16[4096,1024]{1,0:T(8,128)(2,1)} %sources_hbm.3, f32[1,4096]{1,0:T(1,128)} %bitcast.12, bf16[256,4096]{1,0:T(8,128)(2,1)} %encoder_hbm.3), custom_call_target="tpu_custom_call" | custom-call | tf_op jit(solution)/shard_map/pallas_call | solution.py:164
  16.5 0.0 copy-start.2
  16.6 0.0 copy-start.1
  16.6 1.8 %collective-permute-start = (bf16[256,256]{1,0:T(8,128)(2,1)S(1)}, bf16[256,256]{1,0:T(8,128)(2,1)S(1)}, u32[]{:S(2)}, u32[]{:S(2)}) collective-permute-start(bf16[256,256]{1,0:T(8,128)(2,1)S(1)} %shard_map.91.own_ref), channel_id=1, source_target_pairs={{0,8},{8,0},{16,24},{24,16},{1,9},{9,1},{17,25},{25,17},{2,10},{10... | collective-permute-start | bytes 393224 | tf_op jit(solution)/shard_map/ppermute | solution.py:224
  18.4 7.7 %collective-permute-done.partner_ref = bf16[256,256]{1,0:T(8,128)(2,1)S(1)} collective-permute-done((bf16[256,256]{1,0:T(8,128)(2,1)S(1)}, bf16[256,256]{1,0:T(8,128)(2,1)S(1)}, u32[]{:S(2)}, u32[]{:S(2)}) %collective-permute-start) | collective-permute-done | bytes 131104 | tf_op jit(solution)/shard_map/ppermute | solution.py:224
  26.1 0.0 copy-done
  26.1 0.0 copy-done.7
  26.1 0.3 shard_map.92.own_ref
  26.4 0.0 copy-start.8
  26.4 2.8 %collective-permute-start.1 = (bf16[256,256]{1,0:T(8,128)(2,1)S(1)}, bf16[256,256]{1,0:T(8,128)(2,1)S(1)}, u32[]{:S(2)}, u32[]{:S(2)}) collective-permute-start(bf16[256,256]{1,0:T(8,128)(2,1)S(1)} %shard_map.92.own_ref), channel_id=1, source_target_pairs={{0,16},{8,24},{16,0},{24,8},{1,17},{9,25},{17,1},{25,9},{2,18},{10... | collective-permute-start | bytes 393224 | tf_op jit(solution)/shard_map/ppermute | solution.py:224
  29.2 6.0 %collective-permute-done.1.partner_ref = bf16[256,256]{1,0:T(8,128)(2,1)S(1)} collective-permute-done((bf16[256,256]{1,0:T(8,128)(2,1)S(1)}, bf16[256,256]{1,0:T(8,128)(2,1)S(1)}, u32[]{:S(2)}, u32[]{:S(2)}) %collective-permute-start.1) | collective-permute-done | bytes 131104 | tf_op jit(solution)/shard_map/ppermute | solution.py:224
  35.2 0.3 shard_map.93.own_ref
  35.5 0.1 collective-permute-start.2
  35.6 1.1 %shard_map.94 = (bf16[256,512]{1,0:T(8,128)(2,1)S(1)}, bf16[256,512]{1,0:T(8,128)(2,1)S(1)}, bf16[256,512]{1,0:T(8,128)(2,1)S(1)}) custom-call(bf16[3,512,512]{2,1,0:T(8,128)(2,1)} %exp_ref.1), custom_call_target="tpu_custom_call" | custom-call | tf_op jit(solution)/shard_map/pallas_call | solution.py:196
  36.7 0.0 copy-start.5
  36.7 0.7 %copy-done.5 = bf16[256,512]{1,0:T(8,128)(2,1)} copy-done((bf16[256,512]{1,0:T(8,128)(2,1)}, bf16[256,512]{1,0:T(8,128)(2,1)S(1)}, u32[]{:S(2)}) %copy-start.5) | copy-done | bytes 262168
  37.4 0.0 copy-start.3
  37.4 0.0 collective-permute-done.2.partner_ref
  37.4 0.0 copy-done.2
  37.4 0.3 shard_map.95.own_ref
  37.7 0.4 copy-done.3
  38.1 1.5 %collective-permute-start.3 = (bf16[256,256]{1,0:T(8,128)(2,1)S(1)}, bf16[256,256]{1,0:T(8,128)(2,1)S(1)}, u32[]{:S(2)}, u32[]{:S(2)}) collective-permute-start(bf16[256,256]{1,0:T(8,128)(2,1)S(1)} %shard_map.95.own_ref), channel_id=1, source_target_pairs={{0,2},{1,3},{2,0},{3,1},{4,6},{5,7},{6,4},{7,5},{8,10},{9,11},{10,... | collective-permute-start | bytes 393224 | tf_op jit(solution)/shard_map/ppermute | solution.py:224
  39.6 4.4 %collective-permute-done.3.partner_ref = bf16[256,256]{1,0:T(8,128)(2,1)S(1)} collective-permute-done((bf16[256,256]{1,0:T(8,128)(2,1)S(1)}, bf16[256,256]{1,0:T(8,128)(2,1)S(1)}, u32[]{:S(2)}, u32[]{:S(2)}) %collective-permute-start.3) | collective-permute-done | bytes 131104 | tf_op jit(solution)/shard_map/ppermute | solution.py:224
  44.0 0.0 copy-start.6
  44.0 0.9 %copy-done.6 = bf16[256,512]{1,0:T(8,128)(2,1)S(1)} copy-done((bf16[256,512]{1,0:T(8,128)(2,1)S(1)}, bf16[256,512]{1,0:T(8,128)(2,1)}, u32[]{:S(2)}) %copy-start.6) | copy-done | bytes 262168
  45.0 0.3 shard_map.96.own_ref
  45.3 1.6 %collective-permute-start.4 = (bf16[256,256]{1,0:T(8,128)(2,1)S(1)}, bf16[256,256]{1,0:T(8,128)(2,1)S(1)}, u32[]{:S(2)}, u32[]{:S(2)}) collective-permute-start(bf16[256,256]{1,0:T(8,128)(2,1)S(1)} %shard_map.96.own_ref), channel_id=1, source_target_pairs={{0,4},{1,5},{2,6},{3,7},{4,0},{5,1},{6,2},{7,3},{8,12},{9,13},{10,... | collective-permute-start | bytes 393224 | tf_op jit(solution)/shard_map/ppermute | solution.py:224
  46.8 0.0 all-to-all-done.packed_ref
  46.8 0.0 copy-done.1
  46.8 2.2 %shard_map.99 = bf16[32,48,128]{2,1,0:T(8,128)(2,1)} custom-call(bf16[32,56,128]{2,1,0:T(8,128)(2,1)S(1)} %all-to-all-done.packed_ref, bf16[2,512,512]{2,1,0:T(8,128)(2,1)S(1)} %copy-done, bf16[3,512,512]{2,1,0:T(8,128)(2,1)S(1)} %copy-done.1), custom_call_target="tpu_custom_call" | custom-call | tf_op jit(solution)/shard_map/pallas_call | solution.py:268
  49.1 4.1 %all-to-all-start.1 = ((bf16[32,48,128]{2,1,0:T(8,128)(2,1)}), bf16[32,48,128]{2,1,0:T(8,128)(2,1)S(1)}, u32[]{:S(2)}, u32[]{:S(2)}) async-start(bf16[32,48,128]{2,1,0:T(8,128)(2,1)} %shard_map.99), calls=%async_computation.1 | async-start | bytes 786432 | tf_op jit(solution)/shard_map/all_to_all | solution.py:393
  53.2 0.0 copy-done.8
  53.2 1.9 %multiply_convert_fusion.decoder_ref = bf16[4096,256]{1,0:T(8,128)(2,1)S(1)} fusion(bf16[4096,256]{1,0:T(8,128)(2,1)} %param.16, f32[256]{0:T(256)S(1)} %bitcast.13, f32[4096]{0:T(1024)S(1)} %copy-done.8), kind=kLoop, calls=%fused_computation | loop fusion | flops 4194304 | bytes 4211712 | tf_op jit(solution)/shard_map/convert_element_type | solution.py:396
  55.1 0.0 collective-permute-done.4.partner_ref
  55.1 0.0 copy-start.4
  55.1 0.9 %copy-done.4 = bf16[256,512]{1,0:T(8,128)(2,1)S(1)} copy-done((bf16[256,512]{1,0:T(8,128)(2,1)S(1)}, bf16[256,512]{1,0:T(8,128)(2,1)}, u32[]{:S(2)}) %copy-start.4) | copy-done | bytes 262168
  56.1 0.2 shard_map.97.side_ref
  56.3 8.7 %all-to-all-done.1.packed_ref = bf16[32,48,128]{2,1,0:T(8,128)(2,1)S(1)} async-done(((bf16[32,48,128]{2,1,0:T(8,128)(2,1)}), bf16[32,48,128]{2,1,0:T(8,128)(2,1)S(1)}, u32[]{:S(2)}, u32[]{:S(2)}) %all-to-all-start.1) | async-done | bytes 393248 | tf_op jit(solution)/shard_map/all_to_all | solution.py:393
  65.0 3.9 %shard_map.100 = bf16[4096,1024]{1,0:T(8,128)(2,1)} custom-call(bf16[256,256]{1,0:T(8,128)(2,1)S(1)} %shard_map.97.side_ref, bf16[32,48,128]{2,1,0:T(8,128)(2,1)S(1)} %all-to-all-done.1.packed_ref, bf16[4096,256]{1,0:T(8,128)(2,1)S(1)} %multiply_convert_fusion.decoder_ref), custom_call_target="tpu_custom_call" | custom-call | tf_op jit(solution)/shard_map/pallas_call | solution.py:302
  (2 shorter events, 0.0 us)
Async XLA Ops:
  6.0 40.8 %all-to-all-start = ((bf16[32,56,128]{2,1,0:T(8,128)(2,1)}), bf16[32,56,128]{2,1,0:T(8,128)(2,1)S(1)}, u32[]{:S(2)}, u32[]{:S(2)}) async-start(bf16[32,56,128]{2,1,0:T(8,128)(2,1)} %shard_map.98), calls=%async_computation | async-start | bytes 917504 | tf_op jit(solution)/shard_map/all_to_all | solution.py:387
  13.4 12.7 %copy-start = (bf16[2,512,512]{2,1,0:T(8,128)(2,1)S(1)}, bf16[2,512,512]{2,1,0:T(8,128)(2,1)}, u32[]{:S(2)}) copy-start(bf16[2,512,512]{2,1,0:T(8,128)(2,1)} %comp_ref.1) | copy-start | bytes 3145732
  13.4 12.7 %copy-start.7 = (f32[2,1,4,256]{3,2,1,0:T(4,128)S(1)}, f32[2,1,4,256]{3,2,1,0:T(4,128)}, u32[]{:S(2)}) copy-start(f32[2,1,4,256]{3,2,1,0:T(4,128)} %param.13) | copy-start | bytes 24580
  16.5 20.9 %copy-start.2 = (f32[3,1,8,256]{3,2,1,0:T(8,128)S(1)}, f32[3,1,8,256]{3,2,1,0:T(8,128)}, u32[]{:S(2)}) copy-start(f32[3,1,8,256]{3,2,1,0:T(8,128)} %param.15) | copy-start | bytes 73732
  16.6 30.3 %copy-start.1 = (bf16[3,512,512]{2,1,0:T(8,128)(2,1)S(1)}, bf16[3,512,512]{2,1,0:T(8,128)(2,1)}, u32[]{:S(2)}) copy-start(bf16[3,512,512]{2,1,0:T(8,128)(2,1)} %exp_ref.1) | copy-start | bytes 4718596
  16.6 9.5 %collective-permute-start = (bf16[256,256]{1,0:T(8,128)(2,1)S(1)}, bf16[256,256]{1,0:T(8,128)(2,1)S(1)}, u32[]{:S(2)}, u32[]{:S(2)}) collective-permute-start(bf16[256,256]{1,0:T(8,128)(2,1)S(1)} %shard_map.91.own_ref), channel_id=1, source_target_pairs={{0,8},{8,0},{16,24},{24,16},{1,9},{9,1},{17,25},{25,17},{2,10},{10... | collective-permute-start | bytes 393224 | tf_op jit(solution)/shard_map/ppermute | solution.py:224
  26.4 26.8 %copy-start.8 = (f32[4096]{0:T(1024)S(1)}, f32[4096]{0:T(1024)}, u32[]{:S(2)}) copy-start(f32[4096]{0:T(1024)} %param.17) | copy-start | bytes 49156
  26.4 8.8 %collective-permute-start.1 = (bf16[256,256]{1,0:T(8,128)(2,1)S(1)}, bf16[256,256]{1,0:T(8,128)(2,1)S(1)}, u32[]{:S(2)}, u32[]{:S(2)}) collective-permute-start(bf16[256,256]{1,0:T(8,128)(2,1)S(1)} %shard_map.92.own_ref), channel_id=1, source_target_pairs={{0,16},{8,24},{16,0},{24,8},{1,17},{9,25},{17,1},{25,9},{2,18},{10... | collective-permute-start | bytes 393224 | tf_op jit(solution)/shard_map/ppermute | solution.py:224
  35.5 1.9 %collective-permute-start.2 = (bf16[256,256]{1,0:T(8,128)(2,1)S(1)}, bf16[256,256]{1,0:T(8,128)(2,1)S(1)}, u32[]{:S(2)}, u32[]{:S(2)}) collective-permute-start(bf16[256,256]{1,0:T(8,128)(2,1)S(1)} %shard_map.93.own_ref), channel_id=1, source_target_pairs={{0,1},{1,0},{2,3},{3,2},{4,5},{5,4},{6,7},{7,6},{8,9},{9,8},{10,11... | collective-permute-start | bytes 393224 | tf_op jit(solution)/shard_map/ppermute | solution.py:224
  36.7 0.7 %copy-start.5 = (bf16[256,512]{1,0:T(8,128)(2,1)}, bf16[256,512]{1,0:T(8,128)(2,1)S(1)}, u32[]{:S(2)}) copy-start(bf16[256,512]{1,0:T(8,128)(2,1)S(1)} %get-tuple-element.9.rows_ref) | copy-start | bytes 786436
  37.4 0.7 %copy-start.3 = (bf16[256,512]{1,0:T(8,128)(2,1)}, bf16[256,512]{1,0:T(8,128)(2,1)S(1)}, u32[]{:S(2)}) copy-start(bf16[256,512]{1,0:T(8,128)(2,1)S(1)} %get-tuple-element.10.rows_ref) | copy-start | bytes 786436
  38.1 5.9 %collective-permute-start.3 = (bf16[256,256]{1,0:T(8,128)(2,1)S(1)}, bf16[256,256]{1,0:T(8,128)(2,1)S(1)}, u32[]{:S(2)}, u32[]{:S(2)}) collective-permute-start(bf16[256,256]{1,0:T(8,128)(2,1)S(1)} %shard_map.95.own_ref), channel_id=1, source_target_pairs={{0,2},{1,3},{2,0},{3,1},{4,6},{5,7},{6,4},{7,5},{8,10},{9,11},{10,... | collective-permute-start | bytes 393224 | tf_op jit(solution)/shard_map/ppermute | solution.py:224
  44.0 1.0 %copy-start.6 = (bf16[256,512]{1,0:T(8,128)(2,1)S(1)}, bf16[256,512]{1,0:T(8,128)(2,1)}, u32[]{:S(2)}) copy-start(bf16[256,512]{1,0:T(8,128)(2,1)} %copy-done.5) | copy-start | bytes 786436
  45.3 9.9 %collective-permute-start.4 = (bf16[256,256]{1,0:T(8,128)(2,1)S(1)}, bf16[256,256]{1,0:T(8,128)(2,1)S(1)}, u32[]{:S(2)}, u32[]{:S(2)}) collective-permute-start(bf16[256,256]{1,0:T(8,128)(2,1)S(1)} %shard_map.96.own_ref), channel_id=1, source_target_pairs={{0,4},{1,5},{2,6},{3,7},{4,0},{5,1},{6,2},{7,3},{8,12},{9,13},{10,... | collective-permute-start | bytes 393224 | tf_op jit(solution)/shard_map/ppermute | solution.py:224
  49.1 15.9 %all-to-all-start.1 = ((bf16[32,48,128]{2,1,0:T(8,128)(2,1)}), bf16[32,48,128]{2,1,0:T(8,128)(2,1)S(1)}, u32[]{:S(2)}, u32[]{:S(2)}) async-start(bf16[32,48,128]{2,1,0:T(8,128)(2,1)} %shard_map.99), calls=%async_computation.1 | async-start | bytes 786432 | tf_op jit(solution)/shard_map/all_to_all | solution.py:393
  55.1 1.0 %copy-start.4 = (bf16[256,512]{1,0:T(8,128)(2,1)S(1)}, bf16[256,512]{1,0:T(8,128)(2,1)}, u32[]{:S(2)}) copy-start(bf16[256,512]{1,0:T(8,128)(2,1)} %copy-done.3) | copy-start | bytes 786436

commit v7 on v6

--- a/solution.py
+++ b/solution.py
@@ -95,13 +95,19 @@
     gains = jnp.concatenate(gains, axis=0)
     parts, rows, _ = out_ref.shape
     width = (rows - pad) // 2
-    turned = acc_ref[...].T.reshape(parts, width, 2 * LANES)
-    gains = jnp.broadcast_to(gains[None], (parts, pad, LANES))
-    joined = jnp.concatenate([turned[:, :, :LANES], turned[:, :, LANES:], gains], axis=1)
-    out_ref[...] = joined.astype(jnp.bfloat16)
-    copy = pltpu.make_async_copy(out_ref, out_hbm, small.at[len(pairs)])
-    copy.start()
-    copy.wait()
+    groups = 2
+    some = parts // groups
+    gains = jnp.broadcast_to(gains[None], (some, pad, LANES))
+    copies = []
+    for number in range(groups):
+        turned = acc_ref[:, number * some * width : (number + 1) * some * width].T.reshape(some, width, 2 * LANES)
+        joined = jnp.concatenate([turned[:, :, :LANES], turned[:, :, LANES:], gains], axis=1)
+        out_ref[number * some : (number + 1) * some] = joined.astype(jnp.bfloat16)
+        span = pl.ds(number * some, some)
+        copies.append(pltpu.make_async_copy(out_ref.at[span], out_hbm.at[span], small.at[len(pairs) + number]))
+        copies[-1].start()
+    for copy in copies:
+        copy.wait()
 
 
 def encode(sources, enc_scale, encoder, comp_gain, exp_gain, parts, first):
@@ -126,7 +132,7 @@
             pltpu.VMEM(comp_gain.shape, jnp.float32),
             pltpu.VMEM(exp_gain.shape, jnp.float32),
             pltpu.VMEM(packed, jnp.bfloat16),
-            pltpu.SemaphoreType.DMA((4,)),
+            pltpu.SemaphoreType.DMA((5,)),
         ],
     )(sources, in_hbm(enc_scale.reshape(1, points)), encoder, in_hbm(comp_gain), in_hbm(exp_gain))
 
@@ -203,27 +209,32 @@
     )(in_hbm(exp_transfer))
 
 
-def side_level_kernel(axis, bit, scaled, own_ref, partner_ref, rows_ref, gain_ref, out_ref):
+def mix(axis, bit, own_ref, partner_ref, rows_ref):
     skeleton = own_ref.shape[0]
-    position = lax.axis_index(axis)
-    upper = position // 2**bit % 2
+    upper = lax.axis_index(axis) // 2**bit % 2
     here = pl.multiple_of(upper * skeleton, skeleton)
     there = pl.multiple_of((1 - upper) * skeleton, skeleton)
     if len(rows_ref.shape) == 3:
         rows_ref = rows_ref.at[bit, pl.ds(here, skeleton)]
     mixed = mm(rows_ref[:, pl.ds(here, skeleton)], own_ref[...])
-    mixed += mm(rows_ref[:, pl.ds(there, skeleton)], partner_ref[...])
-    if scaled:
-        gain = jnp.broadcast_to(gain_ref[bit, pl.ds(position, 1), :], (8, skeleton)).T
-        mixed *= gain[:, :1]
+    return mixed + mm(rows_ref[:, pl.ds(there, skeleton)], partner_ref[...])
+
+
+def side_level_kernel(axis, bit, own_ref, partner_ref, rows_ref, gain_ref, out_ref):
+    mixed = mix(axis, bit, own_ref, partner_ref, rows_ref)
+    gain = gain_ref[bit, pl.ds(lax.axis_index(axis), 1), :]
+    mixed *= jnp.broadcast_to(gain, (8, gain.shape[1])).T[:, :1]
     out_ref[...] = mixed.astype(jnp.bfloat16)
 
 
-def side_level(own, axis, bit, scaled, rows, gain):
-    pairs = [(source, source ^ 2**bit) for source in range(lax.axis_size(axis))]
-    partner = lax.ppermute(own, axis, pairs)
-    return pl.pallas_call(
-        functools.partial(side_level_kernel, axis, bit, scaled),
+def from_partner(own, axis, bit):
+    return lax.ppermute(own, axis, [(source, source ^ 2**bit) for source in range(lax.axis_size(axis))])
+
+
+def side_level(own, axis, bit, rows, gain):
+    partner = from_partner(own, axis, bit)
+    return pl.pallas_call(
+        functools.partial(side_level_kernel, axis, bit),
         in_specs=[VMEM] * 4,
         compiler_params=pltpu.CompilerParams(vmem_limit_bytes=4 * 2**20),
         out_specs=VMEM,
@@ -274,13 +285,13 @@
     )(on_chip(packed), on_chip(comp_transfer), on_chip(exp_transfer))
 
 
-def decode_kernel(blocks, side_ref, packed_ref, decoder_ref, out_hbm, turned_ref, held, sems):
+def decode_kernel(blocks, bit, side_ref, partner_ref, rows_ref, packed_ref, decoder_ref, out_hbm, turned_ref, held, sems):
     boxes, rows, _ = packed_ref.shape
     width, side = rows // 2, side_ref.shape[1]
     packed = packed_ref[...].astype(jnp.float32)
     coeffs = jnp.concatenate([packed[:, :width, :], packed[:, width:, :]], axis=-1)
     coeffs = coeffs.reshape(boxes * width, 2 * LANES)
-    turned_ref[:, :side] = side_ref[...]
+    turned_ref[:, :side] = mix("row", bit, side_ref, partner_ref, rows_ref).astype(jnp.bfloat16)
     turned_ref[:, side:] = coeffs.T.astype(jnp.bfloat16)
     block = decoder_ref.shape[0] // blocks
     copies = []
@@ -294,14 +305,14 @@
         copy.wait()
 
 
-def decode(side, packed, decoder):
+def decode(bit, side, partner, last_rows, packed, decoder):
     boxes, rows, _ = packed.shape
     points, skeleton = decoder.shape
     width = side.shape[1] + boxes * rows // 2
     blocks = 8
     return pl.pallas_call(
-        functools.partial(decode_kernel, blocks),
-        in_specs=[VMEM, VMEM, VMEM],
+        functools.partial(decode_kernel, blocks, bit),
+        in_specs=[VMEM] * 5,
         compiler_params=pltpu.CompilerParams(vmem_limit_bytes=20 * 2**20),
         out_specs=HBM,
         out_shape=jax.ShapeDtypeStruct((points, width), jnp.bfloat16),
@@ -310,7 +321,7 @@
             pltpu.VMEM((points, width), jnp.bfloat16),
             pltpu.SemaphoreType.DMA((blocks,)),
         ],
-    )(on_chip(side), on_chip(packed), decoder)
+    )(on_chip(side), on_chip(partner), on_chip(last_rows), on_chip(packed), decoder)
 
 
 def plain_encode(sources, enc_scale, encoder, comp_gain, exp_gain, parts):
@@ -388,13 +399,14 @@
     coeffs = side_encode(sources, enc_scale, encoder, side)
     rows = pick(exp_transfer)
     for number in range(comp_levels):
-        coeffs = side_level(coeffs, "col", number, True, comp_transfer, comp_gain)
+        coeffs = side_level(coeffs, "col", number, comp_transfer, comp_gain)
     packed = levels(packed, comp_transfer, exp_transfer, strides, pad)
     packed = lax.all_to_all(packed, ORDER, 0, 0, tiled=True)
-    for number in range(exp_levels):
-        coeffs = side_level(coeffs, "row", number, number + 1 < exp_levels, rows[number], exp_gain)
+    for number in range(exp_levels - 1):
+        coeffs = side_level(coeffs, "row", number, rows[number], exp_gain)
+    partner = from_partner(coeffs, "row", exp_levels - 1)
     table = on_chip((decoder.astype(jnp.float32) * factors).astype(jnp.bfloat16))
-    return decode(coeffs, packed, table)
+    return decode(exp_levels - 1, coeffs, partner, rows[exp_levels - 1], packed, table)
 
 
 def solution(mesh):

time: 70 us -> 71 us (1.014)
  waiting for transfers between devices: 26.7 us -> 27.9 us
  local copies, waits for them, and re-layouts: 3.03 us -> 2.09 us
    all_to_all x2, waiting for transfers between devices: 8.69 us -> 9.88 us  [body(): packed = lax.all_to_all(packed, ORDER, 0, 0, tiled=True)]
    unnamed x18, local copies, waits for them, and re-layouts: 3.02 us -> 2.08 us
    pallas_call x6 -> x5, Pallas kernels: 5.3 us -> 6.08 us  [the longest x1 4.91 us: decode(): pl.pallas_call(functools.partial(decode_kernel, blocks, bit), in_specs=[V...]
  transfers between devices with their start and end apart: 7 -> 7, of which waited for: 4 -> 4; matrix products, arithmetic and copies ran while one was open for 3% -> 3% of each run, Pallas kernels for 12% -> 11%
where the time goes in v7:
time: 71 us; the launch traced here: 69.8 us
  waiting for transfers between devices  27.9 us (39%)
  starting transfers between devices  19.2 us (27%)
  Pallas kernels  18.6 us (26%)
  local copies, waits for them, and re-layouts  2.09 us (3%)
  other arithmetic  1.94 us (3%)
    ppermute x5, waiting for transfers between devices, from_partner(): lax.ppermute(own, axis, [(source, source ^ 2 ** bit) for source in range(...  18.1 us
    all_to_all x2, starting transfers between devices, body(): packed = lax.all_to_all(packed, ORDER, 0, 0, tiled=True)  11.4 us
    all_to_all x2, waiting for transfers between devices, body(): packed = lax.all_to_all(packed, ORDER, 0, 0, tiled=True)  9.88 us
    ppermute x5, starting transfers between devices, from_partner(): lax.ppermute(own, axis, [(source, source ^ 2 ** bit) for source in range(...  7.75 us
    pallas_call x1, Pallas kernels, encode(): pl.pallas_call(functools.partial(encode_kernel, blocks, first), in_specs=...  5.93 us
    pallas_call x1, Pallas kernels, decode(): pl.pallas_call(functools.partial(decode_kernel, blocks, bit), in_specs=[V...  4.91 us
    pallas_call x1, Pallas kernels, side_encode(): pl.pallas_call(functools.partial(side_encode_kernel, blocks), in_specs=[H...  3.16 us
    pallas_call x1, Pallas kernels, levels(): pl.pallas_call(functools.partial(levels_kernel, strides, pad), in_specs=[...  2.23 us
  transfers between devices with their start and end apart: 7, of which 4 were waited for; matrix products, arithmetic and copies ran while one was open for 3% of the time, Pallas kernels for 11%

profile of v7, /device:TPU:0, one launch (start us, length us, event | category | flops | bytes accessed | tf_op | source)
XLA Modules:
  0.0 69.8 jit_solution(16586901252867081520)
XLA Ops:
  0.0 5.9 %shard_map.97 = bf16[32,56,128]{2,1,0:T(8,128)(2,1)} custom-call(bf16[4096,1024]{1,0:T(8,128)(2,1)} %sources_hbm.3, f32[1,4096]{1,0:T(1,128)} %bitcast.10, bf16[256,4096]{1,0:T(8,128)(2,1)} %encoder_hbm.3, f32[2,4,256]{2,1,0:T(4,128)} %bitcast.7, f32[3,8,256]{2,1,0:T(8,128)} %bitcast.4), custom_call_target="tpu_custom_call" | custom-call | tf_op jit(solution)/shard_map/pallas_call | solution.py:120
  5.9 7.3 %all-to-all-start = ((bf16[32,56,128]{2,1,0:T(8,128)(2,1)}), bf16[32,56,128]{2,1,0:T(8,128)(2,1)S(1)}, u32[]{:S(2)}, u32[]{:S(2)}) async-start(bf16[32,56,128]{2,1,0:T(8,128)(2,1)} %shard_map.97), calls=%async_computation | async-start | bytes 917504 | tf_op jit(solution)/shard_map/all_to_all | solution.py:398
  13.3 0.0 copy-start
  13.3 0.0 copy-start.7
  13.3 3.2 %shard_map.91.own_ref = bf16[256,256]{1,0:T(8,128)(2,1)S(1)} custom-call(bf16[4096,1024]{1,0:T(8,128)(2,1)} %sources_hbm.3, f32[1,4096]{1,0:T(1,128)} %bitcast.11, bf16[256,4096]{1,0:T(8,128)(2,1)} %encoder_hbm.3), custom_call_target="tpu_custom_call" | custom-call | tf_op jit(solution)/shard_map/pallas_call | solution.py:170
  16.5 0.0 copy-start.2
  16.5 0.0 copy-start.1
  16.5 1.8 %collective-permute-start = (bf16[256,256]{1,0:T(8,128)(2,1)S(1)}, bf16[256,256]{1,0:T(8,128)(2,1)S(1)}, u32[]{:S(2)}, u32[]{:S(2)}) collective-permute-start(bf16[256,256]{1,0:T(8,128)(2,1)S(1)} %shard_map.91.own_ref), channel_id=1, source_target_pairs={{0,8},{8,0},{16,24},{24,16},{1,9},{9,1},{17,25},{25,17},{2,10},{10... | collective-permute-start | bytes 393224 | tf_op jit(solution)/shard_map/ppermute | solution.py:231
  18.3 7.7 %collective-permute-done.partner_ref = bf16[256,256]{1,0:T(8,128)(2,1)S(1)} collective-permute-done((bf16[256,256]{1,0:T(8,128)(2,1)S(1)}, bf16[256,256]{1,0:T(8,128)(2,1)S(1)}, u32[]{:S(2)}, u32[]{:S(2)}) %collective-permute-start) | collective-permute-done | bytes 131104 | tf_op jit(solution)/shard_map/ppermute | solution.py:231
  26.0 0.0 copy-done
  26.0 0.0 copy-done.7
  26.0 0.3 shard_map.92.own_ref
  26.3 0.0 copy-start.8
  26.3 2.8 %collective-permute-start.1 = (bf16[256,256]{1,0:T(8,128)(2,1)S(1)}, bf16[256,256]{1,0:T(8,128)(2,1)S(1)}, u32[]{:S(2)}, u32[]{:S(2)}) collective-permute-start(bf16[256,256]{1,0:T(8,128)(2,1)S(1)} %shard_map.92.own_ref), channel_id=1, source_target_pairs={{0,16},{8,24},{16,0},{24,8},{1,17},{9,25},{17,1},{25,9},{2,18},{10... | collective-permute-start | bytes 393224 | tf_op jit(solution)/shard_map/ppermute | solution.py:231
  29.1 6.0 %collective-permute-done.1.partner_ref = bf16[256,256]{1,0:T(8,128)(2,1)S(1)} collective-permute-done((bf16[256,256]{1,0:T(8,128)(2,1)S(1)}, bf16[256,256]{1,0:T(8,128)(2,1)S(1)}, u32[]{:S(2)}, u32[]{:S(2)}) %collective-permute-start.1) | collective-permute-done | bytes 131104 | tf_op jit(solution)/shard_map/ppermute | solution.py:231
  35.1 0.3 shard_map.93.own_ref
  35.4 0.1 collective-permute-start.2
  35.5 1.1 %shard_map.94 = (bf16[256,512]{1,0:T(8,128)(2,1)S(1)}, bf16[256,512]{1,0:T(8,128)(2,1)S(1)}, bf16[256,512]{1,0:T(8,128)(2,1)S(1)}) custom-call(bf16[3,512,512]{2,1,0:T(8,128)(2,1)} %exp_ref.1), custom_call_target="tpu_custom_call" | custom-call | tf_op jit(solution)/shard_map/pallas_call | solution.py:202
  36.7 0.0 copy-start.5
  36.7 0.7 copy-done.5
  37.4 0.0 copy-start.3
  37.4 0.0 collective-permute-done.2.partner_ref
  37.4 0.0 copy-done.2
  37.4 0.3 shard_map.95.own_ref
  37.7 0.4 copy-done.3
  38.1 1.5 %collective-permute-start.3 = (bf16[256,256]{1,0:T(8,128)(2,1)S(1)}, bf16[256,256]{1,0:T(8,128)(2,1)S(1)}, u32[]{:S(2)}, u32[]{:S(2)}) collective-permute-start(bf16[256,256]{1,0:T(8,128)(2,1)S(1)} %shard_map.95.own_ref), channel_id=1, source_target_pairs={{0,2},{1,3},{2,0},{3,1},{4,6},{5,7},{6,4},{7,5},{8,10},{9,11},{10,... | collective-permute-start | bytes 393224 | tf_op jit(solution)/shard_map/ppermute | solution.py:231
  39.5 4.4 %collective-permute-done.3.partner_ref = bf16[256,256]{1,0:T(8,128)(2,1)S(1)} collective-permute-done((bf16[256,256]{1,0:T(8,128)(2,1)S(1)}, bf16[256,256]{1,0:T(8,128)(2,1)S(1)}, u32[]{:S(2)}, u32[]{:S(2)}) %collective-permute-start.3) | collective-permute-done | bytes 131104 | tf_op jit(solution)/shard_map/ppermute | solution.py:231
  43.9 0.0 copy-start.6
  43.9 0.9 %copy-done.6 = bf16[256,512]{1,0:T(8,128)(2,1)S(1)} copy-done((bf16[256,512]{1,0:T(8,128)(2,1)S(1)}, bf16[256,512]{1,0:T(8,128)(2,1)}, u32[]{:S(2)}) %copy-start.6) | copy-done | bytes 262168
  44.9 0.3 shard_map.96.side_ref
  45.2 0.0 copy-start.4
  45.2 1.6 %collective-permute-start.4 = (bf16[256,256]{1,0:T(8,128)(2,1)S(1)}, bf16[256,256]{1,0:T(8,128)(2,1)}, u32[]{:S(2)}, u32[]{:S(2)}) collective-permute-start(bf16[256,256]{1,0:T(8,128)(2,1)S(1)} %shard_map.96.side_ref), channel_id=1, source_target_pairs={{0,4},{1,5},{2,6},{3,7},{4,0},{5,1},{6,2},{7,3},{8,12},{9,13},{10,... | collective-permute-start | bytes 393224 | tf_op jit(solution)/shard_map/ppermute | solution.py:231
  46.8 0.0 all-to-all-done.packed_ref
  46.8 0.0 copy-done.1
  46.8 2.2 %shard_map.98 = bf16[32,48,128]{2,1,0:T(8,128)(2,1)} custom-call(bf16[32,56,128]{2,1,0:T(8,128)(2,1)S(1)} %all-to-all-done.packed_ref, bf16[2,512,512]{2,1,0:T(8,128)(2,1)S(1)} %copy-done, bf16[3,512,512]{2,1,0:T(8,128)(2,1)S(1)} %copy-done.1), custom_call_target="tpu_custom_call" | custom-call | tf_op jit(solution)/shard_map/pallas_call | solution.py:279
  49.0 4.1 %all-to-all-start.1 = ((bf16[32,48,128]{2,1,0:T(8,128)(2,1)}), bf16[32,48,128]{2,1,0:T(8,128)(2,1)S(1)}, u32[]{:S(2)}, u32[]{:S(2)}) async-start(bf16[32,48,128]{2,1,0:T(8,128)(2,1)} %shard_map.98), calls=%async_computation.1 | async-start | bytes 786432 | tf_op jit(solution)/shard_map/all_to_all | solution.py:404
  53.1 0.0 copy-done.8
  53.1 1.9 %multiply_convert_fusion.decoder_ref = bf16[4096,256]{1,0:T(8,128)(2,1)S(1)} fusion(bf16[4096,256]{1,0:T(8,128)(2,1)} %param.16, f32[256]{0:T(256)S(1)} %bitcast.12, f32[4096]{0:T(1024)S(1)} %copy-done.8), kind=kLoop, calls=%fused_computation | loop fusion | flops 4194304 | bytes 4211712 | tf_op jit(solution)/shard_map/convert_element_type | solution.py:408
  55.0 0.0 collective-permute-done.4.partner_ref
  55.1 9.9 %all-to-all-done.1.packed_ref = bf16[32,48,128]{2,1,0:T(8,128)(2,1)S(1)} async-done(((bf16[32,48,128]{2,1,0:T(8,128)(2,1)}), bf16[32,48,128]{2,1,0:T(8,128)(2,1)S(1)}, u32[]{:S(2)}, u32[]{:S(2)}) %all-to-all-start.1) | async-done | bytes 393248 | tf_op jit(solution)/shard_map/all_to_all | solution.py:404
  64.9 0.0 copy-done.4
  64.9 4.9 %shard_map.99 = bf16[4096,1024]{1,0:T(8,128)(2,1)} custom-call(bf16[256,256]{1,0:T(8,128)(2,1)S(1)} %shard_map.96.side_ref, bf16[256,256]{1,0:T(8,128)(2,1)} %collective-permute-done.4.partner_ref, bf16[256,512]{1,0:T(8,128)(2,1)S(1)} %copy-done.4, bf16[32,48,128]{2,1,0:T(8,128)(2,1)S(1)} %all-to-all-done.1.packed_ref, ...), custom_call_target="tpu_custom_call" | custom-call | tf_op jit(solution)/shard_map/pallas_call | solution.py:313
  (2 shorter events, 0.0 us)
Async XLA Ops:
  5.9 40.8 %all-to-all-start = ((bf16[32,56,128]{2,1,0:T(8,128)(2,1)}), bf16[32,56,128]{2,1,0:T(8,128)(2,1)S(1)}, u32[]{:S(2)}, u32[]{:S(2)}) async-start(bf16[32,56,128]{2,1,0:T(8,128)(2,1)} %shard_map.97), calls=%async_computation | async-start | bytes 917504 | tf_op jit(solution)/shard_map/all_to_all | solution.py:398
  13.3 12.7 %copy-start = (bf16[2,512,512]{2,1,0:T(8,128)(2,1)S(1)}, bf16[2,512,512]{2,1,0:T(8,128)(2,1)}, u32[]{:S(2)}) copy-start(bf16[2,512,512]{2,1,0:T(8,128)(2,1)} %comp_ref.1) | copy-start | bytes 3145732
  13.3 12.7 %copy-start.7 = (f32[2,1,4,256]{3,2,1,0:T(4,128)S(1)}, f32[2,1,4,256]{3,2,1,0:T(4,128)}, u32[]{:S(2)}) copy-start(f32[2,1,4,256]{3,2,1,0:T(4,128)} %param.13) | copy-start | bytes 24580
  16.5 20.9 %copy-start.2 = (f32[3,1,8,256]{3,2,1,0:T(8,128)S(1)}, f32[3,1,8,256]{3,2,1,0:T(8,128)}, u32[]{:S(2)}) copy-start(f32[3,1,8,256]{3,2,1,0:T(8,128)} %param.15) | copy-start | bytes 73732
  16.5 30.3 %copy-start.1 = (bf16[3,512,512]{2,1,0:T(8,128)(2,1)S(1)}, bf16[3,512,512]{2,1,0:T(8,128)(2,1)}, u32[]{:S(2)}) copy-start(bf16[3,512,512]{2,1,0:T(8,128)(2,1)} %exp_ref.1) | copy-start | bytes 4718596
  16.5 9.5 %collective-permute-start = (bf16[256,256]{1,0:T(8,128)(2,1)S(1)}, bf16[256,256]{1,0:T(8,128)(2,1)S(1)}, u32[]{:S(2)}, u32[]{:S(2)}) collective-permute-start(bf16[256,256]{1,0:T(8,128)(2,1)S(1)} %shard_map.91.own_ref), channel_id=1, source_target_pairs={{0,8},{8,0},{16,24},{24,16},{1,9},{9,1},{17,25},{25,17},{2,10},{10... | collective-permute-start | bytes 393224 | tf_op jit(solution)/shard_map/ppermute | solution.py:231
  26.3 26.8 %copy-start.8 = (f32[4096]{0:T(1024)S(1)}, f32[4096]{0:T(1024)}, u32[]{:S(2)}) copy-start(f32[4096]{0:T(1024)} %param.17) | copy-start | bytes 49156
  26.3 8.8 %collective-permute-start.1 = (bf16[256,256]{1,0:T(8,128)(2,1)S(1)}, bf16[256,256]{1,0:T(8,128)(2,1)S(1)}, u32[]{:S(2)}, u32[]{:S(2)}) collective-permute-start(bf16[256,256]{1,0:T(8,128)(2,1)S(1)} %shard_map.92.own_ref), channel_id=1, source_target_pairs={{0,16},{8,24},{16,0},{24,8},{1,17},{9,25},{17,1},{25,9},{2,18},{10... | collective-permute-start | bytes 393224 | tf_op jit(solution)/shard_map/ppermute | solution.py:231
  35.4 1.9 %collective-permute-start.2 = (bf16[256,256]{1,0:T(8,128)(2,1)S(1)}, bf16[256,256]{1,0:T(8,128)(2,1)S(1)}, u32[]{:S(2)}, u32[]{:S(2)}) collective-permute-start(bf16[256,256]{1,0:T(8,128)(2,1)S(1)} %shard_map.93.own_ref), channel_id=1, source_target_pairs={{0,1},{1,0},{2,3},{3,2},{4,5},{5,4},{6,7},{7,6},{8,9},{9,8},{10,11... | collective-permute-start | bytes 393224 | tf_op jit(solution)/shard_map/ppermute | solution.py:231
  36.7 0.7 copy-start.5
  37.4 0.7 %copy-start.3 = (bf16[256,512]{1,0:T(8,128)(2,1)}, bf16[256,512]{1,0:T(8,128)(2,1)S(1)}, u32[]{:S(2)}) copy-start(bf16[256,512]{1,0:T(8,128)(2,1)S(1)} %get-tuple-element.10.rows_ref) | copy-start | bytes 786436
  38.1 5.9 %collective-permute-start.3 = (bf16[256,256]{1,0:T(8,128)(2,1)S(1)}, bf16[256,256]{1,0:T(8,128)(2,1)S(1)}, u32[]{:S(2)}, u32[]{:S(2)}) collective-permute-start(bf16[256,256]{1,0:T(8,128)(2,1)S(1)} %shard_map.95.own_ref), channel_id=1, source_target_pairs={{0,2},{1,3},{2,0},{3,1},{4,6},{5,7},{6,4},{7,5},{8,10},{9,11},{10,... | collective-permute-start | bytes 393224 | tf_op jit(solution)/shard_map/ppermute | solution.py:231
  43.9 1.0 %copy-start.6 = (bf16[256,512]{1,0:T(8,128)(2,1)S(1)}, bf16[256,512]{1,0:T(8,128)(2,1)}, u32[]{:S(2)}) copy-start(bf16[256,512]{1,0:T(8,128)(2,1)} %copy-done.5) | copy-start | bytes 786436
  45.2 19.7 %copy-start.4 = (bf16[256,512]{1,0:T(8,128)(2,1)S(1)}, bf16[256,512]{1,0:T(8,128)(2,1)}, u32[]{:S(2)}) copy-start(bf16[256,512]{1,0:T(8,128)(2,1)} %copy-done.3) | copy-start | bytes 786436
  45.2 9.9 %collective-permute-start.4 = (bf16[256,256]{1,0:T(8,128)(2,1)S(1)}, bf16[256,256]{1,0:T(8,128)(2,1)}, u32[]{:S(2)}, u32[]{:S(2)}) collective-permute-start(bf16[256,256]{1,0:T(8,128)(2,1)S(1)} %shard_map.96.side_ref), channel_id=1, source_target_pairs={{0,4},{1,5},{2,6},{3,7},{4,0},{5,1},{6,2},{7,3},{8,12},{9,13},{10,... | collective-permute-start | bytes 393224 | tf_op jit(solution)/shard_map/ppermute | solution.py:231
  49.0 15.9 %all-to-all-start.1 = ((bf16[32,48,128]{2,1,0:T(8,128)(2,1)}), bf16[32,48,128]{2,1,0:T(8,128)(2,1)S(1)}, u32[]{:S(2)}, u32[]{:S(2)}) async-start(bf16[32,48,128]{2,1,0:T(8,128)(2,1)} %shard_map.98), calls=%async_computation.1 | async-start | bytes 786432 | tf_op jit(solution)/shard_map/all_to_all | solution.py:404

commit v8 on v7

--- a/solution.py
+++ b/solution.py
@@ -260,7 +260,7 @@
         halves = state.reshape(boxes // (2 * stride), 2, stride * width, skeleton)
         low = halves[:, 0].reshape(boxes // 2 * width, skeleton).astype(jnp.bfloat16)
         high = halves[:, 1].reshape(boxes // 2 * width, skeleton).astype(jnp.bfloat16)
-        mixed = mm(low, transfer[:, :skeleton], NT) + mm(high, transfer[:, skeleton:], NT)
+        mixed = mm(jnp.concatenate([low, high], axis=1), transfer, NT)
         shape = (boxes // (2 * stride), 1, stride, width, skeleton)
         state = jnp.concatenate(
             [mixed[:, :skeleton].reshape(shape), mixed[:, skeleton:].reshape(shape)], axis=1
@@ -285,43 +285,68 @@
     )(on_chip(packed), on_chip(comp_transfer), on_chip(exp_transfer))
 
 
-def decode_kernel(blocks, bit, side_ref, partner_ref, rows_ref, packed_ref, decoder_ref, out_hbm, turned_ref, held, sems):
-    boxes, rows, _ = packed_ref.shape
-    width, side = rows // 2, side_ref.shape[1]
-    packed = packed_ref[...].astype(jnp.float32)
-    coeffs = jnp.concatenate([packed[:, :width, :], packed[:, width:, :]], axis=-1)
-    coeffs = coeffs.reshape(boxes * width, 2 * LANES)
-    turned_ref[:, :side] = mix("row", bit, side_ref, partner_ref, rows_ref).astype(jnp.bfloat16)
-    turned_ref[:, side:] = coeffs.T.astype(jnp.bfloat16)
+def put_out(first, coeffs_ref, decoder_ref, out_hbm, held, sems):
+    blocks = sems.shape[0]
     block = decoder_ref.shape[0] // blocks
     copies = []
     for number in range(blocks):
         span = pl.ds(number * block, block)
         rows_of = slice(number * block, (number + 1) * block)
-        held[rows_of, :] = mm(decoder_ref[rows_of, :], turned_ref[...]).astype(jnp.bfloat16)
-        copies.append(pltpu.make_async_copy(held.at[span], out_hbm.at[span], sems.at[number]))
+        held[rows_of, :] = mm(decoder_ref[rows_of, :], coeffs_ref[...]).astype(jnp.bfloat16)
+        target = out_hbm.at[span, pl.ds(first, held.shape[1])]
+        copies.append(pltpu.make_async_copy(held.at[span], target, sems.at[number]))
         copies[-1].start()
     for copy in copies:
         copy.wait()
 
 
-def decode(bit, side, partner, last_rows, packed, decoder):
+def decode_kernel(first, packed_ref, decoder_ref, out_hbm, turned_ref, held, sems):
+    boxes, rows, _ = packed_ref.shape
+    width = rows // 2
+    packed = packed_ref[...].astype(jnp.float32)
+    coeffs = jnp.concatenate([packed[:, :width, :], packed[:, width:, :]], axis=-1)
+    turned_ref[...] = coeffs.reshape(boxes * width, 2 * LANES).T.astype(jnp.bfloat16)
+    put_out(first, turned_ref, decoder_ref, out_hbm, held, sems)
+
+
+def decode(packed, decoder, first):
     boxes, rows, _ = packed.shape
     points, skeleton = decoder.shape
-    width = side.shape[1] + boxes * rows // 2
-    blocks = 8
-    return pl.pallas_call(
-        functools.partial(decode_kernel, blocks, bit),
-        in_specs=[VMEM] * 5,
-        compiler_params=pltpu.CompilerParams(vmem_limit_bytes=20 * 2**20),
+    width = boxes * rows // 2
+    return pl.pallas_call(
+        functools.partial(decode_kernel, first),
+        in_specs=[VMEM, VMEM],
+        compiler_params=pltpu.CompilerParams(vmem_limit_bytes=16 * 2**20),
         out_specs=HBM,
-        out_shape=jax.ShapeDtypeStruct((points, width), jnp.bfloat16),
+        out_shape=pltpu.HBM((points, first + width), jnp.bfloat16),
         scratch_shapes=[
             pltpu.VMEM((skeleton, width), jnp.bfloat16),
             pltpu.VMEM((points, width), jnp.bfloat16),
-            pltpu.SemaphoreType.DMA((blocks,)),
+            pltpu.SemaphoreType.DMA((8,)),
         ],
-    )(on_chip(side), on_chip(partner), on_chip(last_rows), on_chip(packed), decoder)
+    )(on_chip(packed), decoder)
+
+
+def side_decode_kernel(bit, own_ref, partner_ref, rows_ref, decoder_ref, given_hbm, out_hbm, coeffs_ref, held, sems):
+    coeffs_ref[...] = mix("row", bit, own_ref, partner_ref, rows_ref).astype(jnp.bfloat16)
+    put_out(0, coeffs_ref, decoder_ref, out_hbm, held, sems)
+
+
+def side_decode(bit, own, partner, rows, decoder, given):
+    points = decoder.shape[0]
+    return pl.pallas_call(
+        functools.partial(side_decode_kernel, bit),
+        in_specs=[VMEM] * 4 + [HBM],
+        compiler_params=pltpu.CompilerParams(vmem_limit_bytes=8 * 2**20),
+        out_specs=HBM,
+        out_shape=pltpu.HBM(given.shape, jnp.bfloat16),
+        scratch_shapes=[
+            pltpu.VMEM(own.shape, jnp.bfloat16),
+            pltpu.VMEM((points, own.shape[1]), jnp.bfloat16),
+            pltpu.SemaphoreType.DMA((4,)),
+        ],
+        input_output_aliases={4: 0},
+    )(on_chip(own), on_chip(partner), on_chip(rows), decoder, in_hbm(given))
 
 
 def plain_encode(sources, enc_scale, encoder, comp_gain, exp_gain, parts):
@@ -406,7 +431,8 @@
         coeffs = side_level(coeffs, "row", number, rows[number], exp_gain)
     partner = from_partner(coeffs, "row", exp_levels - 1)
     table = on_chip((decoder.astype(jnp.float32) * factors).astype(jnp.bfloat16))
-    return decode(exp_levels - 1, coeffs, partner, rows[exp_levels - 1], packed, table)
+    field = decode(packed, table, side)
+    return side_decode(exp_levels - 1, coeffs, partner, rows[exp_levels - 1], table, field)
 
 
 def solution(mesh):

time: 71 us -> 71.2 us (level)
    pallas_call x1 -> x2, Pallas kernels: 4.91 us -> 5.27 us  [the longest x1 3.28 us: decode(): pl.pallas_call(functools.partial(decode_kernel, first), in_specs=[VMEM, V...]
  transfers between devices with their start and end apart: 7 -> 7, of which waited for: 4 -> 4; matrix products, arithmetic and copies ran while one was open for 3% -> 3% of each run, Pallas kernels for 11% -> 16%
where the time goes in v8:
time: 71.2 us; the launch traced here: 70.1 us
  waiting for transfers between devices  27.9 us (39%)
  starting transfers between devices  19.2 us (27%)
  Pallas kernels  18.8 us (26%)
  local copies, waits for them, and re-layouts  2.09 us (3%)
  other arithmetic  1.94 us (3%)
    ppermute x5, waiting for transfers between devices, from_partner(): lax.ppermute(own, axis, [(source, source ^ 2 ** bit) for source in range(...  18.1 us
    all_to_all x2, starting transfers between devices, body(): packed = lax.all_to_all(packed, ORDER, 0, 0, tiled=True)  11.4 us
    all_to_all x2, waiting for transfers between devices, body(): packed = lax.all_to_all(packed, ORDER, 0, 0, tiled=True)  9.88 us
    ppermute x5, starting transfers between devices, from_partner(): lax.ppermute(own, axis, [(source, source ^ 2 ** bit) for source in range(...  7.75 us
    pallas_call x1, Pallas kernels, encode(): pl.pallas_call(functools.partial(encode_kernel, blocks, first), in_specs=...  5.93 us
    pallas_call x1, Pallas kernels, decode(): pl.pallas_call(functools.partial(decode_kernel, first), in_specs=[VMEM, V...  3.28 us
    pallas_call x1, Pallas kernels, side_encode(): pl.pallas_call(functools.partial(side_encode_kernel, blocks), in_specs=[H...  3.16 us
    pallas_call x1, Pallas kernels, levels(): pl.pallas_call(functools.partial(levels_kernel, strides, pad), in_specs=[...  2.14 us
  transfers between devices with their start and end apart: 7, of which 4 were waited for; matrix products, arithmetic and copies ran while one was open for 3% of the time, Pallas kernels for 16%

profile of v8, /device:TPU:0, one launch (start us, length us, event | category | flops | bytes accessed | tf_op | source)
XLA Modules:
  0.0 70.1 jit_solution(17820102000783616731)
XLA Ops:
  0.0 5.9 %shard_map.97 = bf16[32,56,128]{2,1,0:T(8,128)(2,1)} custom-call(bf16[4096,1024]{1,0:T(8,128)(2,1)} %sources_hbm.3, f32[1,4096]{1,0:T(1,128)} %bitcast.10, bf16[256,4096]{1,0:T(8,128)(2,1)} %encoder_hbm.3, f32[2,4,256]{2,1,0:T(4,128)} %bitcast.7, f32[3,8,256]{2,1,0:T(8,128)} %bitcast.4), custom_call_target="tpu_custom_call" | custom-call | tf_op jit(solution)/shard_map/pallas_call | solution.py:120
  5.9 7.3 %all-to-all-start = ((bf16[32,56,128]{2,1,0:T(8,128)(2,1)}), bf16[32,56,128]{2,1,0:T(8,128)(2,1)S(1)}, u32[]{:S(2)}, u32[]{:S(2)}) async-start(bf16[32,56,128]{2,1,0:T(8,128)(2,1)} %shard_map.97), calls=%async_computation | async-start | bytes 917504 | tf_op jit(solution)/shard_map/all_to_all | solution.py:423
  13.3 0.0 copy-start
  13.3 0.0 copy-start.7
  13.3 3.2 %shard_map.91.own_ref = bf16[256,256]{1,0:T(8,128)(2,1)S(1)} custom-call(bf16[4096,1024]{1,0:T(8,128)(2,1)} %sources_hbm.3, f32[1,4096]{1,0:T(1,128)} %bitcast.11, bf16[256,4096]{1,0:T(8,128)(2,1)} %encoder_hbm.3), custom_call_target="tpu_custom_call" | custom-call | tf_op jit(solution)/shard_map/pallas_call | solution.py:170
  16.5 0.0 copy-start.2
  16.5 0.0 copy-start.1
  16.5 1.8 %collective-permute-start = (bf16[256,256]{1,0:T(8,128)(2,1)S(1)}, bf16[256,256]{1,0:T(8,128)(2,1)S(1)}, u32[]{:S(2)}, u32[]{:S(2)}) collective-permute-start(bf16[256,256]{1,0:T(8,128)(2,1)S(1)} %shard_map.91.own_ref), channel_id=1, source_target_pairs={{0,8},{8,0},{16,24},{24,16},{1,9},{9,1},{17,25},{25,17},{2,10},{10... | collective-permute-start | bytes 393224 | tf_op jit(solution)/shard_map/ppermute | solution.py:231
  18.3 7.7 %collective-permute-done.partner_ref = bf16[256,256]{1,0:T(8,128)(2,1)S(1)} collective-permute-done((bf16[256,256]{1,0:T(8,128)(2,1)S(1)}, bf16[256,256]{1,0:T(8,128)(2,1)S(1)}, u32[]{:S(2)}, u32[]{:S(2)}) %collective-permute-start) | collective-permute-done | bytes 131104 | tf_op jit(solution)/shard_map/ppermute | solution.py:231
  26.0 0.0 copy-done
  26.0 0.0 copy-done.7
  26.0 0.3 shard_map.92.own_ref
  26.3 0.0 copy-start.8
  26.3 2.8 %collective-permute-start.1 = (bf16[256,256]{1,0:T(8,128)(2,1)S(1)}, bf16[256,256]{1,0:T(8,128)(2,1)S(1)}, u32[]{:S(2)}, u32[]{:S(2)}) collective-permute-start(bf16[256,256]{1,0:T(8,128)(2,1)S(1)} %shard_map.92.own_ref), channel_id=1, source_target_pairs={{0,16},{8,24},{16,0},{24,8},{1,17},{9,25},{17,1},{25,9},{2,18},{10... | collective-permute-start | bytes 393224 | tf_op jit(solution)/shard_map/ppermute | solution.py:231
  29.1 6.0 %collective-permute-done.1.partner_ref = bf16[256,256]{1,0:T(8,128)(2,1)S(1)} collective-permute-done((bf16[256,256]{1,0:T(8,128)(2,1)S(1)}, bf16[256,256]{1,0:T(8,128)(2,1)S(1)}, u32[]{:S(2)}, u32[]{:S(2)}) %collective-permute-start.1) | collective-permute-done | bytes 131104 | tf_op jit(solution)/shard_map/ppermute | solution.py:231
  35.1 0.3 shard_map.93.own_ref
  35.4 0.1 collective-permute-start.2
  35.5 1.1 %shard_map.94 = (bf16[256,512]{1,0:T(8,128)(2,1)S(1)}, bf16[256,512]{1,0:T(8,128)(2,1)S(1)}, bf16[256,512]{1,0:T(8,128)(2,1)S(1)}) custom-call(bf16[3,512,512]{2,1,0:T(8,128)(2,1)} %exp_ref.1), custom_call_target="tpu_custom_call" | custom-call | tf_op jit(solution)/shard_map/pallas_call | solution.py:202
  36.7 0.0 copy-start.5
  36.7 0.7 copy-done.5
  37.4 0.0 copy-start.3
  37.4 0.0 collective-permute-done.2.partner_ref
  37.4 0.0 copy-done.2
  37.4 0.3 shard_map.95.own_ref
  37.7 0.4 copy-done.3
  38.1 1.5 %collective-permute-start.3 = (bf16[256,256]{1,0:T(8,128)(2,1)S(1)}, bf16[256,256]{1,0:T(8,128)(2,1)S(1)}, u32[]{:S(2)}, u32[]{:S(2)}) collective-permute-start(bf16[256,256]{1,0:T(8,128)(2,1)S(1)} %shard_map.95.own_ref), channel_id=1, source_target_pairs={{0,2},{1,3},{2,0},{3,1},{4,6},{5,7},{6,4},{7,5},{8,10},{9,11},{10,... | collective-permute-start | bytes 393224 | tf_op jit(solution)/shard_map/ppermute | solution.py:231
  39.5 4.4 %collective-permute-done.3.partner_ref = bf16[256,256]{1,0:T(8,128)(2,1)S(1)} collective-permute-done((bf16[256,256]{1,0:T(8,128)(2,1)S(1)}, bf16[256,256]{1,0:T(8,128)(2,1)S(1)}, u32[]{:S(2)}, u32[]{:S(2)}) %collective-permute-start.3) | collective-permute-done | bytes 131104 | tf_op jit(solution)/shard_map/ppermute | solution.py:231
  43.9 0.0 copy-start.6
  43.9 0.9 %copy-done.6 = bf16[256,512]{1,0:T(8,128)(2,1)S(1)} copy-done((bf16[256,512]{1,0:T(8,128)(2,1)S(1)}, bf16[256,512]{1,0:T(8,128)(2,1)}, u32[]{:S(2)}) %copy-start.6) | copy-done | bytes 262168
  44.9 0.3 shard_map.96.own_ref
  45.2 1.6 %collective-permute-start.4 = (bf16[256,256]{1,0:T(8,128)(2,1)S(1)}, bf16[256,256]{1,0:T(8,128)(2,1)S(1)}, u32[]{:S(2)}, u32[]{:S(2)}) collective-permute-start(bf16[256,256]{1,0:T(8,128)(2,1)S(1)} %shard_map.96.own_ref), channel_id=1, source_target_pairs={{0,4},{1,5},{2,6},{3,7},{4,0},{5,1},{6,2},{7,3},{8,12},{9,13},{10,... | collective-permute-start | bytes 393224 | tf_op jit(solution)/shard_map/ppermute | solution.py:231
  46.8 0.0 all-to-all-done.packed_ref
  46.8 0.0 copy-done.1
  46.8 2.1 %shard_map.98 = bf16[32,48,128]{2,1,0:T(8,128)(2,1)} custom-call(bf16[32,56,128]{2,1,0:T(8,128)(2,1)S(1)} %all-to-all-done.packed_ref, bf16[2,512,512]{2,1,0:T(8,128)(2,1)S(1)} %copy-done, bf16[3,512,512]{2,1,0:T(8,128)(2,1)S(1)} %copy-done.1), custom_call_target="tpu_custom_call" | custom-call | tf_op jit(solution)/shard_map/pallas_call | solution.py:279
  48.9 4.1 %all-to-all-start.1 = ((bf16[32,48,128]{2,1,0:T(8,128)(2,1)}), bf16[32,48,128]{2,1,0:T(8,128)(2,1)S(1)}, u32[]{:S(2)}, u32[]{:S(2)}) async-start(bf16[32,48,128]{2,1,0:T(8,128)(2,1)} %shard_map.98), calls=%async_computation.1 | async-start | bytes 786432 | tf_op jit(solution)/shard_map/all_to_all | solution.py:429
  53.0 0.0 copy-done.8
  53.0 1.9 %multiply_convert_fusion.decoder_ref = bf16[4096,256]{1,0:T(8,128)(2,1)S(1)} fusion(bf16[4096,256]{1,0:T(8,128)(2,1)} %param.16, f32[256]{0:T(256)S(1)} %bitcast.12, f32[4096]{0:T(1024)S(1)} %copy-done.8), kind=kLoop, calls=%fused_computation | loop fusion | flops 4194304 | bytes 4211712 | tf_op jit(solution)/shard_map/convert_element_type | solution.py:433
  54.9 0.0 copy-start.4
  55.0 9.9 %all-to-all-done.1.packed_ref = bf16[32,48,128]{2,1,0:T(8,128)(2,1)S(1)} async-done(((bf16[32,48,128]{2,1,0:T(8,128)(2,1)}), bf16[32,48,128]{2,1,0:T(8,128)(2,1)S(1)}, u32[]{:S(2)}, u32[]{:S(2)}) %all-to-all-start.1) | async-done | bytes 393248 | tf_op jit(solution)/shard_map/all_to_all | solution.py:429
  64.8 3.3 %shard_map.99.given_hbm = bf16[4096,1024]{1,0:T(8,128)(2,1)} custom-call(bf16[32,48,128]{2,1,0:T(8,128)(2,1)S(1)} %all-to-all-done.1.packed_ref, bf16[4096,256]{1,0:T(8,128)(2,1)S(1)} %multiply_convert_fusion.decoder_ref), custom_call_target="tpu_custom_call" | custom-call | tf_op jit(solution)/shard_map/pallas_call | solution.py:316
  68.1 0.0 collective-permute-done.4.partner_ref
  68.1 0.0 copy-done.4
  68.1 2.0 %shard_map.100 = bf16[4096,1024]{1,0:T(8,128)(2,1)} custom-call(bf16[256,256]{1,0:T(8,128)(2,1)S(1)} %shard_map.96.own_ref, bf16[256,256]{1,0:T(8,128)(2,1)S(1)} %collective-permute-done.4.partner_ref, bf16[256,512]{1,0:T(8,128)(2,1)S(1)} %copy-done.4, bf16[4096,256]{1,0:T(8,128)(2,1)S(1)} %multiply_convert_fusion.decoder_ref, ...), custom_call_target="tpu_custom_call", output_to_operand_aliasing={{}: (4, {})} | custom-call | tf_op jit(solution)/shard_map/pallas_call | solution.py:337
  (2 shorter events, 0.0 us)
Async XLA Ops:
  5.9 40.8 %all-to-all-start = ((bf16[32,56,128]{2,1,0:T(8,128)(2,1)}), bf16[32,56,128]{2,1,0:T(8,128)(2,1)S(1)}, u32[]{:S(2)}, u32[]{:S(2)}) async-start(bf16[32,56,128]{2,1,0:T(8,128)(2,1)} %shard_map.97), calls=%async_computation | async-start | bytes 917504 | tf_op jit(solution)/shard_map/all_to_all | solution.py:423
  13.3 12.7 %copy-start = (bf16[2,512,512]{2,1,0:T(8,128)(2,1)S(1)}, bf16[2,512,512]{2,1,0:T(8,128)(2,1)}, u32[]{:S(2)}) copy-start(bf16[2,512,512]{2,1,0:T(8,128)(2,1)} %comp_ref.1) | copy-start | bytes 3145732
  13.3 12.7 %copy-start.7 = (f32[2,1,4,256]{3,2,1,0:T(4,128)S(1)}, f32[2,1,4,256]{3,2,1,0:T(4,128)}, u32[]{:S(2)}) copy-start(f32[2,1,4,256]{3,2,1,0:T(4,128)} %param.13) | copy-start | bytes 24580
  16.5 20.9 %copy-start.2 = (f32[3,1,8,256]{3,2,1,0:T(8,128)S(1)}, f32[3,1,8,256]{3,2,1,0:T(8,128)}, u32[]{:S(2)}) copy-start(f32[3,1,8,256]{3,2,1,0:T(8,128)} %param.15) | copy-start | bytes 73732
  16.5 30.3 %copy-start.1 = (bf16[3,512,512]{2,1,0:T(8,128)(2,1)S(1)}, bf16[3,512,512]{2,1,0:T(8,128)(2,1)}, u32[]{:S(2)}) copy-start(bf16[3,512,512]{2,1,0:T(8,128)(2,1)} %exp_ref.1) | copy-start | bytes 4718596
  16.5 9.5 %collective-permute-start = (bf16[256,256]{1,0:T(8,128)(2,1)S(1)}, bf16[256,256]{1,0:T(8,128)(2,1)S(1)}, u32[]{:S(2)}, u32[]{:S(2)}) collective-permute-start(bf16[256,256]{1,0:T(8,128)(2,1)S(1)} %shard_map.91.own_ref), channel_id=1, source_target_pairs={{0,8},{8,0},{16,24},{24,16},{1,9},{9,1},{17,25},{25,17},{2,10},{10... | collective-permute-start | bytes 393224 | tf_op jit(solution)/shard_map/ppermute | solution.py:231
  26.3 26.7 %copy-start.8 = (f32[4096]{0:T(1024)S(1)}, f32[4096]{0:T(1024)}, u32[]{:S(2)}) copy-start(f32[4096]{0:T(1024)} %param.17) | copy-start | bytes 49156
  26.3 8.8 %collective-permute-start.1 = (bf16[256,256]{1,0:T(8,128)(2,1)S(1)}, bf16[256,256]{1,0:T(8,128)(2,1)S(1)}, u32[]{:S(2)}, u32[]{:S(2)}) collective-permute-start(bf16[256,256]{1,0:T(8,128)(2,1)S(1)} %shard_map.92.own_ref), channel_id=1, source_target_pairs={{0,16},{8,24},{16,0},{24,8},{1,17},{9,25},{17,1},{25,9},{2,18},{10... | collective-permute-start | bytes 393224 | tf_op jit(solution)/shard_map/ppermute | solution.py:231
  35.4 1.9 %collective-permute-start.2 = (bf16[256,256]{1,0:T(8,128)(2,1)S(1)}, bf16[256,256]{1,0:T(8,128)(2,1)S(1)}, u32[]{:S(2)}, u32[]{:S(2)}) collective-permute-start(bf16[256,256]{1,0:T(8,128)(2,1)S(1)} %shard_map.93.own_ref), channel_id=1, source_target_pairs={{0,1},{1,0},{2,3},{3,2},{4,5},{5,4},{6,7},{7,6},{8,9},{9,8},{10,11... | collective-permute-start | bytes 393224 | tf_op jit(solution)/shard_map/ppermute | solution.py:231
  36.7 0.7 %copy-start.5 = (bf16[256,512]{1,0:T(8,128)(2,1)}, bf16[256,512]{1,0:T(8,128)(2,1)S(1)}, u32[]{:S(2)}) copy-start(bf16[256,512]{1,0:T(8,128)(2,1)S(1)} %get-tuple-element.9.rows_ref) | copy-start | bytes 786436
  37.4 0.7 copy-start.3
  38.1 5.9 %collective-permute-start.3 = (bf16[256,256]{1,0:T(8,128)(2,1)S(1)}, bf16[256,256]{1,0:T(8,128)(2,1)S(1)}, u32[]{:S(2)}, u32[]{:S(2)}) collective-permute-start(bf16[256,256]{1,0:T(8,128)(2,1)S(1)} %shard_map.95.own_ref), channel_id=1, source_target_pairs={{0,2},{1,3},{2,0},{3,1},{4,6},{5,7},{6,4},{7,5},{8,10},{9,11},{10,... | collective-permute-start | bytes 393224 | tf_op jit(solution)/shard_map/ppermute | solution.py:231
  43.9 1.0 %copy-start.6 = (bf16[256,512]{1,0:T(8,128)(2,1)S(1)}, bf16[256,512]{1,0:T(8,128)(2,1)}, u32[]{:S(2)}) copy-start(bf16[256,512]{1,0:T(8,128)(2,1)} %copy-done.5) | copy-start | bytes 786436
  45.2 22.9 %collective-permute-start.4 = (bf16[256,256]{1,0:T(8,128)(2,1)S(1)}, bf16[256,256]{1,0:T(8,128)(2,1)S(1)}, u32[]{:S(2)}, u32[]{:S(2)}) collective-permute-start(bf16[256,256]{1,0:T(8,128)(2,1)S(1)} %shard_map.96.own_ref), channel_id=1, source_target_pairs={{0,4},{1,5},{2,6},{3,7},{4,0},{5,1},{6,2},{7,3},{8,12},{9,13},{10,... | collective-permute-start | bytes 393224 | tf_op jit(solution)/shard_map/ppermute | solution.py:231
  48.9 15.9 %all-to-all-start.1 = ((bf16[32,48,128]{2,1,0:T(8,128)(2,1)}), bf16[32,48,128]{2,1,0:T(8,128)(2,1)S(1)}, u32[]{:S(2)}, u32[]{:S(2)}) async-start(bf16[32,48,128]{2,1,0:T(8,128)(2,1)} %shard_map.98), calls=%async_computation.1 | async-start | bytes 786432 | tf_op jit(solution)/shard_map/all_to_all | solution.py:429
  54.9 13.2 %copy-start.4 = (bf16[256,512]{1,0:T(8,128)(2,1)S(1)}, bf16[256,512]{1,0:T(8,128)(2,1)}, u32[]{:S(2)}) copy-start(bf16[256,512]{1,0:T(8,128)(2,1)} %copy-done.3) | copy-start | bytes 786436
